TPU v7x, 32 devices: a whole 2x2x4 slice. The times are simulated.
32 devices in a mesh: gz: 8 (over z, y), gy: 4 (over x, core).
Axes of the slice: x: 2, y: 2, z: 4, core: 2. Of those that a mesh axis runs over, the one named last changes fastest.
Arguments:
- features: bfloat16 [8, 4, 2, 512, 128], P('gz', 'gy'), may hold values from -6 to 6
- brick_sites: int32 [8, 4, 2], P('gz', 'gy'), may hold values from 0 to 8, as said below
- kernel: bfloat16 [27, 128, 128], replicated, may hold values from -0.109375 to 0.109375
- cotangent: bfloat16 [8, 4, 2, 512, 128], P('gz', 'gy'), may hold values from -6 to 6
Outputs:
- act: bfloat16 [8, 4, 2, 512, 128], P('gz', 'gy')
- grad_in: bfloat16 [8, 4, 2, 512, 128], P('gz', 'gy')
- grad_kernel: float32 [27, 128, 128], replicated
Inputs may be any that keep to these rules, and one draw needn't show every extreme that they name: `brick_sites`: within a block the places of used slots are distinct; empty slots, marked 8, come after the used ones; every block uses at least 1 slots and some block uses all 2.
All inputs are finite; a program needn't handle non-finite values.
Results may differ from a plain program's by a relative error of at most 0.0049.
Values may be sent and summed in bfloat16 or wider, within the bound.
No kernel may reach another device: no remote copies, remote signals or barrier semaphores. Data moves between devices by JAX's collectives and lax.ppermute only.
A program may use at most 128 MiB of HBM per device.

v0:
```python
import jax
import jax.numpy as jnp
from jax import lax
from jax.sharding import PartitionSpec as P

C = 128
VOX = 512
BY = 2
BX = 4
NB = 2
SITES = 8


def padded(block, sides, width):
    for axis, dim in sides:
        count = lax.axis_size(axis)
        forward = [(i, i + 1) for i in range(count - 1)]
        backward = [(target, source) for source, target in forward]
        low = lax.ppermute(
            lax.slice_in_dim(block, block.shape[dim] - width, None, axis=dim), axis, forward
        )
        high = lax.ppermute(lax.slice_in_dim(block, 0, width, axis=dim), axis, backward)
        block = jnp.concatenate([low, block, high], axis=dim)
    return block


def tap_offsets():
    return [(dz, dy, dx) for dz in (-1, 0, 1) for dy in (-1, 0, 1) for dx in (-1, 0, 1)]


def to_grid(bricks, sites):
    dense = jnp.zeros((SITES + 1, VOX, C), bricks.dtype).at[sites].set(bricks)[:SITES]
    dense = dense.reshape(BY, BX, 8, 8, 8, C).transpose(2, 0, 3, 1, 4, 5)
    return dense.reshape(8, BY * 8, BX * 8, C)


def cut_cubes(volume, rows_start, cols_start, width):
    zero = jnp.zeros((), jnp.int32)
    return jax.vmap(
        lambda r, c: lax.dynamic_slice(volume, (zero, r, c, zero), (width, width, width, C))
    )(rows_start, cols_start)


def local(features, brick_sites, kernel, cotangent):
    bricks = features[0, 0]
    sites = brick_sites[0, 0]
    upstream = cotangent[0, 0]
    valid = (sites < SITES)[:, None, None]
    clamped = jnp.minimum(sites, SITES - 1)
    rows_start = clamped // BX * 8
    cols_start = clamped % BX * 8
    offsets = tap_offsets()
    framed = padded(to_grid(bricks, sites), (("gz", 0), ("gy", 1)), 1)
    framed = jnp.pad(framed, ((0, 0), (0, 0), (1, 1), (0, 0)))
    patches = cut_cubes(framed, rows_start, cols_start, 10)
    pre = jnp.zeros((NB, 8, 8, 8, C), jnp.float32)
    for t, (dz, dy, dx) in enumerate(offsets):
        view = patches[:, 1 + dz : 9 + dz, 1 + dy : 9 + dy, 1 + dx : 9 + dx]
        pre = pre + jnp.einsum(
            "nzyxc,cd->nzyxd", view, kernel[t], preferred_element_type=jnp.float32
        )
    pre = pre.reshape(NB, VOX, C)
    sig = jax.nn.sigmoid(pre)
    act = jnp.where(valid, pre * sig, 0.0).astype(jnp.bfloat16)
    dpre = jnp.where(
        valid, upstream.astype(jnp.float32) * sig * (1.0 + pre * (1.0 - sig)), 0.0
    ).astype(jnp.bfloat16)
    dpre_cube = dpre.reshape(NB, 8, 8, 8, C)
    terms = []
    for t, (dz, dy, dx) in enumerate(offsets):
        view = patches[:, 1 + dz : 9 + dz, 1 + dy : 9 + dy, 1 + dx : 9 + dx]
        terms.append(
            jnp.einsum("nzyxc,nzyxd->cd", view, dpre_cube, preferred_element_type=jnp.float32)
        )
    local_kernel = jnp.stack(terms)
    widened = jnp.pad(dpre_cube, ((0, 0), (2, 2), (2, 2), (2, 2), (0, 0)))
    spread = jnp.zeros((NB, 10, 10, 10, C), jnp.float32)
    for t, (dz, dy, dx) in enumerate(offsets):
        view = widened[:, 1 - dz : 11 - dz, 1 - dy : 11 - dy, 1 - dx : 11 - dx]
        spread = spread + jnp.einsum(
            "nzyxd,cd->nzyxc", view, kernel[t], preferred_element_type=jnp.float32
        )
    canvas = jnp.zeros((10, BY * 8 + 2, BX * 8 + 2, C), jnp.float32)
    zero = jnp.zeros((), jnp.int32)
    for slot in range(NB):
        start = (zero, rows_start[slot], cols_start[slot], zero)
        piece = lax.dynamic_slice(canvas, start, (10, 10, 10, C))
        canvas = lax.dynamic_update_slice(canvas, piece + spread[slot], start)
    canvas = canvas[:, :, 1:-1]
    rims = jnp.concatenate([canvas[0:1], canvas[9:10]], axis=0)
    arrived_rims = padded(rims.astype(jnp.bfloat16), (("gz", 0),), 1).astype(rims.dtype)
    inner = canvas[1:9]
    inner = inner.at[0].add(arrived_rims[0]).at[7].add(arrived_rims[3])
    sides = jnp.concatenate([inner[:, 0:1], inner[:, -1:]], axis=1)
    beside = padded(sides.astype(jnp.bfloat16), (("gy", 1),), 1).astype(sides.dtype)
    core = inner[:, 1:-1]
    core = core.at[:, 0].add(beside[:, 0]).at[:, -1].add(beside[:, 3])
    grad = cut_cubes(core, rows_start, cols_start, 8)
    grad_in = jnp.where(valid, grad.reshape(NB, VOX, C), 0.0).astype(jnp.bfloat16)
    total_kernel = lax.psum(local_kernel, ("gz", "gy"))
    count = jnp.float32(NB * VOX * lax.axis_size("gz") * lax.axis_size("gy"))
    grad_kernel = total_kernel / jnp.sqrt(count)
    return (act[None, None], grad_in[None, None], grad_kernel)


def solution(mesh):
    placed = (
        P("gz", "gy", None, None, None),
        P("gz", "gy", None),
        P(),
        P("gz", "gy", None, None, None),
    )
    return jax.shard_map(
        local,
        mesh=mesh,
        in_specs=placed,
        out_specs=(P("gz", "gy", None, None, None), P("gz", "gy", None, None, None), P()),
        check_vma=False,
    )
```

profile of v0, /device:TPU:0, one launch (start us, length us, event | category | flops | bytes accessed | tf_op | source)
XLA Modules:
  0.0 296.4 jit_solution(12816269744148694464)
XLA Ops:
  7.2 1.3 fusion.243
  8.7 1.5 scatter_fusion
  10.6 4.9 %collective-permute-start = (bf16[1,16,32,128]{3,0,2,1:T(2,128)(2,1)S(1)}, bf16[1,16,32,128]{3,0,2,1:T(2,128)(2,1)S(1)}, u32[]{:S(2)}, u32[]{:S(2)}) collective-permute-start(bf16[1,16,32,128]{3,0,2,1:T(2,128)(2,1)S(1)} %copy.91), channel_id=1, source_target_pairs={{0,4},{4,8},{8,12},{12,16},{16,20},{20,24},{24,28},{1,5},{5,9},{9,... | collective-permute-start | bytes 393224 | tf_op jit(solution)/shard_map/ppermute | solution.py:19
  15.8 1.3 collective-permute-start.1
  17.1 1.2 copy.92
  22.6 4.0 %collective-permute-done = bf16[1,16,32,128]{3,0,2,1:T(2,128)(2,1)S(1)} collective-permute-done((bf16[1,16,32,128]{3,0,2,1:T(2,128)(2,1)S(1)}, bf16[1,16,32,128]{3,0,2,1:T(2,128)(2,1)S(1)}, u32[]{:S(2)}, u32[]{:S(2)}) %collective-permute-start) | collective-permute-done | bytes 131104 | tf_op jit(solution)/shard_map/ppermute | solution.py:19
  26.9 1.3 collective-permute-start.2
  28.2 1.3 collective-permute-start.3
  35.8 3.7 %select_maximum_fusion = bf16[10,18,34,128]{3,0,2,1:T(8,128)(2,1)S(1)} fusion(bf16[10,1,32,128]{3,0,2,1:T(8,128)(2,1)} %collective-permute-done.3, bf16[10,1,32,128]{3,0,2,1:T(8,128)(2,1)} %copy-done.57, bf16[1,16,32,128]{3,0,2,1:T(2,128)(2,1)} %copy-done.5, bf16[8,16,32,128]{3,0,2,1:T(8,128)(2,1)S(1)} %bitcast.514, bf16[1,16,32,128]{3,0,2,1:T(2,128)(2,1)} %copy-done.4), kind=kLoop, calls=%fused_computation.33 | loop fusion | flops 14100480 | bytes 3041280 | tf_op jit(solution)/shard_map/concatenate | solution.py:23
  40.8 1.4 fusion.305
  49.0 1.2 fusion.62
  53.1 1.6 fusion.38
  54.6 1.6 fusion.39
  56.2 1.5 fusion.40
  57.7 1.6 fusion.41
  59.4 1.5 fusion.42
  60.9 1.6 fusion.43
  62.5 1.6 fusion.44
  64.1 1.6 fusion.45
  65.7 1.6 fusion.46
  67.3 1.5 fusion.47
  68.8 1.6 fusion.48
  70.4 1.5 fusion.49
  71.9 1.5 fusion.50
  73.5 1.6 fusion.51
  75.0 1.6 fusion.52
  76.6 1.6 fusion.53
  78.2 1.6 fusion.54
  79.8 1.5 fusion.55
  81.3 1.8 fusion.56
  83.1 1.5 fusion.57
  84.7 1.5 fusion.58
  86.2 12.2 %add_add_fusion = f32[2,10,10,10,128]{4,3,2,1,0:T(8,128)S(1)} fusion(f32[2,10,10,10,128]{4,3,2,1,0:T(8,128)} %fusion.58, f32[2,10,10,10,128]{4,3,2,1,0:T(8,128)} %fusion.57, f32[2,10,10,10,128]{4,3,2,1,0:T(8,128)} %fusion.56, f32[2,10,10,10,128]{4,3,2,1,0:T(8,128)} %fusion.55, f32[2,10,10,10,128]{4,3,2,1,0:T(8,128)} %fusion.54, ...), kind=kOutput, calls=%fused_computation.40 | convolution fusion | flops 72192000 | bytes 31014912 | tf_op jit(solution)/shard_map/nzyxd,cd->nzyxc/dot_general | solution.py:80
  98.5 2.1 broadcast_in_dim.41
  100.5 5.0 %dynamic_update_slice.6 = f32[10,18,34,128]{3,2,1,0:T(8,128)} dynamic-update-slice(f32[10,18,34,128]{3,2,1,0:T(8,128)} %broadcast_in_dim.41, f32[10,10,10,128]{3,2,1,0:T(8,128)S(1)} %slice_bitcast_fusion.1, s32[]{:T(128)} %constant.150.clone.1, s32[]{:T(128)S(6)} %select_n.135, s32[]{:T(128)S(6)} %select_n.137, s32[]{:T(128)} %constant.150.clone.1) | dynamic-update-slice | bytes 1024004 | tf_op jit(solution)/shard_map/dynamic_update_slice | solution.py:88
  105.5 1.4 fusion.59
  106.9 5.6 %dynamic_update_slice.7 = f32[10,18,34,128]{3,2,1,0:T(8,128)} dynamic-update-slice(f32[10,18,34,128]{3,2,1,0:T(8,128)} %dynamic_update_slice.6, f32[10,10,10,128]{3,2,1,0:T(8,128)S(1)} %fusion.59, s32[]{:T(128)} %constant.150.clone.1, s32[]{:T(128)S(6)} %select_n.138, s32[]{:T(128)S(6)} %select_n.139, s32[]{:T(128)} %constant.150.clone.1) | dynamic-update-slice | bytes 1024004 | tf_op jit(solution)/shard_map/dynamic_update_slice | solution.py:88
  112.6 2.3 slice.636
  140.3 4.3 %collective-permute-start.4 = (bf16[1,18,32,128]{3,2,1,0:T(8,128)(2,1)S(1)}, bf16[1,18,32,128]{3,2,1,0:T(8,128)(2,1)S(1)}, u32[]{:S(2)}, u32[]{:S(2)}) collective-permute-start(bf16[1,18,32,128]{3,2,1,0:T(8,128)(2,1)S(1)} %get-tuple-element.56), channel_id=1, source_target_pairs={{0,4},{4,8},{8,12},{12,16},{16,20},{20,24},{24,28},{1,5},{5,9},{9,... | collective-permute-start | bytes 442376 | tf_op jit(solution)/shard_map/ppermute | solution.py:19
  144.6 1.3 collective-permute-start.5
  147.6 5.0 %collective-permute-done.5 = bf16[1,18,32,128]{3,2,1,0:T(8,128)(2,1)S(1)} collective-permute-done((bf16[1,18,32,128]{3,2,1,0:T(8,128)(2,1)S(1)}, bf16[1,18,32,128]{3,2,1,0:T(8,128)(2,1)S(1)}, u32[]{:S(2)}, u32[]{:S(2)}) %collective-permute-start.5) | collective-permute-done | bytes 147488 | tf_op jit(solution)/shard_map/ppermute | solution.py:22
  152.6 1.0 fusion.64
  154.0 3.7 %collective-permute-start.6 = (bf16[8,1,32,128]{3,2,1,0:T(8,128)(2,1)S(1)}, bf16[8,1,32,128]{3,2,1,0:T(8,128)(2,1)S(1)}, u32[]{:S(2)}, u32[]{:S(2)}) collective-permute-start(bf16[8,1,32,128]{3,2,1,0:T(8,128)(2,1)S(1)} %get-tuple-element.60), channel_id=1, source_target_pairs={{0,1},{1,2},{2,3},{4,5},{5,6},{6,7},{8,9},{9,10},{10,11},{12,13},{... | collective-permute-start | bytes 196616 | tf_op jit(solution)/shard_map/ppermute | solution.py:19
  157.7 1.6 collective-permute-start.7
  160.4 2.8 collective-permute-done.7
  163.3 1.7 copy.122
  166.5 120.1 %all-reduce.4.cloned.1.call-done = f32[27,128,128]{2,1,0:T(8,128)} async-done(((f32[27,128,128]{2,1,0:T(8,128)}), f32[27,128,128]{2,1,0:T(8,128)}) %all-reduce.4.cloned.1.call-update) | async-done | bytes 1769488 | tf_op jit(solution)/shard_map/psum | solution.py:100
  286.6 2.9 broadcast_multiply_fusion
  (218 shorter events, 44.6 us)
Async XLA Ops:
  7.2 279.4 %all-reduce.4.cloned.1.call-start = ((), (), s32[]{:S(2)}) async-start(), calls=%async_computation | async-start | bytes 3538944 | tf_op jit(solution)/shard_map/psum | solution.py:100
  10.3 8.0 %copy-start.60 = (s32[1,1,2]{2,1,0:T(1,128)S(1)}, s32[1,1,2]{2,1,0:T(1,128)}, u32[]{:S(2)}) copy-start(s32[1,1,2]{2,1,0:T(1,128)} %param.13) | copy-start | bytes 28
  10.6 16.1 %collective-permute-start = (bf16[1,16,32,128]{3,0,2,1:T(2,128)(2,1)S(1)}, bf16[1,16,32,128]{3,0,2,1:T(2,128)(2,1)S(1)}, u32[]{:S(2)}, u32[]{:S(2)}) collective-permute-start(bf16[1,16,32,128]{3,0,2,1:T(2,128)(2,1)S(1)} %copy.91), channel_id=1, source_target_pairs={{0,4},{4,8},{8,12},{12,16},{16,20},{20,24},{24,28},{1,5},{5,9},{9,... | collective-permute-start | bytes 393224 | tf_op jit(solution)/shard_map/ppermute | solution.py:19
  15.8 10.9 %collective-permute-start.1 = (bf16[1,16,32,128]{3,0,2,1:T(2,128)(2,1)S(1)}, bf16[1,16,32,128]{3,0,2,1:T(2,128)(2,1)S(1)}, u32[]{:S(2)}, u32[]{:S(2)}) collective-permute-start(bf16[1,16,32,128]{3,0,2,1:T(2,128)(2,1)S(1)} %copy.94), channel_id=1, source_target_pairs={{4,0},{8,4},{12,8},{16,12},{20,16},{24,20},{28,24},{5,1},{9,5},{13... | collective-permute-start | bytes 393224 | tf_op jit(solution)/shard_map/ppermute | solution.py:22
  26.7 8.4 %copy-start.4 = (bf16[1,16,32,128]{3,0,2,1:T(2,128)(2,1)}, bf16[1,16,32,128]{3,0,2,1:T(2,128)(2,1)S(1)}, u32[]{:S(2)}) copy-start(bf16[1,16,32,128]{3,0,2,1:T(2,128)(2,1)S(1)} %collective-permute-done) | copy-start | bytes 393220
  26.7 8.4 %copy-start.5 = (bf16[1,16,32,128]{3,0,2,1:T(2,128)(2,1)}, bf16[1,16,32,128]{3,0,2,1:T(2,128)(2,1)S(1)}, u32[]{:S(2)}) copy-start(bf16[1,16,32,128]{3,0,2,1:T(2,128)(2,1)S(1)} %collective-permute-done.1) | copy-start | bytes 393220
  26.9 8.2 %collective-permute-start.2 = (bf16[10,1,32,128]{3,0,2,1:T(8,128)(2,1)S(1)}, bf16[10,1,32,128]{3,0,2,1:T(8,128)(2,1)S(1)}, u32[]{:S(2)}, u32[]{:S(2)}) collective-permute-start(bf16[10,1,32,128]{3,0,2,1:T(8,128)(2,1)S(1)} %get-tuple-element.58), channel_id=1, source_target_pairs={{0,1},{1,2},{2,3},{4,5},{5,6},{6,7},{8,9},{9,10},{10,11},{12,13},{... | collective-permute-start | bytes 245768 | tf_op jit(solution)/shard_map/ppermute | solution.py:19
  28.2 7.6 %collective-permute-start.3 = (bf16[10,1,32,128]{3,0,2,1:T(8,128)(2,1)S(1)}, bf16[10,1,32,128]{3,0,2,1:T(8,128)(2,1)}, u32[]{:S(2)}, u32[]{:S(2)}) collective-permute-start(bf16[10,1,32,128]{3,0,2,1:T(8,128)(2,1)S(1)} %get-tuple-element.59), channel_id=1, source_target_pairs={{1,0},{2,1},{3,2},{5,4},{6,5},{7,6},{9,8},{10,9},{11,10},{13,12},{... | collective-permute-start | bytes 245768 | tf_op jit(solution)/shard_map/ppermute | solution.py:22
  40.7 1.6 copy-start.2
  40.7 2.3 copy-start.52
  40.7 2.5 copy-start.50
  40.7 2.7 copy-start.48
  40.7 3.0 copy-start.46
  40.7 3.2 %copy-start.44 = (bf16[2,8,8,8,128]{4,1,3,2,0:T(8,128)(2,1)}, bf16[2,8,8,8,128]{4,1,3,2,0:T(8,128)(2,1)S(1)}, u32[]{:S(2)}) copy-start(bf16[2,8,8,8,128]{4,1,3,2,0:T(8,128)(2,1)S(1)} %get-tuple-element.84) | copy-start | bytes 786436
  40.7 3.4 %copy-start.42 = (bf16[2,8,8,8,128]{4,1,3,2,0:T(8,128)(2,1)}, bf16[2,8,8,8,128]{4,1,3,2,0:T(8,128)(2,1)S(1)}, u32[]{:S(2)}) copy-start(bf16[2,8,8,8,128]{4,1,3,2,0:T(8,128)(2,1)S(1)} %get-tuple-element.83) | copy-start | bytes 786436
  40.7 1.8 copy-start.1
  42.1 2.2 copy-start.40
  42.1 2.5 copy-start.38
  42.1 2.7 copy-start.36
  42.1 2.9 copy-start.34
  42.2 3.1 %copy-start.32 = (bf16[2,8,8,8,128]{4,1,3,2,0:T(8,128)(2,1)}, bf16[2,8,8,8,128]{4,1,3,2,0:T(8,128)(2,1)S(1)}, u32[]{:S(2)}) copy-start(bf16[2,8,8,8,128]{4,1,3,2,0:T(8,128)(2,1)S(1)} %get-tuple-element.78) | copy-start | bytes 786436
  42.2 3.4 %copy-start.30 = (bf16[2,8,8,8,128]{4,1,3,2,0:T(8,128)(2,1)}, bf16[2,8,8,8,128]{4,1,3,2,0:T(8,128)(2,1)S(1)}, u32[]{:S(2)}) copy-start(bf16[2,8,8,8,128]{4,1,3,2,0:T(8,128)(2,1)S(1)} %get-tuple-element.77) | copy-start | bytes 786436
  42.2 3.6 %copy-start.28 = (bf16[2,8,8,8,128]{4,1,3,2,0:T(8,128)(2,1)}, bf16[2,8,8,8,128]{4,1,3,2,0:T(8,128)(2,1)S(1)}, u32[]{:S(2)}) copy-start(bf16[2,8,8,8,128]{4,1,3,2,0:T(8,128)(2,1)S(1)} %get-tuple-element.76) | copy-start | bytes 786436
  42.2 3.8 %copy-start.26 = (bf16[2,8,8,8,128]{4,1,3,2,0:T(8,128)(2,1)}, bf16[2,8,8,8,128]{4,1,3,2,0:T(8,128)(2,1)S(1)}, u32[]{:S(2)}) copy-start(bf16[2,8,8,8,128]{4,1,3,2,0:T(8,128)(2,1)S(1)} %get-tuple-element.75) | copy-start | bytes 786436
  42.2 4.0 %copy-start.24 = (bf16[2,8,8,8,128]{4,1,3,2,0:T(8,128)(2,1)}, bf16[2,8,8,8,128]{4,1,3,2,0:T(8,128)(2,1)S(1)}, u32[]{:S(2)}) copy-start(bf16[2,8,8,8,128]{4,1,3,2,0:T(8,128)(2,1)S(1)} %get-tuple-element.74) | copy-start | bytes 786436
  42.2 4.2 %copy-start.22 = (bf16[2,8,8,8,128]{4,1,3,2,0:T(8,128)(2,1)}, bf16[2,8,8,8,128]{4,1,3,2,0:T(8,128)(2,1)S(1)}, u32[]{:S(2)}) copy-start(bf16[2,8,8,8,128]{4,1,3,2,0:T(8,128)(2,1)S(1)} %get-tuple-element.73) | copy-start | bytes 786436
  42.2 4.5 %copy-start.20 = (bf16[2,8,8,8,128]{4,1,3,2,0:T(8,128)(2,1)}, bf16[2,8,8,8,128]{4,1,3,2,0:T(8,128)(2,1)S(1)}, u32[]{:S(2)}) copy-start(bf16[2,8,8,8,128]{4,1,3,2,0:T(8,128)(2,1)S(1)} %get-tuple-element.72) | copy-start | bytes 786436
  42.2 4.7 %copy-start.18 = (bf16[2,8,8,8,128]{4,1,3,2,0:T(8,128)(2,1)}, bf16[2,8,8,8,128]{4,1,3,2,0:T(8,128)(2,1)S(1)}, u32[]{:S(2)}) copy-start(bf16[2,8,8,8,128]{4,1,3,2,0:T(8,128)(2,1)S(1)} %get-tuple-element.71) | copy-start | bytes 786436
  42.2 4.9 %copy-start.16 = (bf16[2,8,8,8,128]{4,1,3,2,0:T(8,128)(2,1)}, bf16[2,8,8,8,128]{4,1,3,2,0:T(8,128)(2,1)S(1)}, u32[]{:S(2)}) copy-start(bf16[2,8,8,8,128]{4,1,3,2,0:T(8,128)(2,1)S(1)} %get-tuple-element.70) | copy-start | bytes 786436
  42.2 5.1 %copy-start.14 = (bf16[2,8,8,8,128]{4,1,3,2,0:T(8,128)(2,1)}, bf16[2,8,8,8,128]{4,1,3,2,0:T(8,128)(2,1)S(1)}, u32[]{:S(2)}) copy-start(bf16[2,8,8,8,128]{4,1,3,2,0:T(8,128)(2,1)S(1)} %get-tuple-element.69) | copy-start | bytes 786436
  42.3 5.4 %copy-start.12 = (bf16[2,8,8,8,128]{4,1,3,2,0:T(8,128)(2,1)}, bf16[2,8,8,8,128]{4,1,3,2,0:T(8,128)(2,1)S(1)}, u32[]{:S(2)}) copy-start(bf16[2,8,8,8,128]{4,1,3,2,0:T(8,128)(2,1)S(1)} %get-tuple-element.68) | copy-start | bytes 786436
  42.3 5.6 %copy-start.10 = (bf16[2,8,8,8,128]{4,1,3,2,0:T(8,128)(2,1)}, bf16[2,8,8,8,128]{4,1,3,2,0:T(8,128)(2,1)S(1)}, u32[]{:S(2)}) copy-start(bf16[2,8,8,8,128]{4,1,3,2,0:T(8,128)(2,1)S(1)} %get-tuple-element.67) | copy-start | bytes 786436
  42.3 5.8 %copy-start.8 = (bf16[2,8,8,8,128]{4,1,3,2,0:T(8,128)(2,1)}, bf16[2,8,8,8,128]{4,1,3,2,0:T(8,128)(2,1)S(1)}, u32[]{:S(2)}) copy-start(bf16[2,8,8,8,128]{4,1,3,2,0:T(8,128)(2,1)S(1)} %get-tuple-element.66) | copy-start | bytes 786436
  42.3 6.1 %copy-start.6 = (bf16[2,8,8,8,128]{4,1,3,2,0:T(8,128)(2,1)}, bf16[2,8,8,8,128]{4,1,3,2,0:T(8,128)(2,1)S(1)}, u32[]{:S(2)}) copy-start(bf16[2,8,8,8,128]{4,1,3,2,0:T(8,128)(2,1)S(1)} %get-tuple-element.65) | copy-start | bytes 786436
  42.3 6.3 %copy-start.55 = (bf16[2,8,8,8,128]{4,1,3,2,0:T(8,128)(2,1)}, bf16[2,8,8,8,128]{4,1,3,2,0:T(8,128)(2,1)S(1)}, u32[]{:S(2)}) copy-start(bf16[2,8,8,8,128]{4,1,3,2,0:T(8,128)(2,1)S(1)} %get-tuple-element.64) | copy-start | bytes 786436
  48.1 1.0 copy-start.61
  112.6 2.9 copy-start
  115.5 0.9 copy-start.3
  116.4 0.9 copy-start.53
  117.4 0.9 copy-start.51
  118.3 0.9 copy-start.49
  139.3 6.6 %copy-start.56 = (bf16[2,8,8,8,128]{4,1,3,2,0:T(8,128)(2,1)S(1)}, bf16[2,8,8,8,128]{4,1,3,2,0:T(8,128)(2,1)}, u32[]{:S(2)}) copy-start(bf16[2,8,8,8,128]{4,1,3,2,0:T(8,128)(2,1)} %copy-done.55) | copy-start | bytes 786436
  140.3 7.3 %collective-permute-start.4 = (bf16[1,18,32,128]{3,2,1,0:T(8,128)(2,1)S(1)}, bf16[1,18,32,128]{3,2,1,0:T(8,128)(2,1)S(1)}, u32[]{:S(2)}, u32[]{:S(2)}) collective-permute-start(bf16[1,18,32,128]{3,2,1,0:T(8,128)(2,1)S(1)} %get-tuple-element.56), channel_id=1, source_target_pairs={{0,4},{4,8},{8,12},{12,16},{16,20},{20,24},{24,28},{1,5},{5,9},{9,... | collective-permute-start | bytes 442376 | tf_op jit(solution)/shard_map/ppermute | solution.py:19
  144.6 8.0 %collective-permute-start.5 = (bf16[1,18,32,128]{3,2,1,0:T(8,128)(2,1)S(1)}, bf16[1,18,32,128]{3,2,1,0:T(8,128)(2,1)S(1)}, u32[]{:S(2)}, u32[]{:S(2)}) collective-permute-start(bf16[1,18,32,128]{3,2,1,0:T(8,128)(2,1)S(1)} %get-tuple-element.57), channel_id=1, source_target_pairs={{4,0},{8,4},{12,8},{16,12},{20,16},{24,20},{28,24},{5,1},{9,5},{13... | collective-permute-start | bytes 442376 | tf_op jit(solution)/shard_map/ppermute | solution.py:22
  153.7 5.6 %copy-start.54 = (f32[2,8,8,8,128]{4,3,2,1,0:T(8,128)S(1)}, f32[2,8,8,8,128]{4,3,2,1,0:T(8,128)}, u32[]{:S(2)}) copy-start(f32[2,8,8,8,128]{4,3,2,1,0:T(8,128)} %get-tuple-element.97) | copy-start | bytes 1572868
  154.0 6.4 %collective-permute-start.6 = (bf16[8,1,32,128]{3,2,1,0:T(8,128)(2,1)S(1)}, bf16[8,1,32,128]{3,2,1,0:T(8,128)(2,1)S(1)}, u32[]{:S(2)}, u32[]{:S(2)}) collective-permute-start(bf16[8,1,32,128]{3,2,1,0:T(8,128)(2,1)S(1)} %get-tuple-element.60), channel_id=1, source_target_pairs={{0,1},{1,2},{2,3},{4,5},{5,6},{6,7},{8,9},{9,10},{10,11},{12,13},{... | collective-permute-start | bytes 196616 | tf_op jit(solution)/shard_map/ppermute | solution.py:19
  157.7 5.5 %collective-permute-start.7 = (bf16[8,1,32,128]{3,2,1,0:T(8,128)(2,1)S(1)}, bf16[8,1,32,128]{3,2,1,0:T(8,128)(2,1)S(1)}, u32[]{:S(2)}, u32[]{:S(2)}) collective-permute-start(bf16[8,1,32,128]{3,2,1,0:T(8,128)(2,1)S(1)} %get-tuple-element.61), channel_id=1, source_target_pairs={{1,0},{2,1},{3,2},{5,4},{6,5},{7,6},{9,8},{10,9},{11,10},{13,12},{... | collective-permute-start | bytes 196616 | tf_op jit(solution)/shard_map/ppermute | solution.py:22
  163.3 1.7 copy-start.58
  (23 other events, 21.2 us)
Sparse Core Ops, SparseCore 0:
  146.9 139.6 all-reduce.3
where the time goes:
time: 298 us; the launch traced here: 296 us
  waiting for transfers between devices  133 us (45%)
  matrix products  78.7 us (26%)
  local copies, waits for them, and re-layouts  28.8 us (10%)
  between operations  22.5 us (8%)
  starting transfers between devices  19.7 us (7%)
  other arithmetic  13.9 us (5%)
    psum x1, waiting for transfers between devices, local(): total_kernel = lax.psum(local_kernel, ('gz', 'gy'))  120 us
    dot_general x27, matrix products, local(): jnp.einsum('nzyxd,cd->nzyxc', view, kernel[t], preferred_element_type=jnp...  47.3 us
    dot_general x27, matrix products, local(): jnp.einsum('nzyxc,nzyxd->cd', view, dpre_cube, preferred_element_type=jnp...  24.5 us
    ppermute x4, starting transfers between devices, padded(): lax.ppermute(lax.slice_in_dim(block, block.shape[dim] - width, None, axis...  14.2 us
    dynamic_update_slice x2, local copies, waits for them, and re-layouts, local(): canvas = lax.dynamic_update_slice(canvas, piece + spread[slot], start)  10.6 us
    ppermute x4, waiting for transfers between devices, padded(): lax.ppermute(lax.slice_in_dim(block, 0, width, axis=dim), axis, backward)  7.84 us
    dot_general x27, matrix products, local(): jnp.einsum('nzyxc,cd->nzyxd', view, kernel[t], preferred_element_type=jnp...  6.88 us
  transfers between devices with their start and end apart: 9, of which 5 were waited for; matrix products, arithmetic and copies ran while one was open for 4% of the time, Pallas kernels for 0%

commit v1 on v0

--- a/solution.py
+++ b/solution.py
@@ -22,6 +22,81 @@
         high = lax.ppermute(lax.slice_in_dim(block, 0, width, axis=dim), axis, backward)
         block = jnp.concatenate([low, block, high], axis=dim)
     return block
+
+
+AXES = ("gz", "gy")
+
+
+def exchange_plan():
+    gz_bits = [("gz", b) for b in range(lax.axis_size("gz").bit_length() - 1)]
+    gy_bits = [("gy", b) for b in range(lax.axis_size("gy").bit_length() - 1)]
+    groups, gy_bits = [(gy_bits[0],)], gy_bits[1:]
+    while gy_bits and gz_bits:
+        groups.append((gy_bits.pop(0), gz_bits.pop(0)))
+    rest = gy_bits + gz_bits
+    while rest:
+        groups.append(tuple(rest[:2]))
+        rest = rest[2:]
+    return groups
+
+
+def swap_with(value, group, pattern):
+    nz, ny = lax.axis_size("gz"), lax.axis_size("gy")
+    flip = {"gz": 0, "gy": 0}
+    for k, (axis, bit) in enumerate(group):
+        if pattern >> k & 1:
+            flip[axis] |= 1 << bit
+    pairs = [
+        (z * ny + y, (z ^ flip["gz"]) * ny + (y ^ flip["gy"]))
+        for z in range(nz)
+        for y in range(ny)
+    ]
+    return lax.ppermute(value, AXES, pairs)
+
+
+def place_in(group):
+    place = jnp.zeros((), jnp.int32)
+    for k, (axis, bit) in enumerate(group):
+        place = place | (((lax.axis_index(axis) >> bit) & 1) << k)
+    return place
+
+
+def scatter_sum(total, plan):
+    for level, group in enumerate(plan):
+        kind = jnp.float32 if level == 0 else jnp.bfloat16
+        count = 1 << len(group)
+        me = place_in(group)
+        parts = total.reshape(count, -1, C)
+        arrived = [
+            swap_with(lax.dynamic_index_in_dim(parts, me ^ p, 0, False).astype(kind), group, p)
+            for p in range(1, count)
+        ]
+        total = lax.dynamic_index_in_dim(parts, me, 0, False)
+        for piece in arrived:
+            total = total + piece.astype(jnp.float32)
+    return total
+
+
+def gather_parts(piece, plan):
+    for group in reversed(plan):
+        pieces = [piece] + [swap_with(piece, group, p) for p in range(1, 1 << len(group))]
+        piece = jnp.concatenate(pieces)
+    bits = [b for group in plan for b in reversed(group)]
+    piece = piece.reshape((2,) * len(bits) + (-1, C))
+    for dim, (axis, bit) in enumerate(bits):
+        odd = (lax.axis_index(axis) >> bit) & 1
+        piece = jnp.where(odd == 1, jnp.flip(piece, dim), piece)
+    return piece.reshape(-1, C)
+
+
+def sum_over_all(value, scale):
+    plan = exchange_plan()
+    devices = lax.axis_size("gz") * lax.axis_size("gy")
+    rows = value.shape[0] * C
+    padded_rows = -(-rows // (16 * devices)) * 16 * devices
+    flat = jnp.pad(value.reshape(rows, C), ((0, padded_rows - rows), (0, 0)))
+    mine = (scatter_sum(flat, plan) * scale).astype(jnp.bfloat16)
+    return gather_parts(mine, plan)[:rows].reshape(value.shape).astype(jnp.float32)
 
 
 def tap_offsets():
@@ -97,9 +172,8 @@
     core = core.at[:, 0].add(beside[:, 0]).at[:, -1].add(beside[:, 3])
     grad = cut_cubes(core, rows_start, cols_start, 8)
     grad_in = jnp.where(valid, grad.reshape(NB, VOX, C), 0.0).astype(jnp.bfloat16)
-    total_kernel = lax.psum(local_kernel, ("gz", "gy"))
-    count = jnp.float32(NB * VOX * lax.axis_size("gz") * lax.axis_size("gy"))
-    grad_kernel = total_kernel / jnp.sqrt(count)
+    count = NB * VOX * lax.axis_size("gz") * lax.axis_size("gy")
+    grad_kernel = sum_over_all(local_kernel, 1.0 / count**0.5)
     return (act[None, None], grad_in[None, None], grad_kernel)
 
 

time: 298 us -> 195 us (0.65)
  waiting for transfers between devices: 133 us -> 25.3 us
  starting transfers between devices: 19.7 us -> 37.6 us
  local copies, waits for them, and re-layouts: 28.8 us -> 46.2 us
  matrix products: 78.7 us -> 62.1 us
  between operations: 22.5 us -> 9.84 us
    psum x1 -> x0, waiting for transfers between devices: 120 us -> none  [local(): total_kernel = lax.psum(local_kernel, ('gz', 'gy'))]
    ppermute x0 -> x14, starting transfers between devices: none -> 21 us  [swap_with(): return lax.ppermute(value, AXES, pairs)]
    dot_general x27, matrix products: 24.5 us -> 8.05 us  [local(): jnp.einsum('nzyxc,nzyxd->cd', view, dpre_cube, preferred_element_type=jnp...]
    unnamed x124 -> x132, local copies, waits for them, and re-layouts: 3.74 us -> 20.2 us
    ppermute x0 -> x14, waiting for transfers between devices: none -> 14.8 us  [swap_with(): return lax.ppermute(value, AXES, pairs)]
    ppermute x4, starting transfers between devices: 14.2 us -> 11.2 us  [padded(): lax.ppermute(lax.slice_in_dim(block, block.shape[dim] - width, None, axis...]
  transfers between devices with their start and end apart: 9 -> 22, of which waited for: 5 -> 12; matrix products, arithmetic and copies ran while one was open for 4% -> 5% of each run, Pallas kernels for 0% -> 0%
where the time goes in v1:
time: 195 us; the launch traced here: 194 us
  matrix products  62.1 us (32%)
  local copies, waits for them, and re-layouts  46.2 us (24%)
  starting transfers between devices  37.6 us (19%)
  waiting for transfers between devices  25.3 us (13%)
  other arithmetic  12.5 us (6%)
  between operations  9.84 us (5%)
    dot_general x27, matrix products, local(): jnp.einsum('nzyxd,cd->nzyxc', view, kernel[t], preferred_element_type=jnp...  47.2 us
    ppermute x14, starting transfers between devices, swap_with(): return lax.ppermute(value, AXES, pairs)  21 us
    unnamed x132, local copies, waits for them, and re-layouts  20.2 us
    ppermute x14, waiting for transfers between devices, swap_with(): return lax.ppermute(value, AXES, pairs)  14.8 us
    ppermute x4, starting transfers between devices, padded(): lax.ppermute(lax.slice_in_dim(block, block.shape[dim] - width, None, axis...  11.2 us
    dynamic_update_slice x2, local copies, waits for them, and re-layouts, local(): canvas = lax.dynamic_update_slice(canvas, piece + spread[slot], start)  11.1 us
    dot_general x27, matrix products, local(): jnp.einsum('nzyxc,nzyxd->cd', view, dpre_cube, preferred_element_type=jnp...  8.05 us
    dot_general x27, matrix products, local(): jnp.einsum('nzyxc,cd->nzyxd', view, kernel[t], preferred_element_type=jnp...  6.86 us
  transfers between devices with their start and end apart: 22, of which 12 were waited for; matrix products, arithmetic and copies ran while one was open for 5% of the time, Pallas kernels for 0%

profile of v1, /device:TPU:0, one launch (start us, length us, event | category | flops | bytes accessed | tf_op | source)
XLA Modules:
  0.0 193.6 jit_solution(11628305396784305091)
XLA Ops:
  2.0 1.5 scatter_fusion
  4.0 4.9 %collective-permute-start = (bf16[1,16,32,128]{3,0,2,1:T(2,128)(2,1)S(1)}, bf16[1,16,32,128]{3,0,2,1:T(2,128)(2,1)S(1)}, u32[]{:S(2)}, u32[]{:S(2)}) collective-permute-start(bf16[1,16,32,128]{3,0,2,1:T(2,128)(2,1)S(1)} %copy.91), channel_id=1, source_target_pairs={{0,4},{4,8},{8,12},{12,16},{16,20},{20,24},{24,28},{1,5},{5,9},{9,... | collective-permute-start | bytes 393224 | tf_op jit(solution)/shard_map/ppermute | solution.py:19
  16.2 3.8 %collective-permute-done = bf16[1,16,32,128]{3,0,2,1:T(2,128)(2,1)S(1)} collective-permute-done((bf16[1,16,32,128]{3,0,2,1:T(2,128)(2,1)S(1)}, bf16[1,16,32,128]{3,0,2,1:T(2,128)(2,1)S(1)}, u32[]{:S(2)}, u32[]{:S(2)}) %collective-permute-start) | collective-permute-done | bytes 131104 | tf_op jit(solution)/shard_map/ppermute | solution.py:19
  29.4 3.7 %select_maximum_fusion = bf16[10,18,34,128]{3,0,2,1:T(8,128)(2,1)S(1)} fusion(bf16[10,1,32,128]{3,0,2,1:T(8,128)(2,1)} %collective-permute-done.3, bf16[10,1,32,128]{3,0,2,1:T(8,128)(2,1)} %copy-done.58, bf16[1,16,32,128]{3,0,2,1:T(2,128)(2,1)} %copy-done.4, bf16[8,16,32,128]{3,0,2,1:T(8,128)(2,1)S(1)} %bitcast.555, bf16[1,16,32,128]{3,0,2,1:T(2,128)(2,1)} %copy-done.3), kind=kLoop, calls=%fused_computation.33 | loop fusion | flops 14100480 | bytes 3041280 | tf_op jit(solution)/shard_map/concatenate | solution.py:23
  46.7 1.5 fusion.38
  48.2 1.5 fusion.39
  49.8 1.6 fusion.40
  51.4 1.6 fusion.41
  52.9 1.6 fusion.42
  54.5 1.6 fusion.43
  56.0 1.6 fusion.44
  57.7 1.5 fusion.45
  59.2 1.6 fusion.46
  60.8 1.5 fusion.47
  62.3 1.6 fusion.48
  63.9 1.5 fusion.49
  65.4 1.6 fusion.50
  67.0 1.5 fusion.51
  68.5 1.6 fusion.52
  70.1 1.5 fusion.53
  71.7 1.6 fusion.54
  73.3 1.6 fusion.55
  74.9 1.8 fusion.56
  76.7 1.5 fusion.57
  78.3 1.5 fusion.58
  79.8 12.2 %add_add_fusion = f32[2,10,10,10,128]{4,3,2,1,0:T(8,128)S(1)} fusion(f32[2,10,10,10,128]{4,3,2,1,0:T(8,128)} %fusion.58, f32[2,10,10,10,128]{4,3,2,1,0:T(8,128)} %fusion.57, f32[2,10,10,10,128]{4,3,2,1,0:T(8,128)} %fusion.56, f32[2,10,10,10,128]{4,3,2,1,0:T(8,128)} %fusion.55, f32[2,10,10,10,128]{4,3,2,1,0:T(8,128)} %fusion.54, ...), kind=kOutput, calls=%fused_computation.40 | convolution fusion | flops 72192000 | bytes 31014912 | tf_op jit(solution)/shard_map/nzyxd,cd->nzyxc/dot_general | solution.py:155
  92.1 2.1 %broadcast_in_dim.41 = f32[10,18,34,128]{3,2,1,0:T(8,128)} broadcast(f32[]{:T(128)} %constant.196.clone.1), dimensions={} | broadcast | bytes 3133444 | tf_op jit(solution)/shard_map/broadcast_in_dim | solution.py:158
  94.1 5.6 %dynamic_update_slice.6 = f32[10,18,34,128]{3,2,1,0:T(8,128)} dynamic-update-slice(f32[10,18,34,128]{3,2,1,0:T(8,128)} %broadcast_in_dim.41, f32[10,10,10,128]{3,2,1,0:T(8,128)S(1)} %slice_bitcast_fusion.1, s32[]{:T(128)} %constant.185.clone.1, s32[]{:T(128)S(6)} %select_n.200, s32[]{:T(128)S(6)} %select_n.202, s32[]{:T(128)} %constant.185.clone.1) | dynamic-update-slice | bytes 1024004 | tf_op jit(solution)/shard_map/dynamic_update_slice | solution.py:163
  99.8 1.4 fusion.59
  101.2 5.5 %dynamic_update_slice.7 = f32[10,18,34,128]{3,2,1,0:T(8,128)} dynamic-update-slice(f32[10,18,34,128]{3,2,1,0:T(8,128)} %dynamic_update_slice.6, f32[10,10,10,128]{3,2,1,0:T(8,128)S(1)} %fusion.59, s32[]{:T(128)} %constant.185.clone.1, s32[]{:T(128)S(6)} %select_n.203, s32[]{:T(128)S(6)} %select_n.204, s32[]{:T(128)} %constant.185.clone.1) | dynamic-update-slice | bytes 1024004 | tf_op jit(solution)/shard_map/dynamic_update_slice | solution.py:163
  106.7 2.3 %slice.640 = f32[8,18,32,128]{3,2,1,0:T(8,128)S(1)} slice(f32[10,18,34,128]{3,2,1,0:T(8,128)} %dynamic_update_slice.7), slice={[1:9], [0:18], [1:33], [0:128]} | slice | bytes 4718592 | tf_op jit(solution)/shard_map/slice | solution.py:167
  135.4 2.9 %collective-permute-start.8 = (f32[1792,128]{1,0:T(8,128)S(1)}, f32[1792,128]{1,0:T(8,128)S(1)}, u32[]{:S(2)}, u32[]{:S(2)}) collective-permute-start(f32[1792,128]{1,0:T(8,128)S(1)} %dynamic-slice_bitcast_fusion), channel_id=1, source_target_pairs={{0,1},{1,0},{2,3},{3,2},{4,5},{5,4},{6,7},{7,6},{8,9},{9,8},{10,11... | collective-permute-start | bytes 2752520 | tf_op jit(solution)/shard_map/ppermute | solution.py:54
  138.4 3.7 %collective-permute-start.4 = (bf16[1,18,32,128]{3,2,1,0:T(8,128)(2,1)S(1)}, bf16[1,18,32,128]{3,2,1,0:T(8,128)(2,1)S(1)}, u32[]{:S(2)}, u32[]{:S(2)}) collective-permute-start(bf16[1,18,32,128]{3,2,1,0:T(8,128)(2,1)S(1)} %get-tuple-element.58), channel_id=1, source_target_pairs={{0,4},{4,8},{8,12},{12,16},{16,20},{20,24},{24,28},{1,5},{5,9},{9,... | collective-permute-start | bytes 442376 | tf_op jit(solution)/shard_map/ppermute | solution.py:19
  145.4 5.6 %collective-permute-done.5 = bf16[1,18,32,128]{3,2,1,0:T(8,128)(2,1)S(1)} collective-permute-done((bf16[1,18,32,128]{3,2,1,0:T(8,128)(2,1)S(1)}, bf16[1,18,32,128]{3,2,1,0:T(8,128)(2,1)S(1)}, u32[]{:S(2)}, u32[]{:S(2)}) %collective-permute-start.5) | collective-permute-done | bytes 147488 | tf_op jit(solution)/shard_map/ppermute | solution.py:22
  151.5 2.7 %collective-permute-start.10 = (bf16[448,128]{1,0:T(8,128)(2,1)S(1)}, bf16[448,128]{1,0:T(8,128)(2,1)S(1)}, u32[]{:S(2)}, u32[]{:S(2)}) collective-permute-start(bf16[448,128]{1,0:T(8,128)(2,1)S(1)} %get-tuple-element.68), channel_id=1, source_target_pairs={{0,4},{1,5},{2,6},{3,7},{4,0},{5,1},{6,2},{7,3},{8,12},{9,13},{10,... | collective-permute-start | bytes 344072 | tf_op jit(solution)/shard_map/ppermute | solution.py:54
  157.3 1.6 collective-permute-start.7
  160.4 2.8 %collective-permute-start.12 = (bf16[112,128]{1,0:T(8,128)(2,1)S(1)}, bf16[112,128]{1,0:T(8,128)(2,1)S(1)}, u32[]{:S(2)}, u32[]{:S(2)}) collective-permute-start(bf16[112,128]{1,0:T(8,128)(2,1)S(1)} %get-tuple-element.96), channel_id=1, source_target_pairs={{0,8},{1,9},{2,10},{3,11},{4,12},{5,13},{6,14},{7,15},{8,0},{9,1},... | collective-permute-start | bytes 86024 | tf_op jit(solution)/shard_map/ppermute | solution.py:54
  163.2 1.8 collective-permute-start.13
  165.7 2.7 %collective-permute-done.13 = bf16[112,128]{1,0:T(8,128)(2,1)S(1)} collective-permute-done((bf16[112,128]{1,0:T(8,128)(2,1)S(1)}, bf16[112,128]{1,0:T(8,128)(2,1)S(1)}, u32[]{:S(2)}, u32[]{:S(2)}) %collective-permute-start.13) | collective-permute-done | bytes 28704 | tf_op jit(solution)/shard_map/ppermute | solution.py:54
  168.4 2.3 %collective-permute-done.14 = bf16[112,128]{1,0:T(8,128)(2,1)S(1)} collective-permute-done((bf16[112,128]{1,0:T(8,128)(2,1)S(1)}, bf16[112,128]{1,0:T(8,128)(2,1)S(1)}, u32[]{:S(2)}, u32[]{:S(2)}) %collective-permute-start.14) | collective-permute-done | bytes 28704 | tf_op jit(solution)/shard_map/ppermute | solution.py:54
  170.8 1.5 collective-permute-start.16
  172.3 2.9 %collective-permute-start.17 = (bf16[112,128]{1,0:T(8,128)(2,1)S(1)}, bf16[112,128]{1,0:T(8,128)(2,1)S(1)}, u32[]{:S(2)}, u32[]{:S(2)}) collective-permute-start(bf16[112,128]{1,0:T(8,128)(2,1)S(1)} %get-tuple-element.52), channel_id=1, source_target_pairs={{0,24},{1,25},{2,26},{3,27},{4,28},{5,29},{6,30},{7,31},{8,16},{9,... | collective-permute-start | bytes 86024 | tf_op jit(solution)/shard_map/ppermute | solution.py:54
  175.8 2.1 %collective-permute-done.17 = bf16[112,128]{1,0:T(8,128)(2,1)S(1)} collective-permute-done((bf16[112,128]{1,0:T(8,128)(2,1)S(1)}, bf16[112,128]{1,0:T(8,128)(2,1)S(1)}, u32[]{:S(2)}, u32[]{:S(2)}) %collective-permute-start.17) | collective-permute-done | bytes 28704 | tf_op jit(solution)/shard_map/ppermute | solution.py:54
  178.0 2.6 %collective-permute-start.18 = (bf16[448,128]{1,0:T(8,128)(2,1)S(1)}, bf16[448,128]{1,0:T(8,128)(2,1)S(1)}, u32[]{:S(2)}, u32[]{:S(2)}) collective-permute-start(bf16[448,128]{1,0:T(8,128)(2,1)S(1)} %pad_maximum_fusion.6), channel_id=1, source_target_pairs={{0,2},{1,3},{2,0},{3,1},{4,6},{5,7},{6,4},{7,5},{8,10},{9,11},{10,... | collective-permute-start | bytes 344072 | tf_op jit(solution)/shard_map/ppermute | solution.py:54
  180.6 1.5 collective-permute-start.19
  183.4 2.0 %collective-permute-done.19 = bf16[448,128]{1,0:T(8,128)(2,1)S(1)} collective-permute-done((bf16[448,128]{1,0:T(8,128)(2,1)S(1)}, bf16[448,128]{1,0:T(8,128)(2,1)S(1)}, u32[]{:S(2)}, u32[]{:S(2)}) %collective-permute-start.19) | collective-permute-done | bytes 114720 | tf_op jit(solution)/shard_map/ppermute | solution.py:54
  185.4 2.3 %collective-permute-done.20 = bf16[448,128]{1,0:T(8,128)(2,1)S(1)} collective-permute-done((bf16[448,128]{1,0:T(8,128)(2,1)S(1)}, bf16[448,128]{1,0:T(8,128)(2,1)S(1)}, u32[]{:S(2)}, u32[]{:S(2)}) %collective-permute-start.20) | collective-permute-done | bytes 114720 | tf_op jit(solution)/shard_map/ppermute | solution.py:54
  187.9 1.7 copy.122
  (267 shorter events, 64.9 us)
Async XLA Ops:
  3.7 8.1 %copy-start.61 = (s32[1,1,2]{2,1,0:T(1,128)S(1)}, s32[1,1,2]{2,1,0:T(1,128)}, u32[]{:S(2)}) copy-start(s32[1,1,2]{2,1,0:T(1,128)} %param.13) | copy-start | bytes 28
  4.0 16.1 %collective-permute-start = (bf16[1,16,32,128]{3,0,2,1:T(2,128)(2,1)S(1)}, bf16[1,16,32,128]{3,0,2,1:T(2,128)(2,1)S(1)}, u32[]{:S(2)}, u32[]{:S(2)}) collective-permute-start(bf16[1,16,32,128]{3,0,2,1:T(2,128)(2,1)S(1)} %copy.91), channel_id=1, source_target_pairs={{0,4},{4,8},{8,12},{12,16},{16,20},{20,24},{24,28},{1,5},{5,9},{9,... | collective-permute-start | bytes 393224 | tf_op jit(solution)/shard_map/ppermute | solution.py:19
  9.2 10.9 %collective-permute-start.1 = (bf16[1,16,32,128]{3,0,2,1:T(2,128)(2,1)S(1)}, bf16[1,16,32,128]{3,0,2,1:T(2,128)(2,1)S(1)}, u32[]{:S(2)}, u32[]{:S(2)}) collective-permute-start(bf16[1,16,32,128]{3,0,2,1:T(2,128)(2,1)S(1)} %copy.94), channel_id=1, source_target_pairs={{4,0},{8,4},{12,8},{16,12},{20,16},{24,20},{28,24},{5,1},{9,5},{13... | collective-permute-start | bytes 393224 | tf_op jit(solution)/shard_map/ppermute | solution.py:22
  20.0 8.7 %copy-start.3 = (bf16[1,16,32,128]{3,0,2,1:T(2,128)(2,1)}, bf16[1,16,32,128]{3,0,2,1:T(2,128)(2,1)S(1)}, u32[]{:S(2)}) copy-start(bf16[1,16,32,128]{3,0,2,1:T(2,128)(2,1)S(1)} %collective-permute-done) | copy-start | bytes 393220
  20.0 8.7 %copy-start.4 = (bf16[1,16,32,128]{3,0,2,1:T(2,128)(2,1)}, bf16[1,16,32,128]{3,0,2,1:T(2,128)(2,1)S(1)}, u32[]{:S(2)}) copy-start(bf16[1,16,32,128]{3,0,2,1:T(2,128)(2,1)S(1)} %collective-permute-done.1) | copy-start | bytes 393220
  20.2 8.5 %collective-permute-start.2 = (bf16[10,1,32,128]{3,0,2,1:T(8,128)(2,1)S(1)}, bf16[10,1,32,128]{3,0,2,1:T(8,128)(2,1)S(1)}, u32[]{:S(2)}, u32[]{:S(2)}) collective-permute-start(bf16[10,1,32,128]{3,0,2,1:T(8,128)(2,1)S(1)} %get-tuple-element.60), channel_id=1, source_target_pairs={{0,1},{1,2},{2,3},{4,5},{5,6},{6,7},{8,9},{9,10},{10,11},{12,13},{... | collective-permute-start | bytes 245768 | tf_op jit(solution)/shard_map/ppermute | solution.py:19
  21.5 7.9 %collective-permute-start.3 = (bf16[10,1,32,128]{3,0,2,1:T(8,128)(2,1)S(1)}, bf16[10,1,32,128]{3,0,2,1:T(8,128)(2,1)}, u32[]{:S(2)}, u32[]{:S(2)}) collective-permute-start(bf16[10,1,32,128]{3,0,2,1:T(8,128)(2,1)S(1)} %get-tuple-element.61), channel_id=1, source_target_pairs={{1,0},{2,1},{3,2},{5,4},{6,5},{7,6},{9,8},{10,9},{11,10},{13,12},{... | collective-permute-start | bytes 245768 | tf_op jit(solution)/shard_map/ppermute | solution.py:22
  34.4 2.7 %copy-start.49 = (bf16[2,8,8,8,128]{4,1,3,2,0:T(8,128)(2,1)}, bf16[2,8,8,8,128]{4,1,3,2,0:T(8,128)(2,1)S(1)}, u32[]{:S(2)}) copy-start(bf16[2,8,8,8,128]{4,1,3,2,0:T(8,128)(2,1)S(1)} %get-tuple-element.91) | copy-start | bytes 786436
  34.4 2.9 %copy-start.47 = (bf16[2,8,8,8,128]{4,1,3,2,0:T(8,128)(2,1)}, bf16[2,8,8,8,128]{4,1,3,2,0:T(8,128)(2,1)S(1)}, u32[]{:S(2)}) copy-start(bf16[2,8,8,8,128]{4,1,3,2,0:T(8,128)(2,1)S(1)} %get-tuple-element.90) | copy-start | bytes 786436
  34.4 3.2 %copy-start.45 = (bf16[2,8,8,8,128]{4,1,3,2,0:T(8,128)(2,1)}, bf16[2,8,8,8,128]{4,1,3,2,0:T(8,128)(2,1)S(1)}, u32[]{:S(2)}) copy-start(bf16[2,8,8,8,128]{4,1,3,2,0:T(8,128)(2,1)S(1)} %get-tuple-element.89) | copy-start | bytes 786436
  34.4 3.4 %copy-start.43 = (bf16[2,8,8,8,128]{4,1,3,2,0:T(8,128)(2,1)}, bf16[2,8,8,8,128]{4,1,3,2,0:T(8,128)(2,1)S(1)}, u32[]{:S(2)}) copy-start(bf16[2,8,8,8,128]{4,1,3,2,0:T(8,128)(2,1)S(1)} %get-tuple-element.88) | copy-start | bytes 786436
  35.8 2.7 %copy-start.37 = (bf16[2,8,8,8,128]{4,1,3,2,0:T(8,128)(2,1)}, bf16[2,8,8,8,128]{4,1,3,2,0:T(8,128)(2,1)S(1)}, u32[]{:S(2)}) copy-start(bf16[2,8,8,8,128]{4,1,3,2,0:T(8,128)(2,1)S(1)} %get-tuple-element.85) | copy-start | bytes 786436
  35.8 2.9 %copy-start.35 = (bf16[2,8,8,8,128]{4,1,3,2,0:T(8,128)(2,1)}, bf16[2,8,8,8,128]{4,1,3,2,0:T(8,128)(2,1)S(1)}, u32[]{:S(2)}) copy-start(bf16[2,8,8,8,128]{4,1,3,2,0:T(8,128)(2,1)S(1)} %get-tuple-element.84) | copy-start | bytes 786436
  35.8 3.1 %copy-start.33 = (bf16[2,8,8,8,128]{4,1,3,2,0:T(8,128)(2,1)}, bf16[2,8,8,8,128]{4,1,3,2,0:T(8,128)(2,1)S(1)}, u32[]{:S(2)}) copy-start(bf16[2,8,8,8,128]{4,1,3,2,0:T(8,128)(2,1)S(1)} %get-tuple-element.83) | copy-start | bytes 786436
  35.8 3.3 %copy-start.31 = (bf16[2,8,8,8,128]{4,1,3,2,0:T(8,128)(2,1)}, bf16[2,8,8,8,128]{4,1,3,2,0:T(8,128)(2,1)S(1)}, u32[]{:S(2)}) copy-start(bf16[2,8,8,8,128]{4,1,3,2,0:T(8,128)(2,1)S(1)} %get-tuple-element.82) | copy-start | bytes 786436
  35.8 3.6 %copy-start.29 = (bf16[2,8,8,8,128]{4,1,3,2,0:T(8,128)(2,1)}, bf16[2,8,8,8,128]{4,1,3,2,0:T(8,128)(2,1)S(1)}, u32[]{:S(2)}) copy-start(bf16[2,8,8,8,128]{4,1,3,2,0:T(8,128)(2,1)S(1)} %get-tuple-element.81) | copy-start | bytes 786436
  35.8 3.8 %copy-start.27 = (bf16[2,8,8,8,128]{4,1,3,2,0:T(8,128)(2,1)}, bf16[2,8,8,8,128]{4,1,3,2,0:T(8,128)(2,1)S(1)}, u32[]{:S(2)}) copy-start(bf16[2,8,8,8,128]{4,1,3,2,0:T(8,128)(2,1)S(1)} %get-tuple-element.80) | copy-start | bytes 786436
  35.8 4.0 %copy-start.25 = (bf16[2,8,8,8,128]{4,1,3,2,0:T(8,128)(2,1)}, bf16[2,8,8,8,128]{4,1,3,2,0:T(8,128)(2,1)S(1)}, u32[]{:S(2)}) copy-start(bf16[2,8,8,8,128]{4,1,3,2,0:T(8,128)(2,1)S(1)} %get-tuple-element.79) | copy-start | bytes 786436
  35.9 4.2 %copy-start.23 = (bf16[2,8,8,8,128]{4,1,3,2,0:T(8,128)(2,1)}, bf16[2,8,8,8,128]{4,1,3,2,0:T(8,128)(2,1)S(1)}, u32[]{:S(2)}) copy-start(bf16[2,8,8,8,128]{4,1,3,2,0:T(8,128)(2,1)S(1)} %get-tuple-element.78) | copy-start | bytes 786436
  35.9 4.5 %copy-start.21 = (bf16[2,8,8,8,128]{4,1,3,2,0:T(8,128)(2,1)}, bf16[2,8,8,8,128]{4,1,3,2,0:T(8,128)(2,1)S(1)}, u32[]{:S(2)}) copy-start(bf16[2,8,8,8,128]{4,1,3,2,0:T(8,128)(2,1)S(1)} %get-tuple-element.77) | copy-start | bytes 786436
  35.9 4.7 %copy-start.19 = (bf16[2,8,8,8,128]{4,1,3,2,0:T(8,128)(2,1)}, bf16[2,8,8,8,128]{4,1,3,2,0:T(8,128)(2,1)S(1)}, u32[]{:S(2)}) copy-start(bf16[2,8,8,8,128]{4,1,3,2,0:T(8,128)(2,1)S(1)} %get-tuple-element.76) | copy-start | bytes 786436
  35.9 4.9 %copy-start.17 = (bf16[2,8,8,8,128]{4,1,3,2,0:T(8,128)(2,1)}, bf16[2,8,8,8,128]{4,1,3,2,0:T(8,128)(2,1)S(1)}, u32[]{:S(2)}) copy-start(bf16[2,8,8,8,128]{4,1,3,2,0:T(8,128)(2,1)S(1)} %get-tuple-element.75) | copy-start | bytes 786436
  35.9 5.1 %copy-start.15 = (bf16[2,8,8,8,128]{4,1,3,2,0:T(8,128)(2,1)}, bf16[2,8,8,8,128]{4,1,3,2,0:T(8,128)(2,1)S(1)}, u32[]{:S(2)}) copy-start(bf16[2,8,8,8,128]{4,1,3,2,0:T(8,128)(2,1)S(1)} %get-tuple-element.74) | copy-start | bytes 786436
  35.9 5.4 %copy-start.13 = (bf16[2,8,8,8,128]{4,1,3,2,0:T(8,128)(2,1)}, bf16[2,8,8,8,128]{4,1,3,2,0:T(8,128)(2,1)S(1)}, u32[]{:S(2)}) copy-start(bf16[2,8,8,8,128]{4,1,3,2,0:T(8,128)(2,1)S(1)} %get-tuple-element.73) | copy-start | bytes 786436
  35.9 5.6 %copy-start.11 = (bf16[2,8,8,8,128]{4,1,3,2,0:T(8,128)(2,1)}, bf16[2,8,8,8,128]{4,1,3,2,0:T(8,128)(2,1)S(1)}, u32[]{:S(2)}) copy-start(bf16[2,8,8,8,128]{4,1,3,2,0:T(8,128)(2,1)S(1)} %get-tuple-element.72) | copy-start | bytes 786436
  35.9 5.8 %copy-start.9 = (bf16[2,8,8,8,128]{4,1,3,2,0:T(8,128)(2,1)}, bf16[2,8,8,8,128]{4,1,3,2,0:T(8,128)(2,1)S(1)}, u32[]{:S(2)}) copy-start(bf16[2,8,8,8,128]{4,1,3,2,0:T(8,128)(2,1)S(1)} %get-tuple-element.71) | copy-start | bytes 786436
  35.9 6.0 %copy-start.7 = (bf16[2,8,8,8,128]{4,1,3,2,0:T(8,128)(2,1)}, bf16[2,8,8,8,128]{4,1,3,2,0:T(8,128)(2,1)S(1)}, u32[]{:S(2)}) copy-start(bf16[2,8,8,8,128]{4,1,3,2,0:T(8,128)(2,1)S(1)} %get-tuple-element.70) | copy-start | bytes 786436
  35.9 6.3 %copy-start.56 = (bf16[2,8,8,8,128]{4,1,3,2,0:T(8,128)(2,1)}, bf16[2,8,8,8,128]{4,1,3,2,0:T(8,128)(2,1)S(1)}, u32[]{:S(2)}) copy-start(bf16[2,8,8,8,128]{4,1,3,2,0:T(8,128)(2,1)S(1)} %get-tuple-element.69) | copy-start | bytes 786436
  106.7 2.9 %copy-start = (f32[10,18,34,128]{3,2,1,0:T(8,128)S(1)}, f32[10,18,34,128]{3,2,1,0:T(8,128)}, u32[]{:S(2)}) copy-start(f32[10,18,34,128]{3,2,1,0:T(8,128)} %dynamic_update_slice.7) | copy-start | bytes 9400324
  135.3 8.1 %copy-start.55 = (f32[2,8,8,8,128]{4,3,2,1,0:T(8,128)S(1)}, f32[2,8,8,8,128]{4,3,2,1,0:T(8,128)}, u32[]{:S(2)}) copy-start(f32[2,8,8,8,128]{4,3,2,1,0:T(8,128)} %get-tuple-element.117) | copy-start | bytes 1572868
  135.4 16.0 %collective-permute-start.8 = (f32[1792,128]{1,0:T(8,128)S(1)}, f32[1792,128]{1,0:T(8,128)S(1)}, u32[]{:S(2)}, u32[]{:S(2)}) collective-permute-start(f32[1792,128]{1,0:T(8,128)S(1)} %dynamic-slice_bitcast_fusion), channel_id=1, source_target_pairs={{0,1},{1,0},{2,3},{3,2},{4,5},{5,4},{6,7},{7,6},{8,9},{9,8},{10,11... | collective-permute-start | bytes 2752520 | tf_op jit(solution)/shard_map/ppermute | solution.py:54
  138.4 7.0 %collective-permute-start.4 = (bf16[1,18,32,128]{3,2,1,0:T(8,128)(2,1)S(1)}, bf16[1,18,32,128]{3,2,1,0:T(8,128)(2,1)S(1)}, u32[]{:S(2)}, u32[]{:S(2)}) collective-permute-start(bf16[1,18,32,128]{3,2,1,0:T(8,128)(2,1)S(1)} %get-tuple-element.58), channel_id=1, source_target_pairs={{0,4},{4,8},{8,12},{12,16},{16,20},{20,24},{24,28},{1,5},{5,9},{9,... | collective-permute-start | bytes 442376 | tf_op jit(solution)/shard_map/ppermute | solution.py:19
  142.1 8.8 %collective-permute-start.5 = (bf16[1,18,32,128]{3,2,1,0:T(8,128)(2,1)S(1)}, bf16[1,18,32,128]{3,2,1,0:T(8,128)(2,1)S(1)}, u32[]{:S(2)}, u32[]{:S(2)}) collective-permute-start(bf16[1,18,32,128]{3,2,1,0:T(8,128)(2,1)S(1)} %get-tuple-element.59), channel_id=1, source_target_pairs={{4,0},{8,4},{12,8},{16,12},{20,16},{24,20},{28,24},{5,1},{9,5},{13... | collective-permute-start | bytes 442376 | tf_op jit(solution)/shard_map/ppermute | solution.py:22
  151.5 7.3 %collective-permute-start.10 = (bf16[448,128]{1,0:T(8,128)(2,1)S(1)}, bf16[448,128]{1,0:T(8,128)(2,1)S(1)}, u32[]{:S(2)}, u32[]{:S(2)}) collective-permute-start(bf16[448,128]{1,0:T(8,128)(2,1)S(1)} %get-tuple-element.68), channel_id=1, source_target_pairs={{0,4},{1,5},{2,6},{3,7},{4,0},{5,1},{6,2},{7,3},{8,12},{9,13},{10,... | collective-permute-start | bytes 344072 | tf_op jit(solution)/shard_map/ppermute | solution.py:54
  154.2 6.0 %collective-permute-start.11 = (bf16[448,128]{1,0:T(8,128)(2,1)S(1)}, bf16[448,128]{1,0:T(8,128)(2,1)S(1)}, u32[]{:S(2)}, u32[]{:S(2)}) collective-permute-start(bf16[448,128]{1,0:T(8,128)(2,1)S(1)} %get-tuple-element.67), channel_id=1, source_target_pairs={{0,6},{1,7},{2,4},{3,5},{4,2},{5,3},{6,0},{7,1},{8,14},{9,15},{10,... | collective-permute-start | bytes 344072 | tf_op jit(solution)/shard_map/ppermute | solution.py:54
  155.0 5.4 %collective-permute-start.9 = (bf16[448,128]{1,0:T(8,128)(2,1)S(1)}, bf16[448,128]{1,0:T(8,128)(2,1)S(1)}, u32[]{:S(2)}, u32[]{:S(2)}) collective-permute-start(bf16[448,128]{1,0:T(8,128)(2,1)S(1)} %get-tuple-element.66), channel_id=1, source_target_pairs={{0,2},{1,3},{2,0},{3,1},{4,6},{5,7},{6,4},{7,5},{8,10},{9,11},{10,... | collective-permute-start | bytes 344072 | tf_op jit(solution)/shard_map/ppermute | solution.py:54
  156.0 9.7 %collective-permute-start.6 = (bf16[8,1,32,128]{3,2,1,0:T(8,128)(2,1)S(1)}, bf16[8,1,32,128]{3,2,1,0:T(8,128)(2,1)S(1)}, u32[]{:S(2)}, u32[]{:S(2)}) collective-permute-start(bf16[8,1,32,128]{3,2,1,0:T(8,128)(2,1)S(1)} %get-tuple-element.62), channel_id=1, source_target_pairs={{0,1},{1,2},{2,3},{4,5},{5,6},{6,7},{8,9},{9,10},{10,11},{12,13},{... | collective-permute-start | bytes 196616 | tf_op jit(solution)/shard_map/ppermute | solution.py:19
  157.3 8.4 %collective-permute-start.7 = (bf16[8,1,32,128]{3,2,1,0:T(8,128)(2,1)S(1)}, bf16[8,1,32,128]{3,2,1,0:T(8,128)(2,1)S(1)}, u32[]{:S(2)}, u32[]{:S(2)}) collective-permute-start(bf16[8,1,32,128]{3,2,1,0:T(8,128)(2,1)S(1)} %get-tuple-element.63), channel_id=1, source_target_pairs={{1,0},{2,1},{3,2},{5,4},{6,5},{7,6},{9,8},{10,9},{11,10},{13,12},{... | collective-permute-start | bytes 196616 | tf_op jit(solution)/shard_map/ppermute | solution.py:22
  160.4 5.3 %collective-permute-start.12 = (bf16[112,128]{1,0:T(8,128)(2,1)S(1)}, bf16[112,128]{1,0:T(8,128)(2,1)S(1)}, u32[]{:S(2)}, u32[]{:S(2)}) collective-permute-start(bf16[112,128]{1,0:T(8,128)(2,1)S(1)} %get-tuple-element.96), channel_id=1, source_target_pairs={{0,8},{1,9},{2,10},{3,11},{4,12},{5,13},{6,14},{7,15},{8,0},{9,1},... | collective-permute-start | bytes 86024 | tf_op jit(solution)/shard_map/ppermute | solution.py:54
  163.2 5.2 %collective-permute-start.13 = (bf16[112,128]{1,0:T(8,128)(2,1)S(1)}, bf16[112,128]{1,0:T(8,128)(2,1)S(1)}, u32[]{:S(2)}, u32[]{:S(2)}) collective-permute-start(bf16[112,128]{1,0:T(8,128)(2,1)S(1)} %get-tuple-element.98), channel_id=1, source_target_pairs={{0,16},{1,17},{2,18},{3,19},{4,20},{5,21},{6,22},{7,23},{8,24},{9,... | collective-permute-start | bytes 86024 | tf_op jit(solution)/shard_map/ppermute | solution.py:54
  165.0 5.7 %collective-permute-start.14 = (bf16[112,128]{1,0:T(8,128)(2,1)S(1)}, bf16[112,128]{1,0:T(8,128)(2,1)S(1)}, u32[]{:S(2)}, u32[]{:S(2)}) collective-permute-start(bf16[112,128]{1,0:T(8,128)(2,1)S(1)} %get-tuple-element.97), channel_id=1, source_target_pairs={{0,24},{1,25},{2,26},{3,27},{4,28},{5,29},{6,30},{7,31},{8,16},{9,... | collective-permute-start | bytes 86024 | tf_op jit(solution)/shard_map/ppermute | solution.py:54
  170.7 4.5 %collective-permute-start.15 = (bf16[112,128]{1,0:T(8,128)(2,1)S(1)}, bf16[112,128]{1,0:T(8,128)(2,1)S(1)}, u32[]{:S(2)}, u32[]{:S(2)}) collective-permute-start(bf16[112,128]{1,0:T(8,128)(2,1)S(1)} %get-tuple-element.52), channel_id=1, source_target_pairs={{0,8},{1,9},{2,10},{3,11},{4,12},{5,13},{6,14},{7,15},{8,0},{9,1},... | collective-permute-start | bytes 86024 | tf_op jit(solution)/shard_map/ppermute | solution.py:54
  170.8 5.0 %collective-permute-start.16 = (bf16[112,128]{1,0:T(8,128)(2,1)S(1)}, bf16[112,128]{1,0:T(8,128)(2,1)S(1)}, u32[]{:S(2)}, u32[]{:S(2)}) collective-permute-start(bf16[112,128]{1,0:T(8,128)(2,1)S(1)} %get-tuple-element.52), channel_id=1, source_target_pairs={{0,16},{1,17},{2,18},{3,19},{4,20},{5,21},{6,22},{7,23},{8,24},{9,... | collective-permute-start | bytes 86024 | tf_op jit(solution)/shard_map/ppermute | solution.py:54
  172.3 5.7 %collective-permute-start.17 = (bf16[112,128]{1,0:T(8,128)(2,1)S(1)}, bf16[112,128]{1,0:T(8,128)(2,1)S(1)}, u32[]{:S(2)}, u32[]{:S(2)}) collective-permute-start(bf16[112,128]{1,0:T(8,128)(2,1)S(1)} %get-tuple-element.52), channel_id=1, source_target_pairs={{0,24},{1,25},{2,26},{3,27},{4,28},{5,29},{6,30},{7,31},{8,16},{9,... | collective-permute-start | bytes 86024 | tf_op jit(solution)/shard_map/ppermute | solution.py:54
  178.0 5.4 %collective-permute-start.18 = (bf16[448,128]{1,0:T(8,128)(2,1)S(1)}, bf16[448,128]{1,0:T(8,128)(2,1)S(1)}, u32[]{:S(2)}, u32[]{:S(2)}) collective-permute-start(bf16[448,128]{1,0:T(8,128)(2,1)S(1)} %pad_maximum_fusion.6), channel_id=1, source_target_pairs={{0,2},{1,3},{2,0},{3,1},{4,6},{5,7},{6,4},{7,5},{8,10},{9,11},{10,... | collective-permute-start | bytes 344072 | tf_op jit(solution)/shard_map/ppermute | solution.py:54
  180.6 4.8 %collective-permute-start.19 = (bf16[448,128]{1,0:T(8,128)(2,1)S(1)}, bf16[448,128]{1,0:T(8,128)(2,1)S(1)}, u32[]{:S(2)}, u32[]{:S(2)}) collective-permute-start(bf16[448,128]{1,0:T(8,128)(2,1)S(1)} %pad_maximum_fusion.6), channel_id=1, source_target_pairs={{0,4},{1,5},{2,6},{3,7},{4,0},{5,1},{6,2},{7,3},{8,12},{9,13},{10,... | collective-permute-start | bytes 344072 | tf_op jit(solution)/shard_map/ppermute | solution.py:54
  182.0 5.7 %collective-permute-start.20 = (bf16[448,128]{1,0:T(8,128)(2,1)S(1)}, bf16[448,128]{1,0:T(8,128)(2,1)S(1)}, u32[]{:S(2)}, u32[]{:S(2)}) collective-permute-start(bf16[448,128]{1,0:T(8,128)(2,1)S(1)} %pad_maximum_fusion.6), channel_id=1, source_target_pairs={{0,6},{1,7},{2,4},{3,5},{4,2},{5,3},{6,0},{7,1},{8,14},{9,15},{10,... | collective-permute-start | bytes 344072 | tf_op jit(solution)/shard_map/ppermute | solution.py:54
  187.8 3.3 %collective-permute-start.21 = (bf16[1792,128]{1,0:T(8,128)(2,1)S(1)}, bf16[1792,128]{1,0:T(8,128)(2,1)S(1)}, u32[]{:S(2)}, u32[]{:S(2)}) collective-permute-start(bf16[1792,128]{1,0:T(8,128)(2,1)S(1)} %get-tuple-element.99), channel_id=1, source_target_pairs={{0,1},{1,0},{2,3},{3,2},{4,5},{5,4},{6,7},{7,6},{8,9},{9,8},{10,11... | collective-permute-start | bytes 1376264 | tf_op jit(solution)/shard_map/ppermute | solution.py:54
  (37 other events, 43.5 us)

commit v2 on v1

v2 whole, which is shorter than its diff:
```python
import functools

import jax
import jax.numpy as jnp
from jax import lax
from jax.experimental import pallas as pl
from jax.experimental.pallas import tpu as pltpu
from jax.sharding import PartitionSpec as P

C = 128
VOX = 512
BY = 2
BX = 4
NB = 2
SITES = 8
TAPS = 27
HALF = 14

AXES = ("gz", "gy")
F32 = jnp.float32
BF16 = jnp.bfloat16

VZ, VY, VX = 12, 20, 48


def exchange_plan():
    gz_bits = [("gz", b) for b in range(lax.axis_size("gz").bit_length() - 1)]
    gy_bits = [("gy", b) for b in range(lax.axis_size("gy").bit_length() - 1)]
    groups, gy_bits = [(gy_bits[0],)], gy_bits[1:]
    while gy_bits and gz_bits:
        groups.append((gy_bits.pop(0), gz_bits.pop(0)))
    rest = gy_bits + gz_bits
    while rest:
        groups.append(tuple(rest[:2]))
        rest = rest[2:]
    return groups


def swap_with(value, group, pattern):
    nz, ny = lax.axis_size("gz"), lax.axis_size("gy")
    flip = {"gz": 0, "gy": 0}
    for k, (axis, bit) in enumerate(group):
        if pattern >> k & 1:
            flip[axis] |= 1 << bit
    pairs = [
        (z * ny + y, (z ^ flip["gz"]) * ny + (y ^ flip["gy"]))
        for z in range(nz)
        for y in range(ny)
    ]
    return lax.ppermute(value, AXES, pairs)


def place_in(group):
    place = jnp.zeros((), jnp.int32)
    for k, (axis, bit) in enumerate(group):
        place = place | (((lax.axis_index(axis) >> bit) & 1) << k)
    return place


def scatter_sum(total, plan):
    for group in plan:
        count = 1 << len(group)
        me = place_in(group)
        parts = total.reshape(count, -1, C)
        arrived = [
            swap_with(lax.dynamic_index_in_dim(parts, me ^ p, 0, False).astype(BF16), group, p)
            for p in range(1, count)
        ]
        total = lax.dynamic_index_in_dim(parts, me, 0, False)
        for piece in arrived:
            total = total + piece.astype(F32)
    return total


def gather_parts(piece, plan):
    for group in reversed(plan):
        pieces = [piece] + [swap_with(piece, group, p) for p in range(1, 1 << len(group))]
        piece = jnp.concatenate(pieces)
    bits = [b for group in plan for b in reversed(group)]
    piece = piece.reshape((2,) * len(bits) + (-1, C))
    for dim, (axis, bit) in enumerate(bits):
        odd = (lax.axis_index(axis) >> bit) & 1
        piece = jnp.where(odd == 1, jnp.flip(piece, dim), piece)
    return piece.reshape(-1, C)


def neighbours(up, down, axis):
    count = lax.axis_size(axis)
    forward = [(i, i + 1) for i in range(count - 1)]
    backward = [(b, a) for a, b in forward]
    return lax.ppermute(up, axis, forward), lax.ppermute(down, axis, backward)


Z_ROWS = NB * 24
Y_ROWS = NB * 24 + 2 * NB * 5


def pack_z_kernel(x_ref, g_ref, up_ref, down_ref):
    for s in range(NB):
        base = 24 * s
        up_ref[base : base + 16] = x_ref[s, 48:64]
        up_ref[base + 16 : base + 24] = g_ref[s, 56:64]
        down_ref[base : base + 16] = x_ref[s, 0:16]
        down_ref[base + 16 : base + 24] = g_ref[s, 0:8]


def pack_z(x, g):
    shape = jax.ShapeDtypeStruct((Z_ROWS, 8, C), BF16)
    return pl.pallas_call(pack_z_kernel, out_shape=(shape, shape), name="pack_z")(x, g)


def pack_y_kernel(x_ref, g_ref, low_ref, high_ref, up_ref, down_ref):
    for s in range(NB):
        base = 24 * s
        for z in range(8):
            up_ref[base + 2 * z : base + 2 * z + 2] = x_ref[s, 8 * z + 6 : 8 * z + 8]
            up_ref[base + 16 + z] = g_ref[s, 8 * z + 7]
            down_ref[base + 2 * z : base + 2 * z + 2] = x_ref[s, 8 * z : 8 * z + 2]
            down_ref[base + 16 + z] = g_ref[s, 8 * z]
    for side, ref in enumerate((low_ref, high_ref)):
        for s in range(NB):
            base = NB * 24 + 10 * side + 5 * s
            src = 24 * s
            for z in range(2):
                up_ref[base + 2 * z : base + 2 * z + 2] = ref[src + 8 * z + 6 : src + 8 * z + 8]
                down_ref[base + 2 * z : base + 2 * z + 2] = ref[src + 8 * z : src + 8 * z + 2]
            up_ref[base + 4] = ref[src + 16 + 7]
            down_ref[base + 4] = ref[src + 16]


def pack_y(x, g, low, high):
    shape = jax.ShapeDtypeStruct((Y_ROWS, 8, C), BF16)
    return pl.pallas_call(pack_y_kernel, out_shape=(shape, shape), name="pack_y")(x, g, low, high)


def clear(ref):
    rows = ref.shape[0]
    flat = jnp.zeros((1,) + ref.shape[1:], ref.dtype)
    for z in range(rows):
        ref[z : z + 1] = flat


def place_of(site):
    inside = jnp.minimum(site, SITES - 1)
    return inside // BX, pl.multiple_of(inside % BX * 8 + 8, 8)


def fill(vol, codes, x_ref, zl_ref, zh_ref, yl_ref, yh_ref):
    def put(z0, y0, x0, rows):
        vol[z0 : z0 + rows.shape[0], pl.ds(y0, rows.shape[1]), pl.ds(x0, 8)] = rows.astype(F32)

    for s in range(NB):
        site = codes[0, s]
        py, px = place_of(site)

        @pl.when(site < SITES)
        def _():
            put(2, 2 + 8 * py, px, x_ref[s].reshape(8, 8, 8, C))

        for side, ref in ((1, zl_ref), (2, zh_ref)):
            zsite = codes[side, s]
            zpy, zpx = place_of(zsite)

            @pl.when(zsite < SITES)
            def _(ref=ref, side=side, zpy=zpy, zpx=zpx, s=s):
                put(0 if side == 1 else 10, 2 + 8 * zpy, zpx, ref[24 * s : 24 * s + 16].reshape(2, 8, 8, C))

        for first, ref, row, y0 in ((3, yl_ref, 1, 0), (6, yh_ref, 0, 18)):
            for k, (z0, base, depth) in enumerate(
                ((2, 24 * s, 8), (0, 48 + 5 * s, 2), (10, 58 + 5 * s, 2))
            ):
                ysite = codes[first + k, s]
                ypy, ypx = place_of(ysite)

                @pl.when((ysite < SITES) & (ypy == row))
                def _(ref=ref, z0=z0, y0=y0, base=base, depth=depth, ypx=ypx):
                    put(z0, y0, ypx, ref[base : base + 2 * depth].reshape(depth, 2, 8, C))


def stack_x(vol, dst, dst_at, z0, y0s, x0s, nz, ny):
    for z in range(nz):
        for y in range(ny):
            halves = []
            for y0, x0 in zip(y0s, x0s):
                row = vol[z0 + z, y0 + y, pl.ds(x0 - 8, 24)]
                halves.append(
                    jnp.concatenate([row[7:15], row[8:16], row[9:17]], axis=1)
                )
            dst[dst_at + z * ny + y] = jnp.concatenate(halves, axis=0).astype(BF16)


def views(stack, base, ny_all, nz, ny):
    result = []
    for dz in range(3):
        for dy in range(3):
            planes = [
                stack[base + (z + dz) * ny_all + dy : base + (z + dz) * ny_all + dy + ny]
                for z in range(nz)
            ]
            result.append(jnp.concatenate(planes, axis=0).reshape(nz * ny * 16, 3 * C))
    return result


def dot(a, b, dims=((1,), (0,))):
    return lax.dot_general(a, b, (dims, ((), ())), preferred_element_type=F32)


def convolve(stack, base, ny_all, nz, ny, weight):
    total = None
    for k, view in enumerate(views(stack, base, ny_all, nz, ny)):
        term = weight(k, view)
        total = term if total is None else total + term
    return total


def forward_kernel(codes, core, x_ref, g_ref, zl_ref, zh_ref, yl_ref, yh_ref, w_ref,
                   act_ref, dpre_ref, keep_ref, send_ref, vol, stack, turned):
    clear(vol)
    fill(vol, codes, x_ref, zl_ref, zh_ref, yl_ref, yh_ref)
    places = [place_of(codes[0, s]) for s in range(NB)]
    stack_x(vol, stack, 0, 1, [1 + 8 * py for py, _ in places], [px for _, px in places], 10, 10)

    def weight(k, view):
        return dot(view, w_ref[3 * k : 3 * k + 3].reshape(3 * C, C))

    used = [codes[0, s] < SITES for s in range(NB)]
    for half in range(2):
        pre = convolve(stack, 40 * half, 10, 4, 8, weight)
        sig = 1.0 / (1.0 + jnp.exp(-pre))
        act = (pre * sig).reshape(32, 16, C)
        slope = (sig * (1.0 + pre * (1.0 - sig))).reshape(32, 16, C)
        both = []
        for s in range(NB):
            rows = slice(32 * half, 32 * half + 32)
            a = jnp.where(used[s], act[:, 8 * s : 8 * s + 8], 0.0)
            act_ref[s, rows] = a.astype(BF16)
            d = g_ref[s, rows].astype(F32) * slope[:, 8 * s : 8 * s + 8]
            both.append(jnp.where(used[s], d, 0.0))
        d = jnp.concatenate(both, axis=1).astype(BF16)
        dpre_ref[32 * half : 32 * half + 32] = d
        turned[:, 512 * half : 512 * half + 512] = d.reshape(512, C).T

    dt = turned[...]
    for k in range(9):
        dz, dy = divmod(k, 3)
        planes = [stack[(z + dz) * 10 + dy : (z + dz) * 10 + dy + 8] for z in range(8)]
        view = jnp.concatenate(planes, axis=0).reshape(1024, 3 * C)
        term = dot(dt, view)
        for dx in range(3):
            t = 3 * k + dx
            value = term[:, C * dx : C * dx + C].T
            half, at = divmod(t, HALF)

            @pl.when(core[0] == half)
            def _(value=value, at=at):
                keep_ref[at] = value

            @pl.when(core[0] != half)
            def _(value=value, at=at):
                send_ref[at] = value.astype(BF16)
    for t in range(TAPS, 2 * HALF):
        half, at = divmod(t, HALF)

        @pl.when(core[0] == half)
        def _(at=at):
            keep_ref[at] = jnp.zeros((C, C), F32)

        @pl.when(core[0] != half)
        def _(at=at):
            send_ref[at] = jnp.zeros((C, C), BF16)


SMEM = pl.BlockSpec(memory_space=pltpu.SMEM)
VMEM = pl.BlockSpec(memory_space=pltpu.VMEM)


def forward(codes, core, x, g, zl, zh, yl, yh, w):
    rows = jax.ShapeDtypeStruct((NB, 64, 8, C), BF16)
    return pl.pallas_call(
        forward_kernel,
        out_shape=(
            rows,
            jax.ShapeDtypeStruct((64, 16, C), BF16),
            jax.ShapeDtypeStruct((HALF, C, C), F32),
            jax.ShapeDtypeStruct((HALF, C, C), BF16),
        ),
        in_specs=[SMEM, SMEM] + [VMEM] * 7,
        out_specs=(VMEM,) * 4,
        scratch_shapes=[
            pltpu.VMEM((VZ, VY, VX, C), F32),
            pltpu.VMEM((100, 16, 3 * C), BF16),
            pltpu.VMEM((C, 1024), BF16),
        ],
        compiler_params=pltpu.CompilerParams(vmem_limit_bytes=40 << 20),
        cost_estimate=pl.CostEstimate(flops=2 * 10**9, bytes_accessed=5 << 20, transcendentals=1 << 17),
        name="forward",
    )(codes, core, x, g, zl, zh, yl, yh, w)


def backward_kernel(codes, x_ref, dpre_ref, zl_ref, zh_ref, yl_ref, yh_ref, w_ref,
                    grad_ref, vol, stack):
    clear(vol)
    fill(vol, codes, x_ref, zl_ref, zh_ref, yl_ref, yh_ref)

    def weight(k, view):
        return dot(view, w_ref[3 * k : 3 * k + 3].reshape(3 * C, C))

    jobs = []
    for block, z in ((1, 1), (2, 10)):
        jobs.append((block, z, None, 1, 8))
    for first, y in ((3, 1), (6, 18)):
        jobs.append((first, 2, y, 8, 1))
        jobs.append((first + 1, 1, y, 1, 1))
        jobs.append((first + 2, 10, y, 1, 1))
    base = 0
    found = []
    for block, z0, y0, nz, ny in jobs:
        places = [place_of(codes[block, s]) for s in range(NB)]
        y0s = [2 + 8 * py if y0 is None else y0 for py, _ in places]
        x0s = [px for _, px in places]
        stack_x(vol, stack, base, z0 - 1, [y - 1 for y in y0s], x0s, nz + 2, ny + 2)
        pre = convolve(stack, base, ny + 2, nz, ny, weight)
        sig = 1.0 / (1.0 + jnp.exp(-pre))
        slope = (sig * (1.0 + pre * (1.0 - sig))).reshape(nz, ny, 16, C)
        found.append((block, z0, y0, nz, ny, y0s, x0s, slope))
        base += (nz + 2) * (ny + 2)
    values = []
    for block, z0, y0, nz, ny, y0s, x0s, slope in found:
        for s in range(NB):
            if block == 1:
                g = zl_ref[24 * s + 16 : 24 * s + 24]
            elif block == 2:
                g = zh_ref[24 * s + 16 : 24 * s + 24]
            else:
                ref = yl_ref if block < 6 else yh_ref
                kind = (block - 3) % 3
                if kind == 0:
                    g = ref[24 * s + 16 : 24 * s + 24]
                else:
                    at = 48 + 10 * (kind - 1) + 5 * s + 4
                    g = ref[at : at + 1]
            g = g.astype(F32).reshape(nz, ny, 8, C)
            value = (g * slope[:, :, 8 * s : 8 * s + 8]).astype(BF16).astype(F32)
            values.append(value)

    clear(vol)
    for s in range(NB):
        site = codes[0, s]
        py, px = place_of(site)

        @pl.when(site < SITES)
        def _(s=s, py=py, px=px):
            own = dpre_ref[...].astype(F32).reshape(8, 8, 16, C)[:, :, 8 * s : 8 * s + 8]
            vol[2:10, pl.ds(2 + 8 * py, 8), pl.ds(px, 8)] = own

    at = 0
    for block, z0, y0, nz, ny, y0s, x0s, slope in found:
        for s in range(NB):
            site = codes[block, s]
            py, px = place_of(site)
            ok = site < SITES
            if block >= 3:
                ok = ok & (py == (1 if block < 6 else 0))
            value = values[at]
            at += 1

            @pl.when(ok)
            def _(value=value, z0=z0, nz=nz, ny=ny, y0=y0s[s], x0=x0s[s]):
                vol[z0 : z0 + nz, pl.ds(y0, ny), pl.ds(x0, 8)] = value

    places = [place_of(codes[0, s]) for s in range(NB)]
    stack_x(vol, stack, 0, 1, [1 + 8 * py for py, _ in places], [px for _, px in places], 10, 10)

    def back(k, view):
        turned = [w_ref[26 - 3 * k - dx] for dx in range(3)]
        return dot(view, jnp.concatenate(turned, axis=1), ((1,), (1,)))

    for half in range(2):
        grad = convolve(stack, 40 * half, 10, 4, 8, back).reshape(32, 16, C)
        for s in range(NB):
            value = jnp.where(codes[0, s] < SITES, grad[:, 8 * s : 8 * s + 8], 0.0)
            grad_ref[s, 32 * half : 32 * half + 32] = value.astype(BF16)


def backward(codes, x, dpre, zl, zh, yl, yh, w):
    return pl.pallas_call(
        backward_kernel,
        out_shape=jax.ShapeDtypeStruct((NB, 64, 8, C), BF16),
        in_specs=[SMEM] + [VMEM] * 7,
        out_specs=VMEM,
        scratch_shapes=[
            pltpu.VMEM((VZ, VY, VX, C), F32),
            pltpu.VMEM((160, 16, 3 * C), BF16),
        ],
        compiler_params=pltpu.CompilerParams(vmem_limit_bytes=40 << 20),
        cost_estimate=pl.CostEstimate(flops=10**9, bytes_accessed=5 << 20, transcendentals=1 << 16),
        name="backward",
    )(codes, x, dpre, zl, zh, yl, yh, w)


def local(features, brick_sites, kernel, cotangent):
    x = features.reshape(NB, 64, 8, C)
    g = cotangent.reshape(NB, 64, 8, C)
    sites = brick_sites.reshape(NB)
    devices = lax.axis_size("gz") * lax.axis_size("gy")
    up, down = pack_z(x, g)
    zl, zh = neighbours(up, down, "gz")
    own_code = SITES - sites
    code_l, code_h = neighbours(own_code, own_code, "gz")
    trio = jnp.stack([own_code, code_l, code_h])
    up, down = pack_y(x, g, zl, zh)
    yl, yh = neighbours(up, down, "gy")
    trio_l, trio_h = neighbours(trio, trio, "gy")
    codes = SITES - jnp.concatenate([trio, trio_l, trio_h])
    core = (lax.axis_index("gy") & 1).reshape(1).astype(jnp.int32)
    act, dpre, keep, send = forward(codes, core, x, g, zl, zh, yl, yh, kernel)
    grad_in = backward(codes, x, dpre, zl, zh, yl, yh, kernel)

    plan = exchange_plan()
    rows = TAPS * C
    share = 16 * devices
    padded_rows = -(-(2 * HALF * C) // share) * share
    arrived = swap_with(send, plan[0], 1)
    total = (keep + arrived.astype(F32)).reshape(HALF * C, C)
    total = jnp.pad(total, ((0, padded_rows // 2 - HALF * C), (0, 0)))
    scale = 1.0 / (NB * VOX * devices) ** 0.5
    mine = (scatter_sum(total, plan[1:]) * scale).astype(BF16)
    halves = gather_parts(mine, plan).reshape(2, padded_rows // 2, C)
    grad_kernel = halves[:, : HALF * C].reshape(-1, C)[:rows].reshape(TAPS, C, C).astype(F32)
    shape = (1, 1, NB, VOX, C)
    return act.reshape(shape), grad_in.reshape(shape), grad_kernel


def solution(mesh):
    placed = (
        P("gz", "gy", None, None, None),
        P("gz", "gy", None),
        P(),
        P("gz", "gy", None, None, None),
    )
    return jax.shard_map(
        local,
        mesh=mesh,
        in_specs=placed,
        out_specs=(P("gz", "gy", None, None, None), P("gz", "gy", None, None, None), P()),
        check_vma=False,
    )
```

time: 195 us -> 96.9 us (0.50)
  matrix products: 62.1 us -> 0 us
  local copies, waits for them, and re-layouts: 46.2 us -> 10.3 us
  Pallas kernels: 0 us -> 19.6 us
  between operations: 9.84 us -> 0.94 us
  other arithmetic: 12.5 us -> 3.79 us
  waiting for transfers between devices: 25.3 us -> 21.1 us
  starting transfers between devices: 37.6 us -> 40.6 us
    dot_general x81 -> x0, matrix products: 62.1 us -> none  [the longest x27 47.2 us: local(): jnp.einsum('nzyxd,cd->nzyxc', view, kernel[t], preferred_element_type=jnp...]
    pallas_call x0 -> x4, Pallas kernels: none -> 19.6 us  [the longest x1 9.33 us: forward(): pl.pallas_call(forward_kernel, out_shape=(rows, jax.ShapeDtypeStruct((64,...]
    dynamic_update_slice x2 -> x0, local copies, waits for them, and re-layouts: 11.1 us -> none  [local(): canvas = lax.dynamic_update_slice(canvas, piece + spread[slot], start)]
    unnamed x132 -> x28, local copies, waits for them, and re-layouts: 20.2 us -> 9.3 us
    slice x15 -> x1, local copies, waits for them, and re-layouts: 6.25 us -> 0.06 us  [local(): halves[:, :HALF * C].reshape(-1, C)[:rows].reshape(TAPS, C, C).astype(F32)]
    concatenate x3 -> x0, other arithmetic: 5.48 us -> none  [the longest x1 3.69 us: padded(): block = jnp.concatenate([low, block, high], axis=dim)]
    ppermute x8, waiting for transfers between devices: 10.5 us -> 5.63 us  [neighbours(): return (lax.ppermute(up, axis, forward), lax.ppermute(down, axis, backward))]
    ppermute x8, starting transfers between devices: 16.6 us -> 20.1 us  [neighbours(): return (lax.ppermute(up, axis, forward), lax.ppermute(down, axis, backward))]
  transfers between devices with their start and end apart: 22 -> 22, of which waited for: 12 -> 11; matrix products, arithmetic and copies ran while one was open for 5% -> 3% of each run, Pallas kernels for 0% -> 9%
where the time goes in v2:
time: 96.9 us; the launch traced here: 96.3 us
  starting transfers between devices  40.6 us (42%)
  waiting for transfers between devices  21.1 us (22%)
  Pallas kernels  19.6 us (20%)
  local copies, waits for them, and re-layouts  10.3 us (11%)
  other arithmetic  3.79 us (4%)
    ppermute x14, starting transfers between devices, swap_with(): return lax.ppermute(value, AXES, pairs)  20.5 us
    ppermute x8, starting transfers between devices, neighbours(): return (lax.ppermute(up, axis, forward), lax.ppermute(down, axis, backward))  20.1 us
    ppermute x14, waiting for transfers between devices, swap_with(): return lax.ppermute(value, AXES, pairs)  15.5 us
    pallas_call x1, Pallas kernels, forward(): pl.pallas_call(forward_kernel, out_shape=(rows, jax.ShapeDtypeStruct((64,...  9.33 us
    unnamed x28, local copies, waits for them, and re-layouts  9.3 us
    pallas_call x1, Pallas kernels, backward(): pl.pallas_call(backward_kernel, out_shape=jax.ShapeDtypeStruct((NB, 64, 8...  6.75 us
    ppermute x8, waiting for transfers between devices, neighbours(): return (lax.ppermute(up, axis, forward), lax.ppermute(down, axis, backward))  5.63 us
  transfers between devices with their start and end apart: 22, of which 11 were waited for; matrix products, arithmetic and copies ran while one was open for 3% of the time, Pallas kernels for 9%

profile of v2, /device:TPU:0, one launch (start us, length us, event | category | flops | bytes accessed | tf_op | source)
XLA Modules:
  0.0 96.3 jit_solution(10335522612428443840)
XLA Ops:
  0.6 0.7 subtract_bitcast_fusion
  1.3 4.9 %collective-permute-start = (s32[2]{0:T(128)S(1)}, s32[2]{0:T(128)S(1)}, u32[]{:S(2)}, u32[]{:S(2)}) collective-permute-start(s32[2]{0:T(128)S(1)} %get-tuple-element.39), channel_id=1, source_target_pairs={{0,4},{4,8},{8,12},{12,16},{16,20},{20,24},{24,28},{1,5},{5,9},{9,... | collective-permute-start | bytes 32 | tf_op jit(solution)/shard_map/ppermute | solution.py:91
  6.2 1.3 %collective-permute-start.1 = (s32[2]{0:T(128)S(1)}, s32[2]{0:T(128)S(1)}, u32[]{:S(2)}, u32[]{:S(2)}) collective-permute-start(s32[2]{0:T(128)S(1)} %get-tuple-element.39), channel_id=1, source_target_pairs={{4,0},{8,4},{12,8},{16,12},{20,16},{24,20},{28,24},{5,1},{9,5},{13... | collective-permute-start | bytes 32 | tf_op jit(solution)/shard_map/ppermute | solution.py:91
  7.5 1.7 %pack_z.1 = (bf16[48,8,128]{2,1,0:T(8,128)(2,1)}, bf16[48,8,128]{2,1,0:T(8,128)(2,1)}) custom-call(bf16[2,64,8,128]{3,2,1,0:T(8,128)(2,1)} %bitcast.49, bf16[2,64,8,128]{3,2,1,0:T(8,128)(2,1)} %bitcast.46), custom_call_target="tpu_custom_call" | custom-call | tf_op jit(solution)/shard_map/pack_z/pallas_call | solution.py:109
  9.2 4.5 %collective-permute-start.4 = (bf16[48,8,128]{2,1,0:T(8,128)(2,1)}, bf16[48,8,128]{2,1,0:T(8,128)(2,1)S(1)}, u32[]{:S(2)}, u32[]{:S(2)}) collective-permute-start(bf16[48,8,128]{2,1,0:T(8,128)(2,1)} %get-tuple-element.11), channel_id=1, source_target_pairs={{0,4},{4,8},{8,12},{12,16},{16,20},{20,24},{24,28},{1,5},{5,9},{9,... | collective-permute-start | bytes 294920 | tf_op jit(solution)/shard_map/ppermute | solution.py:91
  13.7 1.3 %collective-permute-start.5 = (bf16[48,8,128]{2,1,0:T(8,128)(2,1)}, bf16[48,8,128]{2,1,0:T(8,128)(2,1)S(1)}, u32[]{:S(2)}, u32[]{:S(2)}) collective-permute-start(bf16[48,8,128]{2,1,0:T(8,128)(2,1)} %get-tuple-element.12), channel_id=1, source_target_pairs={{4,0},{8,4},{12,8},{16,12},{20,16},{24,20},{28,24},{5,1},{9,5},{13... | collective-permute-start | bytes 294920 | tf_op jit(solution)/shard_map/ppermute | solution.py:91
  15.1 1.3 %collective-permute-start.2 = (s32[3,2]{1,0:T(4,128)S(1)}, s32[3,2]{1,0:T(4,128)S(1)}, u32[]{:S(2)}, u32[]{:S(2)}) collective-permute-start(s32[3,2]{1,0:T(4,128)S(1)} %pad_add_fusion), channel_id=1, source_target_pairs={{0,1},{1,2},{2,3},{4,5},{5,6},{6,7},{8,9},{9,10},{10,11},{12,13},{... | collective-permute-start | bytes 80 | tf_op jit(solution)/shard_map/ppermute | solution.py:91
  16.4 1.3 %collective-permute-start.3 = (s32[3,2]{1,0:T(4,128)S(1)}, s32[3,2]{1,0:T(4,128)S(1)}, u32[]{:S(2)}, u32[]{:S(2)}) collective-permute-start(s32[3,2]{1,0:T(4,128)S(1)} %pad_add_fusion), channel_id=1, source_target_pairs={{1,0},{2,1},{3,2},{5,4},{6,5},{7,6},{9,8},{10,9},{11,10},{13,12},{... | collective-permute-start | bytes 80 | tf_op jit(solution)/shard_map/ppermute | solution.py:91
  17.7 3.5 %collective-permute-done.3 = s32[3,2]{1,0:T(4,128)S(1)} collective-permute-done((s32[3,2]{1,0:T(4,128)S(1)}, s32[3,2]{1,0:T(4,128)S(1)}, u32[]{:S(2)}, u32[]{:S(2)}) %collective-permute-start.3) | collective-permute-done | bytes 56 | tf_op jit(solution)/shard_map/ppermute | solution.py:91
  21.3 0.6 copy-done.3
  21.9 0.6 copy-done.6
  22.6 1.8 %pack_y.1 = (bf16[68,8,128]{2,1,0:T(8,128)(2,1)}, bf16[68,8,128]{2,1,0:T(8,128)(2,1)}) custom-call(bf16[2,64,8,128]{3,2,1,0:T(8,128)(2,1)} %bitcast.50, bf16[2,64,8,128]{3,2,1,0:T(8,128)(2,1)} %bitcast.47, bf16[48,8,128]{2,1,0:T(8,128)(2,1)} %copy-done.3, bf16[48,8,128]{2,1,0:T(8,128)(2,1)} %copy-done.6), custom_call_target="tpu_custom_call" | custom-call | tf_op jit(solution)/shard_map/pack_y/pallas_call | solution.py:133
  24.4 4.2 %collective-permute-start.6 = (bf16[68,8,128]{2,1,0:T(8,128)(2,1)}, bf16[68,8,128]{2,1,0:T(8,128)(2,1)S(1)}, u32[]{:S(2)}, u32[]{:S(2)}) collective-permute-start(bf16[68,8,128]{2,1,0:T(8,128)(2,1)} %get-tuple-element.13), channel_id=1, source_target_pairs={{0,1},{1,2},{2,3},{4,5},{5,6},{6,7},{8,9},{9,10},{10,11},{12,13},{... | collective-permute-start | bytes 417800 | tf_op jit(solution)/shard_map/ppermute | solution.py:91
  28.6 1.3 %collective-permute-start.7 = (bf16[68,8,128]{2,1,0:T(8,128)(2,1)}, bf16[68,8,128]{2,1,0:T(8,128)(2,1)S(1)}, u32[]{:S(2)}, u32[]{:S(2)}) collective-permute-start(bf16[68,8,128]{2,1,0:T(8,128)(2,1)} %get-tuple-element.14), channel_id=1, source_target_pairs={{1,0},{2,1},{3,2},{5,4},{6,5},{7,6},{9,8},{10,9},{11,10},{13,12},{... | collective-permute-start | bytes 417800 | tf_op jit(solution)/shard_map/ppermute | solution.py:91
  29.9 2.1 %collective-permute-done.7.yh_ref = bf16[68,8,128]{2,1,0:T(8,128)(2,1)S(1)} collective-permute-done((bf16[68,8,128]{2,1,0:T(8,128)(2,1)}, bf16[68,8,128]{2,1,0:T(8,128)(2,1)S(1)}, u32[]{:S(2)}, u32[]{:S(2)}) %collective-permute-start.7) | collective-permute-done | bytes 139296 | tf_op jit(solution)/shard_map/ppermute | solution.py:91
  32.1 0.9 copy-done
  33.0 0.9 copy-done.1
  34.0 0.9 copy-done.4
  34.9 0.9 copy-done.7
  35.8 1.2 %copy-done.9 = bf16[27,128,128]{2,1,0:T(8,128)(2,1)S(1)} copy-done((bf16[27,128,128]{2,1,0:T(8,128)(2,1)S(1)}, bf16[27,128,128]{2,1,0:T(8,128)(2,1)}, u32[]{:S(2)}) %copy-start.9) | copy-done | bytes 884760
  36.9 9.3 %forward.1 = (bf16[2,64,8,128]{3,2,1,0:T(8,128)(2,1)}, bf16[64,16,128]{2,1,0:T(8,128)(2,1)S(1)}, f32[14,128,128]{2,1,0:T(8,128)S(1)}, bf16[14,128,128]{2,1,0:T(8,128)(2,1)S(1)}) custom-call(s32[9,2]{1,0:T(8,128)S(1)} %broadcast_subtract_fusion.codes, s32[1]{0:T(128)} %bitcast.4.core, bf16[2,64,8,128]{3,2,1,0:T(8,128)(2,1)S(1)} %bitcast.51, ...), custom_call_target="tpu_custom_call" | custom-call | flops 2000000000 | bytes 5242880 | tf_op jit(solution)/shard_map/forward/pallas_call | solution.py:279
  46.3 3.2 %collective-permute-start.8 = (bf16[14,128,128]{2,1,0:T(8,128)(2,1)S(1)}, bf16[14,128,128]{2,1,0:T(8,128)(2,1)S(1)}, u32[]{:S(2)}, u32[]{:S(2)}) collective-permute-start(bf16[14,128,128]{2,1,0:T(8,128)(2,1)S(1)} %get-tuple-element.18), channel_id=1, source_target_pairs={{0,1},{1,0},{2,3},{3,2},{4,5},{5,4},{6,7},{7,6},{8,9},{9,8},{10,11... | collective-permute-start | bytes 1376264 | tf_op jit(solution)/shard_map/ppermute | solution.py:50
  49.5 1.4 %collective-permute-done.8 = bf16[14,128,128]{2,1,0:T(8,128)(2,1)S(1)} collective-permute-done((bf16[14,128,128]{2,1,0:T(8,128)(2,1)S(1)}, bf16[14,128,128]{2,1,0:T(8,128)(2,1)S(1)}, u32[]{:S(2)}, u32[]{:S(2)}) %collective-permute-start.8) | collective-permute-done | bytes 458784 | tf_op jit(solution)/shard_map/ppermute | solution.py:50
  51.1 2.7 %collective-permute-start.11 = (bf16[448,128]{1,0:T(8,128)(2,1)S(1)}, bf16[448,128]{1,0:T(8,128)(2,1)S(1)}, u32[]{:S(2)}, u32[]{:S(2)}) collective-permute-start(bf16[448,128]{1,0:T(8,128)(2,1)S(1)} %get-tuple-element.22), channel_id=1, source_target_pairs={{0,6},{1,7},{2,4},{3,5},{4,2},{5,3},{6,0},{7,1},{8,14},{9,15},{10,... | collective-permute-start | bytes 344072 | tf_op jit(solution)/shard_map/ppermute | solution.py:50
  54.3 1.4 %collective-permute-start.9 = (bf16[448,128]{1,0:T(8,128)(2,1)S(1)}, bf16[448,128]{1,0:T(8,128)(2,1)S(1)}, u32[]{:S(2)}, u32[]{:S(2)}) collective-permute-start(bf16[448,128]{1,0:T(8,128)(2,1)S(1)} %get-tuple-element.21), channel_id=1, source_target_pairs={{0,2},{1,3},{2,0},{3,1},{4,6},{5,7},{6,4},{7,5},{8,10},{9,11},{10,... | collective-permute-start | bytes 344072 | tf_op jit(solution)/shard_map/ppermute | solution.py:50
  55.7 1.9 %collective-permute-done.11 = bf16[448,128]{1,0:T(8,128)(2,1)S(1)} collective-permute-done((bf16[448,128]{1,0:T(8,128)(2,1)S(1)}, bf16[448,128]{1,0:T(8,128)(2,1)S(1)}, u32[]{:S(2)}, u32[]{:S(2)}) %collective-permute-start.11) | collective-permute-done | bytes 114720 | tf_op jit(solution)/shard_map/ppermute | solution.py:50
  57.6 2.4 %collective-permute-done.10 = bf16[448,128]{1,0:T(8,128)(2,1)S(1)} collective-permute-done((bf16[448,128]{1,0:T(8,128)(2,1)S(1)}, bf16[448,128]{1,0:T(8,128)(2,1)S(1)}, u32[]{:S(2)}, u32[]{:S(2)}) %collective-permute-start.10) | collective-permute-done | bytes 114720 | tf_op jit(solution)/shard_map/ppermute | solution.py:50
  60.0 1.6 %collective-permute-done.9 = bf16[448,128]{1,0:T(8,128)(2,1)S(1)} collective-permute-done((bf16[448,128]{1,0:T(8,128)(2,1)S(1)}, bf16[448,128]{1,0:T(8,128)(2,1)S(1)}, u32[]{:S(2)}, u32[]{:S(2)}) %collective-permute-start.9) | collective-permute-done | bytes 114720 | tf_op jit(solution)/shard_map/ppermute | solution.py:50
  61.7 4.1 %collective-permute-start.14 = (bf16[112,128]{1,0:T(8,128)(2,1)S(1)}, bf16[112,128]{1,0:T(8,128)(2,1)S(1)}, u32[]{:S(2)}, u32[]{:S(2)}) collective-permute-start(bf16[112,128]{1,0:T(8,128)(2,1)S(1)} %get-tuple-element.25), channel_id=1, source_target_pairs={{0,24},{1,25},{2,26},{3,27},{4,28},{5,29},{6,30},{7,31},{8,16},{9,... | collective-permute-start | bytes 86024 | tf_op jit(solution)/shard_map/ppermute | solution.py:50
  65.8 0.6 collective-permute-start.12
  66.4 1.3 %collective-permute-done.14 = bf16[112,128]{1,0:T(8,128)(2,1)S(1)} collective-permute-done((bf16[112,128]{1,0:T(8,128)(2,1)S(1)}, bf16[112,128]{1,0:T(8,128)(2,1)S(1)}, u32[]{:S(2)}, u32[]{:S(2)}) %collective-permute-start.14) | collective-permute-done | bytes 28704 | tf_op jit(solution)/shard_map/ppermute | solution.py:50
  67.8 2.8 %collective-permute-done.13 = bf16[112,128]{1,0:T(8,128)(2,1)S(1)} collective-permute-done((bf16[112,128]{1,0:T(8,128)(2,1)S(1)}, bf16[112,128]{1,0:T(8,128)(2,1)S(1)}, u32[]{:S(2)}, u32[]{:S(2)}) %collective-permute-start.13) | collective-permute-done | bytes 28704 | tf_op jit(solution)/shard_map/ppermute | solution.py:50
  70.6 0.6 constant_dynamic-update-slice_fusion.6
  71.2 2.0 %collective-permute-start.16 = (bf16[112,128]{1,0:T(8,128)(2,1)S(1)}, bf16[112,128]{1,0:T(8,128)(2,1)S(1)}, u32[]{:S(2)}, u32[]{:S(2)}) collective-permute-start(bf16[112,128]{1,0:T(8,128)(2,1)S(1)} %get-tuple-element.20), channel_id=1, source_target_pairs={{0,16},{1,17},{2,18},{3,19},{4,20},{5,21},{6,22},{7,23},{8,24},{9,... | collective-permute-start | bytes 86024 | tf_op jit(solution)/shard_map/ppermute | solution.py:50
  73.2 2.4 %collective-permute-start.17 = (bf16[112,128]{1,0:T(8,128)(2,1)S(1)}, bf16[112,128]{1,0:T(8,128)(2,1)S(1)}, u32[]{:S(2)}, u32[]{:S(2)}) collective-permute-start(bf16[112,128]{1,0:T(8,128)(2,1)S(1)} %get-tuple-element.20), channel_id=1, source_target_pairs={{0,24},{1,25},{2,26},{3,27},{4,28},{5,29},{6,30},{7,31},{8,16},{9,... | collective-permute-start | bytes 86024 | tf_op jit(solution)/shard_map/ppermute | solution.py:50
  76.1 2.8 %collective-permute-done.17 = bf16[112,128]{1,0:T(8,128)(2,1)S(1)} collective-permute-done((bf16[112,128]{1,0:T(8,128)(2,1)S(1)}, bf16[112,128]{1,0:T(8,128)(2,1)S(1)}, u32[]{:S(2)}, u32[]{:S(2)}) %collective-permute-start.17) | collective-permute-done | bytes 28704 | tf_op jit(solution)/shard_map/ppermute | solution.py:50
  78.9 0.9 collective-permute-start.18
  79.8 0.9 collective-permute-start.19
  80.6 1.8 %collective-permute-start.20 = (bf16[448,128]{1,0:T(8,128)(2,1)S(1)}, bf16[448,128]{1,0:T(8,128)(2,1)S(1)}, u32[]{:S(2)}, u32[]{:S(2)}) collective-permute-start(bf16[448,128]{1,0:T(8,128)(2,1)S(1)} %pad_maximum_fusion), channel_id=1, source_target_pairs={{0,6},{1,7},{2,4},{3,5},{4,2},{5,3},{6,0},{7,1},{8,14},{9,15},{10,... | collective-permute-start | bytes 344072 | tf_op jit(solution)/shard_map/ppermute | solution.py:50
  82.5 0.6 constant_dynamic-update-slice_fusion.5
  83.1 0.6 constant_dynamic-update-slice_fusion.4
  83.7 0.6 constant_dynamic-update-slice_fusion.3
  84.3 0.7 constant_dynamic-update-slice_fusion.2
  85.0 0.7 constant_dynamic-update-slice_fusion.1
  85.7 0.7 collective-permute-done.20
  86.3 0.7 constant_dynamic-update-slice_fusion
  87.0 6.7 %backward.1 = bf16[2,64,8,128]{3,2,1,0:T(8,128)(2,1)} custom-call(s32[9,2]{1,0:T(8,128)S(1)} %broadcast_subtract_fusion.codes, bf16[2,64,8,128]{3,2,1,0:T(8,128)(2,1)S(1)} %bitcast.52, bf16[64,16,128]{2,1,0:T(8,128)(2,1)S(1)} %get-tuple-element.16.dpre_ref, bf16[48,8,128]{2,1,0:T(8,128)(2,1)S(1)} %copy-done.5, bf16[48,8,128]{2,1,0:T(8,128)(2,1)S(1)} %copy-done.8, ...), custom_call_target="tpu_custom_call" | custom-call | flops 1000000000 | bytes 5242880 | tf_op jit(solution)/shard_map/backward/pallas_call | solution.py:386
  94.9 1.4 %convert.1 = f32[27,128,128]{2,1,0:T(8,128)} convert(bf16[27,128,128]{2,1,0:T(8,128)(2,1)S(1)} %bitcast.54) | non-fusion elementwise | flops 442368 | bytes 2654208 | tf_op jit(solution)/shard_map/convert_element_type | solution.py:429
  (47 shorter events, 2.4 us)
Async XLA Ops:
  1.3 13.8 %collective-permute-start = (s32[2]{0:T(128)S(1)}, s32[2]{0:T(128)S(1)}, u32[]{:S(2)}, u32[]{:S(2)}) collective-permute-start(s32[2]{0:T(128)S(1)} %get-tuple-element.39), channel_id=1, source_target_pairs={{0,4},{4,8},{8,12},{12,16},{16,20},{20,24},{24,28},{1,5},{5,9},{9,... | collective-permute-start | bytes 32 | tf_op jit(solution)/shard_map/ppermute | solution.py:91
  6.2 8.9 %collective-permute-start.1 = (s32[2]{0:T(128)S(1)}, s32[2]{0:T(128)S(1)}, u32[]{:S(2)}, u32[]{:S(2)}) collective-permute-start(s32[2]{0:T(128)S(1)} %get-tuple-element.39), channel_id=1, source_target_pairs={{4,0},{8,4},{12,8},{16,12},{20,16},{24,20},{28,24},{5,1},{9,5},{13... | collective-permute-start | bytes 32 | tf_op jit(solution)/shard_map/ppermute | solution.py:91
  9.2 12.1 %collective-permute-start.4 = (bf16[48,8,128]{2,1,0:T(8,128)(2,1)}, bf16[48,8,128]{2,1,0:T(8,128)(2,1)S(1)}, u32[]{:S(2)}, u32[]{:S(2)}) collective-permute-start(bf16[48,8,128]{2,1,0:T(8,128)(2,1)} %get-tuple-element.11), channel_id=1, source_target_pairs={{0,4},{4,8},{8,12},{12,16},{16,20},{20,24},{24,28},{1,5},{5,9},{9,... | collective-permute-start | bytes 294920 | tf_op jit(solution)/shard_map/ppermute | solution.py:91
  13.7 7.6 %collective-permute-start.5 = (bf16[48,8,128]{2,1,0:T(8,128)(2,1)}, bf16[48,8,128]{2,1,0:T(8,128)(2,1)S(1)}, u32[]{:S(2)}, u32[]{:S(2)}) collective-permute-start(bf16[48,8,128]{2,1,0:T(8,128)(2,1)} %get-tuple-element.12), channel_id=1, source_target_pairs={{4,0},{8,4},{12,8},{16,12},{20,16},{24,20},{28,24},{5,1},{9,5},{13... | collective-permute-start | bytes 294920 | tf_op jit(solution)/shard_map/ppermute | solution.py:91
  15.1 2.6 %collective-permute-start.2 = (s32[3,2]{1,0:T(4,128)S(1)}, s32[3,2]{1,0:T(4,128)S(1)}, u32[]{:S(2)}, u32[]{:S(2)}) collective-permute-start(s32[3,2]{1,0:T(4,128)S(1)} %pad_add_fusion), channel_id=1, source_target_pairs={{0,1},{1,2},{2,3},{4,5},{5,6},{6,7},{8,9},{9,10},{10,11},{12,13},{... | collective-permute-start | bytes 80 | tf_op jit(solution)/shard_map/ppermute | solution.py:91
  16.4 4.8 %collective-permute-start.3 = (s32[3,2]{1,0:T(4,128)S(1)}, s32[3,2]{1,0:T(4,128)S(1)}, u32[]{:S(2)}, u32[]{:S(2)}) collective-permute-start(s32[3,2]{1,0:T(4,128)S(1)} %pad_add_fusion), channel_id=1, source_target_pairs={{1,0},{2,1},{3,2},{5,4},{6,5},{7,6},{9,8},{10,9},{11,10},{13,12},{... | collective-permute-start | bytes 80 | tf_op jit(solution)/shard_map/ppermute | solution.py:91
  21.3 0.6 copy-start.3
  21.9 0.6 copy-start.6
  24.4 5.6 %collective-permute-start.6 = (bf16[68,8,128]{2,1,0:T(8,128)(2,1)}, bf16[68,8,128]{2,1,0:T(8,128)(2,1)S(1)}, u32[]{:S(2)}, u32[]{:S(2)}) collective-permute-start(bf16[68,8,128]{2,1,0:T(8,128)(2,1)} %get-tuple-element.13), channel_id=1, source_target_pairs={{0,1},{1,2},{2,3},{4,5},{5,6},{6,7},{8,9},{9,10},{10,11},{12,13},{... | collective-permute-start | bytes 417800 | tf_op jit(solution)/shard_map/ppermute | solution.py:91
  28.6 3.5 %collective-permute-start.7 = (bf16[68,8,128]{2,1,0:T(8,128)(2,1)}, bf16[68,8,128]{2,1,0:T(8,128)(2,1)S(1)}, u32[]{:S(2)}, u32[]{:S(2)}) collective-permute-start(bf16[68,8,128]{2,1,0:T(8,128)(2,1)} %get-tuple-element.14), channel_id=1, source_target_pairs={{1,0},{2,1},{3,2},{5,4},{6,5},{7,6},{9,8},{10,9},{11,10},{13,12},{... | collective-permute-start | bytes 417800 | tf_op jit(solution)/shard_map/ppermute | solution.py:91
  32.1 1.0 copy-start
  33.0 0.9 copy-start.1
  34.0 0.9 copy-start.4
  34.9 0.9 copy-start.7
  35.8 1.2 %copy-start.9 = (bf16[27,128,128]{2,1,0:T(8,128)(2,1)S(1)}, bf16[27,128,128]{2,1,0:T(8,128)(2,1)}, u32[]{:S(2)}) copy-start(bf16[27,128,128]{2,1,0:T(8,128)(2,1)} %w_ref.3) | copy-start | bytes 2654212
  46.3 4.6 %collective-permute-start.8 = (bf16[14,128,128]{2,1,0:T(8,128)(2,1)S(1)}, bf16[14,128,128]{2,1,0:T(8,128)(2,1)S(1)}, u32[]{:S(2)}, u32[]{:S(2)}) collective-permute-start(bf16[14,128,128]{2,1,0:T(8,128)(2,1)S(1)} %get-tuple-element.18), channel_id=1, source_target_pairs={{0,1},{1,0},{2,3},{3,2},{4,5},{5,4},{6,7},{7,6},{8,9},{9,8},{10,11... | collective-permute-start | bytes 1376264 | tf_op jit(solution)/shard_map/ppermute | solution.py:50
  51.0 36.0 %copy-start.2 = (bf16[1,1,2,512,128]{4,3,2,1,0:T(8,128)(2,1)S(1)}, bf16[1,1,2,512,128]{4,3,2,1,0:T(8,128)(2,1)}, u32[]{:S(2)}) copy-start(bf16[1,1,2,512,128]{4,3,2,1,0:T(8,128)(2,1)} %param.4) | copy-start | bytes 786436
  51.0 36.0 %copy-start.5 = (bf16[48,8,128]{2,1,0:T(8,128)(2,1)S(1)}, bf16[48,8,128]{2,1,0:T(8,128)(2,1)}, u32[]{:S(2)}) copy-start(bf16[48,8,128]{2,1,0:T(8,128)(2,1)} %copy-done.3) | copy-start | bytes 294916
  51.0 36.0 %copy-start.8 = (bf16[48,8,128]{2,1,0:T(8,128)(2,1)S(1)}, bf16[48,8,128]{2,1,0:T(8,128)(2,1)}, u32[]{:S(2)}) copy-start(bf16[48,8,128]{2,1,0:T(8,128)(2,1)} %copy-done.6) | copy-start | bytes 294916
  51.0 36.0 %copy-start.10 = (bf16[27,128,128]{2,1,0:T(8,128)(2,1)S(1)}, bf16[27,128,128]{2,1,0:T(8,128)(2,1)}, u32[]{:S(2)}) copy-start(bf16[27,128,128]{2,1,0:T(8,128)(2,1)} %w_ref.3) | copy-start | bytes 2654212
  51.1 6.5 %collective-permute-start.11 = (bf16[448,128]{1,0:T(8,128)(2,1)S(1)}, bf16[448,128]{1,0:T(8,128)(2,1)S(1)}, u32[]{:S(2)}, u32[]{:S(2)}) collective-permute-start(bf16[448,128]{1,0:T(8,128)(2,1)S(1)} %get-tuple-element.22), channel_id=1, source_target_pairs={{0,6},{1,7},{2,4},{3,5},{4,2},{5,3},{6,0},{7,1},{8,14},{9,15},{10,... | collective-permute-start | bytes 344072 | tf_op jit(solution)/shard_map/ppermute | solution.py:50
  53.8 6.1 %collective-permute-start.10 = (bf16[448,128]{1,0:T(8,128)(2,1)S(1)}, bf16[448,128]{1,0:T(8,128)(2,1)S(1)}, u32[]{:S(2)}, u32[]{:S(2)}) collective-permute-start(bf16[448,128]{1,0:T(8,128)(2,1)S(1)} %get-tuple-element.23), channel_id=1, source_target_pairs={{0,4},{1,5},{2,6},{3,7},{4,0},{5,1},{6,2},{7,3},{8,12},{9,13},{10,... | collective-permute-start | bytes 344072 | tf_op jit(solution)/shard_map/ppermute | solution.py:50
  54.3 7.3 %collective-permute-start.9 = (bf16[448,128]{1,0:T(8,128)(2,1)S(1)}, bf16[448,128]{1,0:T(8,128)(2,1)S(1)}, u32[]{:S(2)}, u32[]{:S(2)}) collective-permute-start(bf16[448,128]{1,0:T(8,128)(2,1)S(1)} %get-tuple-element.21), channel_id=1, source_target_pairs={{0,2},{1,3},{2,0},{3,1},{4,6},{5,7},{6,4},{7,5},{8,10},{9,11},{10,... | collective-permute-start | bytes 344072 | tf_op jit(solution)/shard_map/ppermute | solution.py:50
  61.7 6.1 %collective-permute-start.14 = (bf16[112,128]{1,0:T(8,128)(2,1)S(1)}, bf16[112,128]{1,0:T(8,128)(2,1)S(1)}, u32[]{:S(2)}, u32[]{:S(2)}) collective-permute-start(bf16[112,128]{1,0:T(8,128)(2,1)S(1)} %get-tuple-element.25), channel_id=1, source_target_pairs={{0,24},{1,25},{2,26},{3,27},{4,28},{5,29},{6,30},{7,31},{8,16},{9,... | collective-permute-start | bytes 86024 | tf_op jit(solution)/shard_map/ppermute | solution.py:50
  65.8 4.8 %collective-permute-start.13 = (bf16[112,128]{1,0:T(8,128)(2,1)S(1)}, bf16[112,128]{1,0:T(8,128)(2,1)S(1)}, u32[]{:S(2)}, u32[]{:S(2)}) collective-permute-start(bf16[112,128]{1,0:T(8,128)(2,1)S(1)} %get-tuple-element.26), channel_id=1, source_target_pairs={{0,16},{1,17},{2,18},{3,19},{4,20},{5,21},{6,22},{7,23},{8,24},{9,... | collective-permute-start | bytes 86024 | tf_op jit(solution)/shard_map/ppermute | solution.py:50
  65.8 4.8 %collective-permute-start.12 = (bf16[112,128]{1,0:T(8,128)(2,1)S(1)}, bf16[112,128]{1,0:T(8,128)(2,1)S(1)}, u32[]{:S(2)}, u32[]{:S(2)}) collective-permute-start(bf16[112,128]{1,0:T(8,128)(2,1)S(1)} %get-tuple-element.24), channel_id=1, source_target_pairs={{0,8},{1,9},{2,10},{3,11},{4,12},{5,13},{6,14},{7,15},{8,0},{9,1},... | collective-permute-start | bytes 86024 | tf_op jit(solution)/shard_map/ppermute | solution.py:50
  71.2 4.4 %collective-permute-start.15 = (bf16[112,128]{1,0:T(8,128)(2,1)S(1)}, bf16[112,128]{1,0:T(8,128)(2,1)S(1)}, u32[]{:S(2)}, u32[]{:S(2)}) collective-permute-start(bf16[112,128]{1,0:T(8,128)(2,1)S(1)} %get-tuple-element.20), channel_id=1, source_target_pairs={{0,8},{1,9},{2,10},{3,11},{4,12},{5,13},{6,14},{7,15},{8,0},{9,1},... | collective-permute-start | bytes 86024 | tf_op jit(solution)/shard_map/ppermute | solution.py:50
  71.2 4.9 %collective-permute-start.16 = (bf16[112,128]{1,0:T(8,128)(2,1)S(1)}, bf16[112,128]{1,0:T(8,128)(2,1)S(1)}, u32[]{:S(2)}, u32[]{:S(2)}) collective-permute-start(bf16[112,128]{1,0:T(8,128)(2,1)S(1)} %get-tuple-element.20), channel_id=1, source_target_pairs={{0,16},{1,17},{2,18},{3,19},{4,20},{5,21},{6,22},{7,23},{8,24},{9,... | collective-permute-start | bytes 86024 | tf_op jit(solution)/shard_map/ppermute | solution.py:50
  73.2 5.7 %collective-permute-start.17 = (bf16[112,128]{1,0:T(8,128)(2,1)S(1)}, bf16[112,128]{1,0:T(8,128)(2,1)S(1)}, u32[]{:S(2)}, u32[]{:S(2)}) collective-permute-start(bf16[112,128]{1,0:T(8,128)(2,1)S(1)} %get-tuple-element.20), channel_id=1, source_target_pairs={{0,24},{1,25},{2,26},{3,27},{4,28},{5,29},{6,30},{7,31},{8,16},{9,... | collective-permute-start | bytes 86024 | tf_op jit(solution)/shard_map/ppermute | solution.py:50
  78.9 5.4 %collective-permute-start.18 = (bf16[448,128]{1,0:T(8,128)(2,1)S(1)}, bf16[448,128]{1,0:T(8,128)(2,1)S(1)}, u32[]{:S(2)}, u32[]{:S(2)}) collective-permute-start(bf16[448,128]{1,0:T(8,128)(2,1)S(1)} %pad_maximum_fusion), channel_id=1, source_target_pairs={{0,2},{1,3},{2,0},{3,1},{4,6},{5,7},{6,4},{7,5},{8,10},{9,11},{10,... | collective-permute-start | bytes 344072 | tf_op jit(solution)/shard_map/ppermute | solution.py:50
  79.8 5.2 %collective-permute-start.19 = (bf16[448,128]{1,0:T(8,128)(2,1)S(1)}, bf16[448,128]{1,0:T(8,128)(2,1)S(1)}, u32[]{:S(2)}, u32[]{:S(2)}) collective-permute-start(bf16[448,128]{1,0:T(8,128)(2,1)S(1)} %pad_maximum_fusion), channel_id=1, source_target_pairs={{0,4},{1,5},{2,6},{3,7},{4,0},{5,1},{6,2},{7,3},{8,12},{9,13},{10,... | collective-permute-start | bytes 344072 | tf_op jit(solution)/shard_map/ppermute | solution.py:50
  80.6 5.7 %collective-permute-start.20 = (bf16[448,128]{1,0:T(8,128)(2,1)S(1)}, bf16[448,128]{1,0:T(8,128)(2,1)S(1)}, u32[]{:S(2)}, u32[]{:S(2)}) collective-permute-start(bf16[448,128]{1,0:T(8,128)(2,1)S(1)} %pad_maximum_fusion), channel_id=1, source_target_pairs={{0,6},{1,7},{2,4},{3,5},{4,2},{5,3},{6,0},{7,1},{8,14},{9,15},{10,... | collective-permute-start | bytes 344072 | tf_op jit(solution)/shard_map/ppermute | solution.py:50
  87.0 6.8 %collective-permute-start.21 = (bf16[1792,128]{1,0:T(8,128)(2,1)}, bf16[1792,128]{1,0:T(8,128)(2,1)S(1)}, u32[]{:S(2)}, u32[]{:S(2)}) collective-permute-start(bf16[1792,128]{1,0:T(8,128)(2,1)} %get-tuple-element.27), channel_id=1, source_target_pairs={{0,1},{1,0},{2,3},{3,2},{4,5},{5,4},{6,7},{7,6},{8,9},{9,8},{10,11... | collective-permute-start | bytes 1376264 | tf_op jit(solution)/shard_map/ppermute | solution.py:50

commit v3 on v2

--- a/solution.py
+++ b/solution.py
@@ -21,6 +21,10 @@
 BF16 = jnp.bfloat16
 
 VZ, VY, VX = 12, 20, 48
+
+SMEM = pl.BlockSpec(memory_space=pltpu.SMEM)
+VMEM = pl.BlockSpec(memory_space=pltpu.VMEM)
+ANY = pl.BlockSpec(memory_space=pl.ANY)
 
 
 def exchange_plan():
@@ -57,31 +61,23 @@
     return place
 
 
-def scatter_sum(total, plan):
-    for group in plan:
-        count = 1 << len(group)
-        me = place_in(group)
-        parts = total.reshape(count, -1, C)
-        arrived = [
-            swap_with(lax.dynamic_index_in_dim(parts, me ^ p, 0, False).astype(BF16), group, p)
-            for p in range(1, count)
-        ]
-        total = lax.dynamic_index_in_dim(parts, me, 0, False)
-        for piece in arrived:
-            total = total + piece.astype(F32)
+def part_of(parts, index):
+    return lax.dynamic_index_in_dim(parts, index, 0, False)
+
+
+def exchange_sum(total, group, ahead=None):
+    count = 1 << len(group)
+    me = place_in(group)
+    parts = total.reshape(count, -1, C)
+    arrived = [
+        swap_with(part_of(parts, me ^ p).astype(BF16), group, p) for p in range(1, count)
+    ]
+    total = part_of(parts, me)
+    if ahead is not None:
+        arrived = ahead(arrived)
+    for piece in arrived:
+        total = total + piece.astype(F32)
     return total
-
-
-def gather_parts(piece, plan):
-    for group in reversed(plan):
-        pieces = [piece] + [swap_with(piece, group, p) for p in range(1, 1 << len(group))]
-        piece = jnp.concatenate(pieces)
-    bits = [b for group in plan for b in reversed(group)]
-    piece = piece.reshape((2,) * len(bits) + (-1, C))
-    for dim, (axis, bit) in enumerate(bits):
-        odd = (lax.axis_index(axis) >> bit) & 1
-        piece = jnp.where(odd == 1, jnp.flip(piece, dim), piece)
-    return piece.reshape(-1, C)
 
 
 def neighbours(up, down, axis):
@@ -91,32 +87,63 @@
     return lax.ppermute(up, axis, forward), lax.ppermute(down, axis, backward)
 
 
-Z_ROWS = NB * 24
-Y_ROWS = NB * 24 + 2 * NB * 5
-
-
-def pack_z_kernel(x_ref, g_ref, up_ref, down_ref):
+Z_ROWS = NB * 24 + 1
+Y_ROWS = NB * 24 + 2 * NB * 5 + 3
+
+
+def pack_z_kernel(sites_ref, x_ref, g_ref, up_ref, down_ref, beside_up, beside_down, sites, sems):
+    moves = [(sites_ref, sites)]
     for s in range(NB):
         base = 24 * s
-        up_ref[base : base + 16] = x_ref[s, 48:64]
-        up_ref[base + 16 : base + 24] = g_ref[s, 56:64]
-        down_ref[base : base + 16] = x_ref[s, 0:16]
-        down_ref[base + 16 : base + 24] = g_ref[s, 0:8]
-
-
-def pack_z(x, g):
+        first, last = slice(base, base + 16), slice(base + 16, base + 24)
+        moves += [
+            (x_ref.at[s, 6:8], up_ref.at[first].reshape(2, 8, 8, C)),
+            (g_ref.at[s, 7], up_ref.at[last]),
+            (x_ref.at[s, 0:2], down_ref.at[first].reshape(2, 8, 8, C)),
+            (g_ref.at[s, 0], down_ref.at[last]),
+            (x_ref.at[s, :, 6:8], beside_up.at[first].reshape(8, 2, 8, C)),
+            (g_ref.at[s, :, 7], beside_up.at[last]),
+            (x_ref.at[s, :, 0:2], beside_down.at[first].reshape(8, 2, 8, C)),
+            (g_ref.at[s, :, 0], beside_down.at[last]),
+        ]
+    copies = [
+        pltpu.make_async_copy(src, dst, sems.at[k]) for k, (src, dst) in enumerate(moves)
+    ]
+    for copy in copies:
+        copy.start()
+    copies[0].wait()
+    lane = lax.broadcasted_iota(jnp.int32, (8, C), 1)
+    code = jnp.zeros((8, C), jnp.int32)
+    for s in range(NB):
+        code = jnp.where(lane == s, SITES - sites[s], code)
+    code = code.astype(F32).astype(BF16)
+    up_ref[Z_ROWS - 1] = code
+    down_ref[Z_ROWS - 1] = code
+    for copy in copies[1:]:
+        copy.wait()
+
+
+def small(limit):
+    return pltpu.CompilerParams(vmem_limit_bytes=limit << 20)
+
+
+def pack_z(sites, x, g):
     shape = jax.ShapeDtypeStruct((Z_ROWS, 8, C), BF16)
-    return pl.pallas_call(pack_z_kernel, out_shape=(shape, shape), name="pack_z")(x, g)
-
-
-def pack_y_kernel(x_ref, g_ref, low_ref, high_ref, up_ref, down_ref):
-    for s in range(NB):
-        base = 24 * s
-        for z in range(8):
-            up_ref[base + 2 * z : base + 2 * z + 2] = x_ref[s, 8 * z + 6 : 8 * z + 8]
-            up_ref[base + 16 + z] = g_ref[s, 8 * z + 7]
-            down_ref[base + 2 * z : base + 2 * z + 2] = x_ref[s, 8 * z : 8 * z + 2]
-            down_ref[base + 16 + z] = g_ref[s, 8 * z]
+    beside = jax.ShapeDtypeStruct((NB * 24, 8, C), BF16)
+    return pl.pallas_call(
+        pack_z_kernel,
+        out_shape=(shape, shape, beside, beside),
+        in_specs=[ANY, ANY, ANY],
+        out_specs=(VMEM,) * 4,
+        scratch_shapes=[pltpu.SMEM((NB,), jnp.int32), pltpu.SemaphoreType.DMA((1 + 8 * NB,))],
+        compiler_params=small(4),
+        name="pack_z",
+    )(sites, x, g)
+
+
+def pack_y_kernel(own_up, own_down, mine_ref, low_ref, high_ref, up_ref, down_ref):
+    up_ref[: NB * 24] = own_up[...]
+    down_ref[: NB * 24] = own_down[...]
     for side, ref in enumerate((low_ref, high_ref)):
         for s in range(NB):
             base = NB * 24 + 10 * side + 5 * s
@@ -126,11 +153,21 @@
                 down_ref[base + 2 * z : base + 2 * z + 2] = ref[src + 8 * z : src + 8 * z + 2]
             up_ref[base + 4] = ref[src + 16 + 7]
             down_ref[base + 4] = ref[src + 16]
-
-
-def pack_y(x, g, low, high):
+    for k, ref in enumerate((mine_ref, low_ref, high_ref)):
+        up_ref[Y_ROWS - 3 + k] = ref[Z_ROWS - 1]
+        down_ref[Y_ROWS - 3 + k] = ref[Z_ROWS - 1]
+
+
+def pack_y(own_up, own_down, mine, low, high):
     shape = jax.ShapeDtypeStruct((Y_ROWS, 8, C), BF16)
-    return pl.pallas_call(pack_y_kernel, out_shape=(shape, shape), name="pack_y")(x, g, low, high)
+    return pl.pallas_call(
+        pack_y_kernel,
+        out_shape=(shape, shape),
+        in_specs=[VMEM] * 5,
+        out_specs=(VMEM, VMEM),
+        compiler_params=small(4),
+        name="pack_y",
+    )(own_up, own_down, mine, low, high)
 
 
 def clear(ref):
@@ -155,7 +192,7 @@
 
         @pl.when(site < SITES)
         def _():
-            put(2, 2 + 8 * py, px, x_ref[s].reshape(8, 8, 8, C))
+            put(2, 2 + 8 * py, px, x_ref[s])
 
         for side, ref in ((1, zl_ref), (2, zh_ref)):
             zsite = codes[side, s]
@@ -213,9 +250,16 @@
     return total
 
 
-def forward_kernel(codes, core, x_ref, g_ref, zl_ref, zh_ref, yl_ref, yh_ref, w_ref,
-                   act_ref, dpre_ref, keep_ref, send_ref, vol, stack, turned):
+def forward_kernel(codes, core, x_hbm, g_hbm, zl_ref, zh_ref, yl_ref, yh_ref, w_hbm,
+                   act_ref, dpre_ref, keep_ref, send_ref, vol, stack, turned, x_ref, g_ref, w_ref, sems):
+    copies = [
+        pltpu.make_async_copy(src, dst, sems.at[k])
+        for k, (src, dst) in enumerate(((x_hbm, x_ref), (w_hbm, w_ref), (g_hbm, g_ref)))
+    ]
+    for copy in copies:
+        copy.start()
     clear(vol)
+    copies[0].wait()
     fill(vol, codes, x_ref, zl_ref, zh_ref, yl_ref, yh_ref)
     places = [place_of(codes[0, s]) for s in range(NB)]
     stack_x(vol, stack, 0, 1, [1 + 8 * py for py, _ in places], [px for _, px in places], 10, 10)
@@ -224,6 +268,8 @@
         return dot(view, w_ref[3 * k : 3 * k + 3].reshape(3 * C, C))
 
     used = [codes[0, s] < SITES for s in range(NB)]
+    copies[1].wait()
+    copies[2].wait()
     for half in range(2):
         pre = convolve(stack, 40 * half, 10, 4, 8, weight)
         sig = 1.0 / (1.0 + jnp.exp(-pre))
@@ -234,7 +280,7 @@
             rows = slice(32 * half, 32 * half + 32)
             a = jnp.where(used[s], act[:, 8 * s : 8 * s + 8], 0.0)
             act_ref[s, rows] = a.astype(BF16)
-            d = g_ref[s, rows].astype(F32) * slope[:, 8 * s : 8 * s + 8]
+            d = g_ref[s, 4 * half : 4 * half + 4].astype(F32).reshape(32, 8, C) * slope[:, 8 * s : 8 * s + 8]
             both.append(jnp.where(used[s], d, 0.0))
         d = jnp.concatenate(both, axis=1).astype(BF16)
         dpre_ref[32 * half : 32 * half + 32] = d
@@ -270,10 +316,6 @@
             send_ref[at] = jnp.zeros((C, C), BF16)
 
 
-SMEM = pl.BlockSpec(memory_space=pltpu.SMEM)
-VMEM = pl.BlockSpec(memory_space=pltpu.VMEM)
-
-
 def forward(codes, core, x, g, zl, zh, yl, yh, w):
     rows = jax.ShapeDtypeStruct((NB, 64, 8, C), BF16)
     return pl.pallas_call(
@@ -284,22 +326,34 @@
             jax.ShapeDtypeStruct((HALF, C, C), F32),
             jax.ShapeDtypeStruct((HALF, C, C), BF16),
         ),
-        in_specs=[SMEM, SMEM] + [VMEM] * 7,
+        in_specs=[SMEM, SMEM, ANY, ANY] + [VMEM] * 4 + [ANY],
         out_specs=(VMEM,) * 4,
         scratch_shapes=[
             pltpu.VMEM((VZ, VY, VX, C), F32),
             pltpu.VMEM((100, 16, 3 * C), BF16),
             pltpu.VMEM((C, 1024), BF16),
+            pltpu.VMEM((NB, 8, 8, 8, C), BF16),
+            pltpu.VMEM((NB, 8, 8, 8, C), BF16),
+            pltpu.VMEM((TAPS, C, C), BF16),
+            pltpu.SemaphoreType.DMA((3,)),
         ],
-        compiler_params=pltpu.CompilerParams(vmem_limit_bytes=40 << 20),
+        compiler_params=small(24),
         cost_estimate=pl.CostEstimate(flops=2 * 10**9, bytes_accessed=5 << 20, transcendentals=1 << 17),
         name="forward",
     )(codes, core, x, g, zl, zh, yl, yh, w)
 
 
-def backward_kernel(codes, x_ref, dpre_ref, zl_ref, zh_ref, yl_ref, yh_ref, w_ref,
-                    grad_ref, vol, stack):
+def backward_kernel(codes, x_hbm, dpre_ref, zl_ref, zh_ref, yl_ref, yh_ref, w_hbm,
+                    grad_ref, vol, stack, x_ref, w_ref, sems):
+    copies = [
+        pltpu.make_async_copy(src, dst, sems.at[k])
+        for k, (src, dst) in enumerate(((x_hbm, x_ref), (w_hbm, w_ref)))
+    ]
+    for copy in copies:
+        copy.start()
     clear(vol)
+    for copy in copies:
+        copy.wait()
     fill(vol, codes, x_ref, zl_ref, zh_ref, yl_ref, yh_ref)
 
     def weight(k, view):
@@ -386,49 +440,113 @@
     return pl.pallas_call(
         backward_kernel,
         out_shape=jax.ShapeDtypeStruct((NB, 64, 8, C), BF16),
-        in_specs=[SMEM] + [VMEM] * 7,
+        in_specs=[SMEM, ANY] + [VMEM] * 5 + [ANY],
         out_specs=VMEM,
         scratch_shapes=[
             pltpu.VMEM((VZ, VY, VX, C), F32),
             pltpu.VMEM((160, 16, 3 * C), BF16),
+            pltpu.VMEM((NB, 8, 8, 8, C), BF16),
+            pltpu.VMEM((TAPS, C, C), BF16),
+            pltpu.SemaphoreType.DMA((2,)),
         ],
-        compiler_params=pltpu.CompilerParams(vmem_limit_bytes=40 << 20),
+        compiler_params=small(24),
         cost_estimate=pl.CostEstimate(flops=10**9, bytes_accessed=5 << 20, transcendentals=1 << 16),
         name="backward",
     )(codes, x, dpre, zl, zh, yl, yh, w)
 
 
+def finish_kernel(first, share, sizes, me, *refs):
+    pieces, out = refs[:-1], refs[-1]
+    middle, inner_sizes = sizes[1], sizes[2:]
+    inner = 1
+    for n in inner_sizes:
+        inner *= n
+    for k, ref in enumerate(pieces):
+        half = (k // middle) ^ me[0]
+        outer = (k % middle) ^ me[1]
+        for r in range(inner):
+            block, stride, rest = outer * inner, inner, r
+            for level, n in enumerate(inner_sizes):
+                stride //= n
+                digit, rest = divmod(rest, stride)
+                block = block + (digit ^ me[2 + level]) * stride
+            value = ref[r * share : (r + 1) * share].astype(F32)
+            for h in range(2):
+                whole, rem = divmod(min(first, TAPS * C - h * first), share)
+
+                @pl.when((half == h) & (block < whole))
+                def _(value=value, h=h, block=block):
+                    out[pl.ds(pl.multiple_of(h * first + block * share, 8), share)] = value
+
+                if rem:
+
+                    @pl.when((half == h) & (block == whole))
+                    def _(value=value, h=h, whole=whole, rem=rem):
+                        at = h * first + whole * share
+                        out[at : at + rem] = value[:rem]
+
+
+def finish(first, share, plan, pieces):
+    sizes = [1 << len(group) for group in plan]
+    me = jnp.stack([place_in(group) for group in plan])
+    return pl.pallas_call(
+        functools.partial(finish_kernel, first, share, sizes),
+        out_shape=jax.ShapeDtypeStruct((TAPS * C, C), F32),
+        in_specs=[SMEM] + [VMEM] * len(pieces),
+        out_specs=VMEM,
+        compiler_params=small(8),
+        name="finish",
+    )(me, *pieces)
+
+
 def local(features, brick_sites, kernel, cotangent):
-    x = features.reshape(NB, 64, 8, C)
-    g = cotangent.reshape(NB, 64, 8, C)
+    x = features.reshape(NB, 8, 8, 8, C)
+    g = cotangent.reshape(NB, 8, 8, 8, C)
     sites = brick_sites.reshape(NB)
     devices = lax.axis_size("gz") * lax.axis_size("gy")
-    up, down = pack_z(x, g)
-    zl, zh = neighbours(up, down, "gz")
-    own_code = SITES - sites
-    code_l, code_h = neighbours(own_code, own_code, "gz")
-    trio = jnp.stack([own_code, code_l, code_h])
-    up, down = pack_y(x, g, zl, zh)
-    yl, yh = neighbours(up, down, "gy")
-    trio_l, trio_h = neighbours(trio, trio, "gy")
-    codes = SITES - jnp.concatenate([trio, trio_l, trio_h])
+    z_up, z_down, own_up, own_down = pack_z(sites, x, g)
+    zl, zh = neighbours(z_up, z_down, "gz")
+    y_up, y_down = pack_y(own_up, own_down, z_up, zl, zh)
+    yl, yh = neighbours(y_up, y_down, "gy")
+    codes = jnp.concatenate(
+        [sites[None]]
+        + [SITES - m[rows:, 0, :NB].astype(jnp.int32)
+           for m, rows in ((zl, Z_ROWS - 1), (zh, Z_ROWS - 1), (yl, Y_ROWS - 3), (yh, Y_ROWS - 3))]
+    )
     core = (lax.axis_index("gy") & 1).reshape(1).astype(jnp.int32)
     act, dpre, keep, send = forward(codes, core, x, g, zl, zh, yl, yh, kernel)
-    grad_in = backward(codes, x, dpre, zl, zh, yl, yh, kernel)
 
     plan = exchange_plan()
-    rows = TAPS * C
-    share = 16 * devices
-    padded_rows = -(-(2 * HALF * C) // share) * share
+    first = HALF * C
+    sharers = devices // 2
+    share = -(-first // (16 * sharers)) * 16
+    half_rows = share * sharers
     arrived = swap_with(send, plan[0], 1)
-    total = (keep + arrived.astype(F32)).reshape(HALF * C, C)
-    total = jnp.pad(total, ((0, padded_rows // 2 - HALF * C), (0, 0)))
+    total = (keep + arrived.astype(F32)).reshape(first, C)
+    total = jnp.pad(total, ((0, half_rows - first), (0, 0)))
+    done = []
+
+    def ahead(arrived):
+        grad = backward(codes, x, dpre, zl, zh, yl, yh, kernel)
+        tied = lax.optimization_barrier(tuple(arrived) + (grad,))
+        done.append(tied[-1])
+        return tied[:-1]
+
+    for level, group in enumerate(plan[1:]):
+        total = exchange_sum(total, group, ahead if level == 0 else None)
     scale = 1.0 / (NB * VOX * devices) ** 0.5
-    mine = (scatter_sum(total, plan[1:]) * scale).astype(BF16)
-    halves = gather_parts(mine, plan).reshape(2, padded_rows // 2, C)
-    grad_kernel = halves[:, : HALF * C].reshape(-1, C)[:rows].reshape(TAPS, C, C).astype(F32)
+    piece = (total * scale).astype(BF16)
+    grad_in = done[0]
+
+    pieces = [piece]
+    for level, group in enumerate(reversed(plan[1:])):
+        if level > 0:
+            pieces = [jnp.concatenate(pieces)]
+        pieces = [pieces[0]] + [swap_with(pieces[0], group, p) for p in range(1, 1 << len(group))]
+    others = [swap_with(p, plan[0], 1) for p in pieces]
+    grad_kernel = finish(first, share, plan, pieces + others)
     shape = (1, 1, NB, VOX, C)
-    return act.reshape(shape), grad_in.reshape(shape), grad_kernel
+    return act.reshape(shape), grad_in.reshape(shape), grad_kernel.reshape(TAPS, C, C)
 
 
 def solution(mesh):

time: 96.9 us -> 81.7 us (0.84)
  starting transfers between devices: 40.6 us -> 32.1 us
  local copies, waits for them, and re-layouts: 10.3 us -> 7.74 us
  waiting for transfers between devices: 21.1 us -> 18.6 us
  other arithmetic: 3.79 us -> 2.23 us
    ppermute x8 -> x4, starting transfers between devices: 20.1 us -> 10 us  [neighbours(): return (lax.ppermute(up, axis, forward), lax.ppermute(down, axis, backward))]
    ppermute x14 -> x17, waiting for transfers between devices: 15.5 us -> 12.5 us  [swap_with(): return lax.ppermute(value, AXES, pairs)]
    unnamed x28 -> x18, local copies, waits for them, and re-layouts: 9.3 us -> 6.54 us
    add x2, other arithmetic: 0.13 us -> 2.1 us  [the longest x1 1.1 us: local(): total = (keep + arrived.astype(F32)).reshape(first, C)]
    ppermute x14 -> x17, starting transfers between devices: 20.5 us -> 22.1 us  [swap_with(): return lax.ppermute(value, AXES, pairs)]
    convert_element_type x1, other arithmetic: 1.41 us -> 0.02 us  [local(): piece = (total * scale).astype(BF16)]
    ppermute x8 -> x4, waiting for transfers between devices: 5.63 us -> 6.06 us  [neighbours(): return (lax.ppermute(up, axis, forward), lax.ppermute(down, axis, backward))]
    pallas_call x2 -> x3, Pallas kernels: 3.52 us -> 3.2 us  [the longest x1 2.46 us: finish(): pl.pallas_call(functools.partial(finish_kernel, first, share, sizes), out...]
  transfers between devices with their start and end apart: 22 -> 21, of which waited for: 11 -> 15; matrix products, arithmetic and copies ran while one was open for 3% -> 0% of each run, Pallas kernels for 9% -> 9%
where the time goes in v3:
time: 81.7 us; the launch traced here: 81.3 us
  starting transfers between devices  32.1 us (39%)
  Pallas kernels  19.9 us (24%)
  waiting for transfers between devices  18.6 us (23%)
  local copies, waits for them, and re-layouts  7.74 us (9%)
  other arithmetic  2.23 us (3%)
  between operations  0.85 us (1%)
    ppermute x17, starting transfers between devices, swap_with(): return lax.ppermute(value, AXES, pairs)  22.1 us
    ppermute x17, waiting for transfers between devices, swap_with(): return lax.ppermute(value, AXES, pairs)  12.5 us
    ppermute x4, starting transfers between devices, neighbours(): return (lax.ppermute(up, axis, forward), lax.ppermute(down, axis, backward))  10 us
    pallas_call x1, Pallas kernels, forward(): pl.pallas_call(forward_kernel, out_shape=(rows, jax.ShapeDtypeStruct((64,...  9.72 us
    pallas_call x1, Pallas kernels, backward(): pl.pallas_call(backward_kernel, out_shape=jax.ShapeDtypeStruct((NB, 64, 8...  6.94 us
    unnamed x18, local copies, waits for them, and re-layouts  6.54 us
    ppermute x4, waiting for transfers between devices, neighbours(): return (lax.ppermute(up, axis, forward), lax.ppermute(down, axis, backward))  6.06 us
    pallas_call x1, Pallas kernels, finish(): pl.pallas_call(functools.partial(finish_kernel, first, share, sizes), out...  2.46 us
  transfers between devices with their start and end apart: 21, of which 15 were waited for; matrix products, arithmetic and copies ran while one was open for 0% of the time, Pallas kernels for 9%

profile of v3, /device:TPU:0, one launch (start us, length us, event | category | flops | bytes accessed | tf_op | source)
XLA Modules:
  0.0 81.3 jit_solution(13889724004674378641)
XLA Ops:
  0.6 0.9 %copy-done = bf16[1,1,2,512,128]{4,3,2,1,0:T(8,128)(2,1)S(1)} copy-done((bf16[1,1,2,512,128]{4,3,2,1,0:T(8,128)(2,1)S(1)}, bf16[1,1,2,512,128]{4,3,2,1,0:T(8,128)(2,1)}, u32[]{:S(2)}) %copy-start) | copy-done | bytes 262168
  1.6 0.9 %copy-done.2 = bf16[1,1,2,512,128]{4,3,2,1,0:T(8,128)(2,1)S(1)} copy-done((bf16[1,1,2,512,128]{4,3,2,1,0:T(8,128)(2,1)S(1)}, bf16[1,1,2,512,128]{4,3,2,1,0:T(8,128)(2,1)}, u32[]{:S(2)}) %copy-start.2) | copy-done | bytes 262168
  2.5 0.7 copy-done.5
  3.2 0.7 pack_z.1
  3.9 1.3 %collective-permute-start.1 = (bf16[49,8,128]{2,1,0:T(8,128)(2,1)S(1)}, bf16[49,8,128]{2,1,0:T(8,128)(2,1)S(1)}, u32[]{:S(2)}, u32[]{:S(2)}) collective-permute-start(bf16[49,8,128]{2,1,0:T(8,128)(2,1)S(1)} %get-tuple-element.18), channel_id=1, source_target_pairs={{4,0},{8,4},{12,8},{16,12},{20,16},{24,20},{28,24},{5,1},{9,5},{13... | collective-permute-start | bytes 301064 | tf_op jit(solution)/shard_map/ppermute | solution.py:87
  5.2 5.5 %collective-permute-start = (bf16[49,8,128]{2,1,0:T(8,128)(2,1)S(1)}, bf16[49,8,128]{2,1,0:T(8,128)(2,1)S(1)}, u32[]{:S(2)}, u32[]{:S(2)}) collective-permute-start(bf16[49,8,128]{2,1,0:T(8,128)(2,1)S(1)} %get-tuple-element.17.mine_ref), channel_id=1, source_target_pairs={{0,4},{4,8},{8,12},{12,16},{16,20},{20,24},{24,28},{1,5},{5,9},{9,... | collective-permute-start | bytes 301064 | tf_op jit(solution)/shard_map/ppermute | solution.py:87
  10.8 0.9 %collective-permute-done.1.high_ref.zh_ref = bf16[49,8,128]{2,1,0:T(8,128)(2,1)S(1)} collective-permute-done((bf16[49,8,128]{2,1,0:T(8,128)(2,1)S(1)}, bf16[49,8,128]{2,1,0:T(8,128)(2,1)S(1)}, u32[]{:S(2)}, u32[]{:S(2)}) %collective-permute-start.1) | collective-permute-done | bytes 100384 | tf_op jit(solution)/shard_map/ppermute | solution.py:87
  11.7 2.3 %collective-permute-done.low_ref.zl_ref = bf16[49,8,128]{2,1,0:T(8,128)(2,1)S(1)} collective-permute-done((bf16[49,8,128]{2,1,0:T(8,128)(2,1)S(1)}, bf16[49,8,128]{2,1,0:T(8,128)(2,1)S(1)}, u32[]{:S(2)}, u32[]{:S(2)}) %collective-permute-start) | collective-permute-done | bytes 100384 | tf_op jit(solution)/shard_map/ppermute | solution.py:87
  14.0 1.9 %collective-permute-start.2 = (bf16[71,8,128]{2,1,0:T(8,128)(2,1)S(1)}, bf16[71,8,128]{2,1,0:T(8,128)(2,1)S(1)}, u32[]{:S(2)}, u32[]{:S(2)}) collective-permute-start(bf16[71,8,128]{2,1,0:T(8,128)(2,1)S(1)} %get-tuple-element.21), channel_id=1, source_target_pairs={{0,1},{1,2},{2,3},{4,5},{5,6},{6,7},{8,9},{9,10},{10,11},{12,13},{... | collective-permute-start | bytes 436232 | tf_op jit(solution)/shard_map/ppermute | solution.py:87
  15.9 1.3 %collective-permute-start.3 = (bf16[71,8,128]{2,1,0:T(8,128)(2,1)S(1)}, bf16[71,8,128]{2,1,0:T(8,128)(2,1)S(1)}, u32[]{:S(2)}, u32[]{:S(2)}) collective-permute-start(bf16[71,8,128]{2,1,0:T(8,128)(2,1)S(1)} %get-tuple-element.22), channel_id=1, source_target_pairs={{1,0},{2,1},{3,2},{5,4},{6,5},{7,6},{9,8},{10,9},{11,10},{13,12},{... | collective-permute-start | bytes 436232 | tf_op jit(solution)/shard_map/ppermute | solution.py:87
  17.4 0.1 copy.26
  17.5 2.9 %collective-permute-done.3.yh_ref = bf16[71,8,128]{2,1,0:T(8,128)(2,1)S(1)} collective-permute-done((bf16[71,8,128]{2,1,0:T(8,128)(2,1)S(1)}, bf16[71,8,128]{2,1,0:T(8,128)(2,1)S(1)}, u32[]{:S(2)}, u32[]{:S(2)}) %collective-permute-start.3) | collective-permute-done | bytes 145440 | tf_op jit(solution)/shard_map/ppermute | solution.py:87
  20.5 0.7 concatenate.6.codes
  21.3 0.9 %copy-done.1 = bf16[1,1,2,512,128]{4,3,2,1,0:T(8,128)(2,1)S(1)} copy-done((bf16[1,1,2,512,128]{4,3,2,1,0:T(8,128)(2,1)S(1)}, bf16[1,1,2,512,128]{4,3,2,1,0:T(8,128)(2,1)}, u32[]{:S(2)}) %copy-start.1) | copy-done | bytes 262168
  22.2 0.9 %copy-done.3 = bf16[1,1,2,512,128]{4,3,2,1,0:T(8,128)(2,1)S(1)} copy-done((bf16[1,1,2,512,128]{4,3,2,1,0:T(8,128)(2,1)S(1)}, bf16[1,1,2,512,128]{4,3,2,1,0:T(8,128)(2,1)}, u32[]{:S(2)}) %copy-start.3) | copy-done | bytes 262168
  23.2 1.2 %copy-done.6 = bf16[27,128,128]{2,1,0:T(8,128)(2,1)S(1)} copy-done((bf16[27,128,128]{2,1,0:T(8,128)(2,1)S(1)}, bf16[27,128,128]{2,1,0:T(8,128)(2,1)}, u32[]{:S(2)}) %copy-start.6) | copy-done | bytes 884760
  24.4 9.7 %forward.1 = (bf16[2,64,8,128]{3,2,1,0:T(8,128)(2,1)}, bf16[64,16,128]{2,1,0:T(8,128)(2,1)S(1)}, f32[14,128,128]{2,1,0:T(8,128)S(1)}, bf16[14,128,128]{2,1,0:T(8,128)(2,1)S(1)}) custom-call(s32[9,2]{1,0:T(8,128)S(1)} %concatenate.6.codes, s32[1]{0:T(128)} %bitcast.8.core, bf16[2,8,8,8,128]{4,3,2,1,0:T(8,128)(2,1)S(1)} %bitcast.50, ...), custom_call_target="tpu_custom_call" | custom-call | flops 2000000000 | bytes 5242880 | tf_op jit(solution)/shard_map/forward/pallas_call | solution.py:321
  34.1 3.7 %collective-permute-start.4 = (bf16[14,128,128]{2,1,0:T(8,128)(2,1)S(1)}, bf16[14,128,128]{2,1,0:T(8,128)(2,1)}, u32[]{:S(2)}, u32[]{:S(2)}) collective-permute-start(bf16[14,128,128]{2,1,0:T(8,128)(2,1)S(1)} %get-tuple-element.25), channel_id=1, source_target_pairs={{0,1},{1,0},{2,3},{3,2},{4,5},{5,4},{6,7},{7,6},{8,9},{9,8},{10,11... | collective-permute-start | bytes 1376264 | tf_op jit(solution)/shard_map/ppermute | solution.py:54
  37.8 1.6 %collective-permute-done.4 = bf16[14,128,128]{2,1,0:T(8,128)(2,1)} collective-permute-done((bf16[14,128,128]{2,1,0:T(8,128)(2,1)S(1)}, bf16[14,128,128]{2,1,0:T(8,128)(2,1)}, u32[]{:S(2)}, u32[]{:S(2)}) %collective-permute-start.4) | collective-permute-done | bytes 458784 | tf_op jit(solution)/shard_map/ppermute | solution.py:54
  39.4 1.1 %convert_add_fusion = f32[14,128,128]{2,1,0:T(8,128)S(1)} fusion(f32[14,128,128]{2,1,0:T(8,128)S(1)} %get-tuple-element.24, bf16[14,128,128]{2,1,0:T(8,128)(2,1)} %collective-permute-done.4), kind=kLoop, calls=%fused_computation | loop fusion | flops 458752 | bytes 2293760 | tf_op jit(solution)/shard_map/add | solution.py:525
  40.5 0.9 %copy-done.8 = f32[14,128,128]{2,1,0:T(8,128)} copy-done((f32[14,128,128]{2,1,0:T(8,128)}, f32[14,128,128]{2,1,0:T(8,128)S(1)}, u32[]{:S(2)}) %copy-start.8) | copy-done | bytes 917528
  41.5 2.1 %collective-permute-start.7 = (bf16[448,128]{1,0:T(8,128)(2,1)S(1)}, bf16[448,128]{1,0:T(8,128)(2,1)S(1)}, u32[]{:S(2)}, u32[]{:S(2)}) collective-permute-start(bf16[448,128]{1,0:T(8,128)(2,1)S(1)} %get-tuple-element.31), channel_id=1, source_target_pairs={{0,6},{1,7},{2,4},{3,5},{4,2},{5,3},{6,0},{7,1},{8,14},{9,15},{10,... | collective-permute-start | bytes 344072 | tf_op jit(solution)/shard_map/ppermute | solution.py:54
  43.6 0.6 collective-permute-start.6
  44.2 1.4 %collective-permute-start.5 = (bf16[448,128]{1,0:T(8,128)(2,1)S(1)}, bf16[448,128]{1,0:T(8,128)(2,1)S(1)}, u32[]{:S(2)}, u32[]{:S(2)}) collective-permute-start(bf16[448,128]{1,0:T(8,128)(2,1)S(1)} %get-tuple-element.33), channel_id=1, source_target_pairs={{0,2},{1,3},{2,0},{3,1},{4,6},{5,7},{6,4},{7,5},{8,10},{9,11},{10,... | collective-permute-start | bytes 344072 | tf_op jit(solution)/shard_map/ppermute | solution.py:54
  45.6 6.9 %backward.1 = bf16[2,64,8,128]{3,2,1,0:T(8,128)(2,1)} custom-call(s32[9,2]{1,0:T(8,128)S(1)} %concatenate.6.codes, bf16[2,8,8,8,128]{4,3,2,1,0:T(8,128)(2,1)S(1)} %bitcast.51, bf16[64,16,128]{2,1,0:T(8,128)(2,1)S(1)} %get-tuple-element.26.dpre_ref, bf16[49,8,128]{2,1,0:T(8,128)(2,1)S(1)} %collective-permute-done.low_ref.zl_ref, ...), custom_call_target="tpu_custom_call" | custom-call | flops 1000000000 | bytes 5242880 | tf_op jit(solution)/shard_map/backward/pallas_call | solution.py:440
  52.5 1.0 %fusion.1 = f32[448,128]{1,0:T(8,128)S(1)} fusion(bf16[448,128]{1,0:T(8,128)(2,1)S(1)} %collective-permute-done.7, bf16[448,128]{1,0:T(8,128)(2,1)S(1)} %collective-permute-done.6, bf16[448,128]{1,0:T(8,128)(2,1)S(1)} %collective-permute-done.5, f32[4,448,128]{2,1,0:T(8,128)} %bitcast.55, s32[]{:T(128)S(6)} %select_n.29), kind=kLoop, calls=%fused_computation.3 | loop fusion | flops 344064 | bytes 802820 | tf_op jit(solution)/shard_map/add | solution.py:79
  53.6 3.3 %collective-permute-start.8 = (bf16[112,128]{1,0:T(8,128)(2,1)S(1)}, bf16[112,128]{1,0:T(8,128)(2,1)S(1)}, u32[]{:S(2)}, u32[]{:S(2)}) collective-permute-start(bf16[112,128]{1,0:T(8,128)(2,1)S(1)} %get-tuple-element.34), channel_id=1, source_target_pairs={{0,8},{1,9},{2,10},{3,11},{4,12},{5,13},{6,14},{7,15},{8,0},{9,1},... | collective-permute-start | bytes 86024 | tf_op jit(solution)/shard_map/ppermute | solution.py:54
  56.8 2.5 %collective-permute-start.10 = (bf16[112,128]{1,0:T(8,128)(2,1)S(1)}, bf16[112,128]{1,0:T(8,128)(2,1)S(1)}, u32[]{:S(2)}, u32[]{:S(2)}) collective-permute-start(bf16[112,128]{1,0:T(8,128)(2,1)S(1)} %get-tuple-element.35), channel_id=1, source_target_pairs={{0,24},{1,25},{2,26},{3,27},{4,28},{5,29},{6,30},{7,31},{8,16},{9,... | collective-permute-start | bytes 86024 | tf_op jit(solution)/shard_map/ppermute | solution.py:54
  59.5 3.1 %collective-permute-done.10 = bf16[112,128]{1,0:T(8,128)(2,1)S(1)} collective-permute-done((bf16[112,128]{1,0:T(8,128)(2,1)S(1)}, bf16[112,128]{1,0:T(8,128)(2,1)S(1)}, u32[]{:S(2)}, u32[]{:S(2)}) %collective-permute-start.10) | collective-permute-done | bytes 28704 | tf_op jit(solution)/shard_map/ppermute | solution.py:54
  62.6 1.8 %collective-permute-done.9 = bf16[112,128]{1,0:T(8,128)(2,1)S(1)} collective-permute-done((bf16[112,128]{1,0:T(8,128)(2,1)S(1)}, bf16[112,128]{1,0:T(8,128)(2,1)S(1)}, u32[]{:S(2)}, u32[]{:S(2)}) %collective-permute-start.9) | collective-permute-done | bytes 28704 | tf_op jit(solution)/shard_map/ppermute | solution.py:54
  64.5 1.3 %collective-permute-start.13 = (bf16[112,128]{1,0:T(8,128)(2,1)S(1)}, bf16[112,128]{1,0:T(8,128)(2,1)S(1)}, u32[]{:S(2)}, u32[]{:S(2)}) collective-permute-start(bf16[112,128]{1,0:T(8,128)(2,1)S(1)} %fusion.8), channel_id=1, source_target_pairs={{0,24},{1,25},{2,26},{3,27},{4,28},{5,29},{6,30},{7,31},{8,16},{9,... | collective-permute-start | bytes 86024 | tf_op jit(solution)/shard_map/ppermute | solution.py:54
  65.7 0.7 collective-permute-start.12
  66.4 2.5 %collective-permute-start.11 = (bf16[112,128]{1,0:T(8,128)(2,1)S(1)}, bf16[112,128]{1,0:T(8,128)(2,1)S(1)}, u32[]{:S(2)}, u32[]{:S(2)}) collective-permute-start(bf16[112,128]{1,0:T(8,128)(2,1)S(1)} %fusion.8), channel_id=1, source_target_pairs={{0,8},{1,9},{2,10},{3,11},{4,12},{5,13},{6,14},{7,15},{8,0},{9,1},... | collective-permute-start | bytes 86024 | tf_op jit(solution)/shard_map/ppermute | solution.py:54
  68.9 1.3 %collective-permute-done.13 = bf16[112,128]{1,0:T(8,128)(2,1)S(1)} collective-permute-done((bf16[112,128]{1,0:T(8,128)(2,1)S(1)}, bf16[112,128]{1,0:T(8,128)(2,1)S(1)}, u32[]{:S(2)}, u32[]{:S(2)}) %collective-permute-start.13) | collective-permute-done | bytes 28704 | tf_op jit(solution)/shard_map/ppermute | solution.py:54
  70.2 0.7 collective-permute-done.12
  70.9 0.1 collective-permute-done.11
  71.1 0.1 collective-permute-start.16
  71.2 1.6 %collective-permute-start.15 = (bf16[448,128]{1,0:T(8,128)(2,1)S(1)}, bf16[448,128]{1,0:T(8,128)(2,1)S(1)}, u32[]{:S(2)}, u32[]{:S(2)}) collective-permute-start(bf16[448,128]{1,0:T(8,128)(2,1)S(1)} %pad_maximum_fusion.refs_0_), channel_id=1, source_target_pairs={{0,4},{1,5},{2,6},{3,7},{4,0},{5,1},{6,2},{7,3},{8,12},{9,13},{10,... | collective-permute-start | bytes 344072 | tf_op jit(solution)/shard_map/ppermute | solution.py:54
  72.8 1.9 %collective-permute-start.14 = (bf16[448,128]{1,0:T(8,128)(2,1)S(1)}, bf16[448,128]{1,0:T(8,128)(2,1)S(1)}, u32[]{:S(2)}, u32[]{:S(2)}) collective-permute-start(bf16[448,128]{1,0:T(8,128)(2,1)S(1)} %pad_maximum_fusion.refs_0_), channel_id=1, source_target_pairs={{0,2},{1,3},{2,0},{3,1},{4,6},{5,7},{6,4},{7,5},{8,10},{9,11},{10,... | collective-permute-start | bytes 344072 | tf_op jit(solution)/shard_map/ppermute | solution.py:54
  74.6 2.3 %collective-permute-done.16.refs_3_ = bf16[448,128]{1,0:T(8,128)(2,1)S(1)} collective-permute-done((bf16[448,128]{1,0:T(8,128)(2,1)S(1)}, bf16[448,128]{1,0:T(8,128)(2,1)S(1)}, u32[]{:S(2)}, u32[]{:S(2)}) %collective-permute-start.16) | collective-permute-done | bytes 114720 | tf_op jit(solution)/shard_map/ppermute | solution.py:54
  76.9 0.3 collective-permute-done.15.refs_2_
  77.2 0.2 collective-permute-start.19
  77.4 0.1 collective-permute-done.14.refs_1_
  77.6 0.2 collective-permute-start.18
  77.8 0.4 collective-permute-done.20.refs_7_
  78.3 0.3 collective-permute-done.19.refs_6_
  78.6 0.3 collective-permute-done.18.refs_5_
  78.9 2.5 %finish.1 = f32[3456,128]{1,0:T(8,128)} custom-call(s32[3]{0:T(128)S(1)} %pad_add_fusion.me, bf16[448,128]{1,0:T(8,128)(2,1)S(1)} %pad_maximum_fusion.refs_0_, bf16[448,128]{1,0:T(8,128)(2,1)S(1)} %collective-permute-done.14.refs_1_, bf16[448,128]{1,0:T(8,128)(2,1)S(1)} %collective-permute-done.15.refs_2_, ...), custom_call_target="tpu_custom_call" | custom-call | tf_op jit(solution)/shard_map/finish/pallas_call | solution.py:492
  (33 shorter events, 0.6 us)
Async XLA Ops:
  0.6 1.0 %copy-start = (bf16[1,1,2,512,128]{4,3,2,1,0:T(8,128)(2,1)S(1)}, bf16[1,1,2,512,128]{4,3,2,1,0:T(8,128)(2,1)}, u32[]{:S(2)}) copy-start(bf16[1,1,2,512,128]{4,3,2,1,0:T(8,128)(2,1)} %param.7) | copy-start | bytes 786436
  1.6 0.9 %copy-start.2 = (bf16[1,1,2,512,128]{4,3,2,1,0:T(8,128)(2,1)S(1)}, bf16[1,1,2,512,128]{4,3,2,1,0:T(8,128)(2,1)}, u32[]{:S(2)}) copy-start(bf16[1,1,2,512,128]{4,3,2,1,0:T(8,128)(2,1)} %param.4) | copy-start | bytes 786436
  2.5 0.7 copy-start.5
  3.9 7.7 %collective-permute-start.1 = (bf16[49,8,128]{2,1,0:T(8,128)(2,1)S(1)}, bf16[49,8,128]{2,1,0:T(8,128)(2,1)S(1)}, u32[]{:S(2)}, u32[]{:S(2)}) collective-permute-start(bf16[49,8,128]{2,1,0:T(8,128)(2,1)S(1)} %get-tuple-element.18), channel_id=1, source_target_pairs={{4,0},{8,4},{12,8},{16,12},{20,16},{24,20},{28,24},{5,1},{9,5},{13... | collective-permute-start | bytes 301064 | tf_op jit(solution)/shard_map/ppermute | solution.py:87
  5.2 8.7 %collective-permute-start = (bf16[49,8,128]{2,1,0:T(8,128)(2,1)S(1)}, bf16[49,8,128]{2,1,0:T(8,128)(2,1)S(1)}, u32[]{:S(2)}, u32[]{:S(2)}) collective-permute-start(bf16[49,8,128]{2,1,0:T(8,128)(2,1)S(1)} %get-tuple-element.17.mine_ref), channel_id=1, source_target_pairs={{0,4},{4,8},{8,12},{12,16},{16,20},{20,24},{24,28},{1,5},{5,9},{9,... | collective-permute-start | bytes 301064 | tf_op jit(solution)/shard_map/ppermute | solution.py:87
  14.0 3.3 %collective-permute-start.2 = (bf16[71,8,128]{2,1,0:T(8,128)(2,1)S(1)}, bf16[71,8,128]{2,1,0:T(8,128)(2,1)S(1)}, u32[]{:S(2)}, u32[]{:S(2)}) collective-permute-start(bf16[71,8,128]{2,1,0:T(8,128)(2,1)S(1)} %get-tuple-element.21), channel_id=1, source_target_pairs={{0,1},{1,2},{2,3},{4,5},{5,6},{6,7},{8,9},{9,10},{10,11},{12,13},{... | collective-permute-start | bytes 436232 | tf_op jit(solution)/shard_map/ppermute | solution.py:87
  15.9 4.4 %collective-permute-start.3 = (bf16[71,8,128]{2,1,0:T(8,128)(2,1)S(1)}, bf16[71,8,128]{2,1,0:T(8,128)(2,1)S(1)}, u32[]{:S(2)}, u32[]{:S(2)}) collective-permute-start(bf16[71,8,128]{2,1,0:T(8,128)(2,1)S(1)} %get-tuple-element.22), channel_id=1, source_target_pairs={{1,0},{2,1},{3,2},{5,4},{6,5},{7,6},{9,8},{10,9},{11,10},{13,12},{... | collective-permute-start | bytes 436232 | tf_op jit(solution)/shard_map/ppermute | solution.py:87
  21.3 1.0 %copy-start.1 = (bf16[1,1,2,512,128]{4,3,2,1,0:T(8,128)(2,1)S(1)}, bf16[1,1,2,512,128]{4,3,2,1,0:T(8,128)(2,1)}, u32[]{:S(2)}) copy-start(bf16[1,1,2,512,128]{4,3,2,1,0:T(8,128)(2,1)} %param.7) | copy-start | bytes 786436
  22.2 0.9 %copy-start.3 = (bf16[1,1,2,512,128]{4,3,2,1,0:T(8,128)(2,1)S(1)}, bf16[1,1,2,512,128]{4,3,2,1,0:T(8,128)(2,1)}, u32[]{:S(2)}) copy-start(bf16[1,1,2,512,128]{4,3,2,1,0:T(8,128)(2,1)} %param.4) | copy-start | bytes 786436
  23.2 1.2 %copy-start.6 = (bf16[27,128,128]{2,1,0:T(8,128)(2,1)S(1)}, bf16[27,128,128]{2,1,0:T(8,128)(2,1)}, u32[]{:S(2)}) copy-start(bf16[27,128,128]{2,1,0:T(8,128)(2,1)} %w_hbm.3) | copy-start | bytes 2654212
  34.1 11.5 %copy-start.4 = (bf16[1,1,2,512,128]{4,3,2,1,0:T(8,128)(2,1)S(1)}, bf16[1,1,2,512,128]{4,3,2,1,0:T(8,128)(2,1)}, u32[]{:S(2)}) copy-start(bf16[1,1,2,512,128]{4,3,2,1,0:T(8,128)(2,1)} %param.4) | copy-start | bytes 786436
  34.1 11.5 %copy-start.7 = (bf16[27,128,128]{2,1,0:T(8,128)(2,1)S(1)}, bf16[27,128,128]{2,1,0:T(8,128)(2,1)}, u32[]{:S(2)}) copy-start(bf16[27,128,128]{2,1,0:T(8,128)(2,1)} %w_hbm.3) | copy-start | bytes 2654212
  34.1 5.3 %collective-permute-start.4 = (bf16[14,128,128]{2,1,0:T(8,128)(2,1)S(1)}, bf16[14,128,128]{2,1,0:T(8,128)(2,1)}, u32[]{:S(2)}, u32[]{:S(2)}) collective-permute-start(bf16[14,128,128]{2,1,0:T(8,128)(2,1)S(1)} %get-tuple-element.25), channel_id=1, source_target_pairs={{0,1},{1,0},{2,3},{3,2},{4,5},{5,4},{6,7},{7,6},{8,9},{9,8},{10,11... | collective-permute-start | bytes 1376264 | tf_op jit(solution)/shard_map/ppermute | solution.py:54
  40.5 0.9 %copy-start.8 = (f32[14,128,128]{2,1,0:T(8,128)}, f32[14,128,128]{2,1,0:T(8,128)S(1)}, u32[]{:S(2)}) copy-start(f32[14,128,128]{2,1,0:T(8,128)S(1)} %convert_add_fusion) | copy-start | bytes 2752516
  41.5 11.0 %collective-permute-start.7 = (bf16[448,128]{1,0:T(8,128)(2,1)S(1)}, bf16[448,128]{1,0:T(8,128)(2,1)S(1)}, u32[]{:S(2)}, u32[]{:S(2)}) collective-permute-start(bf16[448,128]{1,0:T(8,128)(2,1)S(1)} %get-tuple-element.31), channel_id=1, source_target_pairs={{0,6},{1,7},{2,4},{3,5},{4,2},{5,3},{6,0},{7,1},{8,14},{9,15},{10,... | collective-permute-start | bytes 344072 | tf_op jit(solution)/shard_map/ppermute | solution.py:54
  43.6 8.9 %collective-permute-start.6 = (bf16[448,128]{1,0:T(8,128)(2,1)S(1)}, bf16[448,128]{1,0:T(8,128)(2,1)S(1)}, u32[]{:S(2)}, u32[]{:S(2)}) collective-permute-start(bf16[448,128]{1,0:T(8,128)(2,1)S(1)} %get-tuple-element.32), channel_id=1, source_target_pairs={{0,4},{1,5},{2,6},{3,7},{4,0},{5,1},{6,2},{7,3},{8,12},{9,13},{10,... | collective-permute-start | bytes 344072 | tf_op jit(solution)/shard_map/ppermute | solution.py:54
  44.2 8.4 %collective-permute-start.5 = (bf16[448,128]{1,0:T(8,128)(2,1)S(1)}, bf16[448,128]{1,0:T(8,128)(2,1)S(1)}, u32[]{:S(2)}, u32[]{:S(2)}) collective-permute-start(bf16[448,128]{1,0:T(8,128)(2,1)S(1)} %get-tuple-element.33), channel_id=1, source_target_pairs={{0,2},{1,3},{2,0},{3,1},{4,6},{5,7},{6,4},{7,5},{8,10},{9,11},{10,... | collective-permute-start | bytes 344072 | tf_op jit(solution)/shard_map/ppermute | solution.py:54
  53.6 5.9 %collective-permute-start.8 = (bf16[112,128]{1,0:T(8,128)(2,1)S(1)}, bf16[112,128]{1,0:T(8,128)(2,1)S(1)}, u32[]{:S(2)}, u32[]{:S(2)}) collective-permute-start(bf16[112,128]{1,0:T(8,128)(2,1)S(1)} %get-tuple-element.34), channel_id=1, source_target_pairs={{0,8},{1,9},{2,10},{3,11},{4,12},{5,13},{6,14},{7,15},{8,0},{9,1},... | collective-permute-start | bytes 86024 | tf_op jit(solution)/shard_map/ppermute | solution.py:54
  56.8 5.8 %collective-permute-start.10 = (bf16[112,128]{1,0:T(8,128)(2,1)S(1)}, bf16[112,128]{1,0:T(8,128)(2,1)S(1)}, u32[]{:S(2)}, u32[]{:S(2)}) collective-permute-start(bf16[112,128]{1,0:T(8,128)(2,1)S(1)} %get-tuple-element.35), channel_id=1, source_target_pairs={{0,24},{1,25},{2,26},{3,27},{4,28},{5,29},{6,30},{7,31},{8,16},{9,... | collective-permute-start | bytes 86024 | tf_op jit(solution)/shard_map/ppermute | solution.py:54
  59.4 5.1 %collective-permute-start.9 = (bf16[112,128]{1,0:T(8,128)(2,1)S(1)}, bf16[112,128]{1,0:T(8,128)(2,1)S(1)}, u32[]{:S(2)}, u32[]{:S(2)}) collective-permute-start(bf16[112,128]{1,0:T(8,128)(2,1)S(1)} %get-tuple-element.36), channel_id=1, source_target_pairs={{0,16},{1,17},{2,18},{3,19},{4,20},{5,21},{6,22},{7,23},{8,24},{9,... | collective-permute-start | bytes 86024 | tf_op jit(solution)/shard_map/ppermute | solution.py:54
  64.5 5.7 %collective-permute-start.13 = (bf16[112,128]{1,0:T(8,128)(2,1)S(1)}, bf16[112,128]{1,0:T(8,128)(2,1)S(1)}, u32[]{:S(2)}, u32[]{:S(2)}) collective-permute-start(bf16[112,128]{1,0:T(8,128)(2,1)S(1)} %fusion.8), channel_id=1, source_target_pairs={{0,24},{1,25},{2,26},{3,27},{4,28},{5,29},{6,30},{7,31},{8,16},{9,... | collective-permute-start | bytes 86024 | tf_op jit(solution)/shard_map/ppermute | solution.py:54
  65.7 5.2 %collective-permute-start.12 = (bf16[112,128]{1,0:T(8,128)(2,1)S(1)}, bf16[112,128]{1,0:T(8,128)(2,1)S(1)}, u32[]{:S(2)}, u32[]{:S(2)}) collective-permute-start(bf16[112,128]{1,0:T(8,128)(2,1)S(1)} %fusion.8), channel_id=1, source_target_pairs={{0,16},{1,17},{2,18},{3,19},{4,20},{5,21},{6,22},{7,23},{8,24},{9,... | collective-permute-start | bytes 86024 | tf_op jit(solution)/shard_map/ppermute | solution.py:54
  66.4 4.6 %collective-permute-start.11 = (bf16[112,128]{1,0:T(8,128)(2,1)S(1)}, bf16[112,128]{1,0:T(8,128)(2,1)S(1)}, u32[]{:S(2)}, u32[]{:S(2)}) collective-permute-start(bf16[112,128]{1,0:T(8,128)(2,1)S(1)} %fusion.8), channel_id=1, source_target_pairs={{0,8},{1,9},{2,10},{3,11},{4,12},{5,13},{6,14},{7,15},{8,0},{9,1},... | collective-permute-start | bytes 86024 | tf_op jit(solution)/shard_map/ppermute | solution.py:54
  71.1 5.9 %collective-permute-start.16 = (bf16[448,128]{1,0:T(8,128)(2,1)S(1)}, bf16[448,128]{1,0:T(8,128)(2,1)S(1)}, u32[]{:S(2)}, u32[]{:S(2)}) collective-permute-start(bf16[448,128]{1,0:T(8,128)(2,1)S(1)} %pad_maximum_fusion.refs_0_), channel_id=1, source_target_pairs={{0,6},{1,7},{2,4},{3,5},{4,2},{5,3},{6,0},{7,1},{8,14},{9,15},{10,... | collective-permute-start | bytes 344072 | tf_op jit(solution)/shard_map/ppermute | solution.py:54
  71.2 6.0 %collective-permute-start.15 = (bf16[448,128]{1,0:T(8,128)(2,1)S(1)}, bf16[448,128]{1,0:T(8,128)(2,1)S(1)}, u32[]{:S(2)}, u32[]{:S(2)}) collective-permute-start(bf16[448,128]{1,0:T(8,128)(2,1)S(1)} %pad_maximum_fusion.refs_0_), channel_id=1, source_target_pairs={{0,4},{1,5},{2,6},{3,7},{4,0},{5,1},{6,2},{7,3},{8,12},{9,13},{10,... | collective-permute-start | bytes 344072 | tf_op jit(solution)/shard_map/ppermute | solution.py:54
  72.8 4.8 %collective-permute-start.14 = (bf16[448,128]{1,0:T(8,128)(2,1)S(1)}, bf16[448,128]{1,0:T(8,128)(2,1)S(1)}, u32[]{:S(2)}, u32[]{:S(2)}) collective-permute-start(bf16[448,128]{1,0:T(8,128)(2,1)S(1)} %pad_maximum_fusion.refs_0_), channel_id=1, source_target_pairs={{0,2},{1,3},{2,0},{3,1},{4,6},{5,7},{6,4},{7,5},{8,10},{9,11},{10,... | collective-permute-start | bytes 344072 | tf_op jit(solution)/shard_map/ppermute | solution.py:54
  74.6 3.2 %collective-permute-start.17 = (bf16[448,128]{1,0:T(8,128)(2,1)S(1)}, bf16[448,128]{1,0:T(8,128)(2,1)S(1)}, u32[]{:S(2)}, u32[]{:S(2)}) collective-permute-start(bf16[448,128]{1,0:T(8,128)(2,1)S(1)} %pad_maximum_fusion.refs_0_), channel_id=1, source_target_pairs={{0,1},{1,0},{2,3},{3,2},{4,5},{5,4},{6,7},{7,6},{8,9},{9,8},{10,11... | collective-permute-start | bytes 344072 | tf_op jit(solution)/shard_map/ppermute | solution.py:54
  76.9 1.3 %collective-permute-start.20 = (bf16[448,128]{1,0:T(8,128)(2,1)S(1)}, bf16[448,128]{1,0:T(8,128)(2,1)S(1)}, u32[]{:S(2)}, u32[]{:S(2)}) collective-permute-start(bf16[448,128]{1,0:T(8,128)(2,1)S(1)} %collective-permute-done.16.refs_3_), channel_id=1, source_target_pairs={{0,1},{1,0},{2,3},{3,2},{4,5},{5,4},{6,7},{7,6},{8,9},{9,8},{10,11... | collective-permute-start | bytes 344072 | tf_op jit(solution)/shard_map/ppermute | solution.py:54
  77.2 1.3 %collective-permute-start.19 = (bf16[448,128]{1,0:T(8,128)(2,1)S(1)}, bf16[448,128]{1,0:T(8,128)(2,1)S(1)}, u32[]{:S(2)}, u32[]{:S(2)}) collective-permute-start(bf16[448,128]{1,0:T(8,128)(2,1)S(1)} %collective-permute-done.15.refs_2_), channel_id=1, source_target_pairs={{0,1},{1,0},{2,3},{3,2},{4,5},{5,4},{6,7},{7,6},{8,9},{9,8},{10,11... | collective-permute-start | bytes 344072 | tf_op jit(solution)/shard_map/ppermute | solution.py:54
  77.6 1.3 %collective-permute-start.18 = (bf16[448,128]{1,0:T(8,128)(2,1)S(1)}, bf16[448,128]{1,0:T(8,128)(2,1)S(1)}, u32[]{:S(2)}, u32[]{:S(2)}) collective-permute-start(bf16[448,128]{1,0:T(8,128)(2,1)S(1)} %collective-permute-done.14.refs_1_), channel_id=1, source_target_pairs={{0,1},{1,0},{2,3},{3,2},{4,5},{5,4},{6,7},{7,6},{8,9},{9,8},{10,11... | collective-permute-start | bytes 344072 | tf_op jit(solution)/shard_map/ppermute | solution.py:54

commit v4 on v3

--- a/solution.py
+++ b/solution.py
@@ -59,25 +59,6 @@
     for k, (axis, bit) in enumerate(group):
         place = place | (((lax.axis_index(axis) >> bit) & 1) << k)
     return place
-
-
-def part_of(parts, index):
-    return lax.dynamic_index_in_dim(parts, index, 0, False)
-
-
-def exchange_sum(total, group, ahead=None):
-    count = 1 << len(group)
-    me = place_in(group)
-    parts = total.reshape(count, -1, C)
-    arrived = [
-        swap_with(part_of(parts, me ^ p).astype(BF16), group, p) for p in range(1, count)
-    ]
-    total = part_of(parts, me)
-    if ahead is not None:
-        arrived = ahead(arrived)
-    for piece in arrived:
-        total = total + piece.astype(F32)
-    return total
 
 
 def neighbours(up, down, axis):
@@ -136,7 +117,7 @@
         in_specs=[ANY, ANY, ANY],
         out_specs=(VMEM,) * 4,
         scratch_shapes=[pltpu.SMEM((NB,), jnp.int32), pltpu.SemaphoreType.DMA((1 + 8 * NB,))],
-        compiler_params=small(4),
+        compiler_params=pltpu.CompilerParams(vmem_limit_bytes=67043328),
         name="pack_z",
     )(sites, x, g)
 
@@ -182,6 +163,17 @@
     return inside // BX, pl.multiple_of(inside % BX * 8 + 8, 8)
 
 
+def read_codes(sites, zl_ref, zh_ref, yl_ref, yh_ref):
+    rows = [zl_ref[Z_ROWS - 1], zh_ref[Z_ROWS - 1]]
+    rows += [ref[Y_ROWS - 3 + k] for ref in (yl_ref, yh_ref) for k in range(3)]
+    codes = {(0, s): sites[s] for s in range(NB)}
+    for k, row in enumerate(rows):
+        row = row.astype(F32)
+        for s in range(NB):
+            codes[k + 1, s] = SITES - row[0, s].astype(jnp.int32)
+    return codes
+
+
 def fill(vol, codes, x_ref, zl_ref, zh_ref, yl_ref, yh_ref):
     def put(z0, y0, x0, rows):
         vol[z0 : z0 + rows.shape[0], pl.ds(y0, rows.shape[1]), pl.ds(x0, 8)] = rows.astype(F32)
@@ -250,16 +242,11 @@
     return total
 
 
-def forward_kernel(codes, core, x_hbm, g_hbm, zl_ref, zh_ref, yl_ref, yh_ref, w_hbm,
-                   act_ref, dpre_ref, keep_ref, send_ref, vol, stack, turned, x_ref, g_ref, w_ref, sems):
-    copies = [
-        pltpu.make_async_copy(src, dst, sems.at[k])
-        for k, (src, dst) in enumerate(((x_hbm, x_ref), (w_hbm, w_ref), (g_hbm, g_ref)))
-    ]
-    for copy in copies:
-        copy.start()
+def forward_kernel(sites, x_ref, g_ref, zl_ref, zh_ref, yl_ref, yh_ref, w_ref,
+                   act_ref, dpre_ref, keep_ref, send_ref, vol, stack, turned, split):
+    codes = read_codes(sites, zl_ref, zh_ref, yl_ref, yh_ref)
+    core = lax.axis_index("gy") & 1
     clear(vol)
-    copies[0].wait()
     fill(vol, codes, x_ref, zl_ref, zh_ref, yl_ref, yh_ref)
     places = [place_of(codes[0, s]) for s in range(NB)]
     stack_x(vol, stack, 0, 1, [1 + 8 * py for py, _ in places], [px for _, px in places], 10, 10)
@@ -268,8 +255,6 @@
         return dot(view, w_ref[3 * k : 3 * k + 3].reshape(3 * C, C))
 
     used = [codes[0, s] < SITES for s in range(NB)]
-    copies[1].wait()
-    copies[2].wait()
     for half in range(2):
         pre = convolve(stack, 40 * half, 10, 4, 8, weight)
         sig = 1.0 / (1.0 + jnp.exp(-pre))
@@ -296,27 +281,15 @@
             t = 3 * k + dx
             value = term[:, C * dx : C * dx + C].T
             half, at = divmod(t, HALF)
-
-            @pl.when(core[0] == half)
-            def _(value=value, at=at):
-                keep_ref[at] = value
-
-            @pl.when(core[0] != half)
-            def _(value=value, at=at):
-                send_ref[at] = value.astype(BF16)
+            split[(half ^ core) * HALF + at] = value
     for t in range(TAPS, 2 * HALF):
         half, at = divmod(t, HALF)
-
-        @pl.when(core[0] == half)
-        def _(at=at):
-            keep_ref[at] = jnp.zeros((C, C), F32)
-
-        @pl.when(core[0] != half)
-        def _(at=at):
-            send_ref[at] = jnp.zeros((C, C), BF16)
-
-
-def forward(codes, core, x, g, zl, zh, yl, yh, w):
+        split[(half ^ core) * HALF + at] = jnp.zeros((C, C), F32)
+    keep_ref[...] = split[:HALF]
+    send_ref[...] = split[HALF:].astype(BF16)
+
+
+def forward(sites, x, g, zl, zh, yl, yh, w):
     rows = jax.ShapeDtypeStruct((NB, 64, 8, C), BF16)
     return pl.pallas_call(
         forward_kernel,
@@ -326,34 +299,24 @@
             jax.ShapeDtypeStruct((HALF, C, C), F32),
             jax.ShapeDtypeStruct((HALF, C, C), BF16),
         ),
-        in_specs=[SMEM, SMEM, ANY, ANY] + [VMEM] * 4 + [ANY],
+        in_specs=[SMEM] + [VMEM] * 7,
         out_specs=(VMEM,) * 4,
         scratch_shapes=[
             pltpu.VMEM((VZ, VY, VX, C), F32),
             pltpu.VMEM((100, 16, 3 * C), BF16),
             pltpu.VMEM((C, 1024), BF16),
-            pltpu.VMEM((NB, 8, 8, 8, C), BF16),
-            pltpu.VMEM((NB, 8, 8, 8, C), BF16),
-            pltpu.VMEM((TAPS, C, C), BF16),
-            pltpu.SemaphoreType.DMA((3,)),
+            pltpu.VMEM((2 * HALF, C, C), F32),
         ],
-        compiler_params=small(24),
+        compiler_params=small(18),
         cost_estimate=pl.CostEstimate(flops=2 * 10**9, bytes_accessed=5 << 20, transcendentals=1 << 17),
         name="forward",
-    )(codes, core, x, g, zl, zh, yl, yh, w)
-
-
-def backward_kernel(codes, x_hbm, dpre_ref, zl_ref, zh_ref, yl_ref, yh_ref, w_hbm,
-                    grad_ref, vol, stack, x_ref, w_ref, sems):
-    copies = [
-        pltpu.make_async_copy(src, dst, sems.at[k])
-        for k, (src, dst) in enumerate(((x_hbm, x_ref), (w_hbm, w_ref)))
-    ]
-    for copy in copies:
-        copy.start()
+    )(sites, x, g, zl, zh, yl, yh, w)
+
+
+def backward_kernel(sites, x_ref, dpre_ref, zl_ref, zh_ref, yl_ref, yh_ref, w_ref,
+                    grad_ref, vol, stack):
+    codes = read_codes(sites, zl_ref, zh_ref, yl_ref, yh_ref)
     clear(vol)
-    for copy in copies:
-        copy.wait()
     fill(vol, codes, x_ref, zl_ref, zh_ref, yl_ref, yh_ref)
 
     def weight(k, view):
@@ -436,27 +399,70 @@
             grad_ref[s, 32 * half : 32 * half + 32] = value.astype(BF16)
 
 
-def backward(codes, x, dpre, zl, zh, yl, yh, w):
+def backward(sites, x, dpre, zl, zh, yl, yh, w):
     return pl.pallas_call(
         backward_kernel,
         out_shape=jax.ShapeDtypeStruct((NB, 64, 8, C), BF16),
-        in_specs=[SMEM, ANY] + [VMEM] * 5 + [ANY],
+        in_specs=[SMEM] + [VMEM] * 7,
         out_specs=VMEM,
         scratch_shapes=[
             pltpu.VMEM((VZ, VY, VX, C), F32),
             pltpu.VMEM((160, 16, 3 * C), BF16),
-            pltpu.VMEM((NB, 8, 8, 8, C), BF16),
-            pltpu.VMEM((TAPS, C, C), BF16),
-            pltpu.SemaphoreType.DMA((2,)),
         ],
-        compiler_params=small(24),
+        compiler_params=small(18),
         cost_estimate=pl.CostEstimate(flops=10**9, bytes_accessed=5 << 20, transcendentals=1 << 16),
         name="backward",
-    )(codes, x, dpre, zl, zh, yl, yh, w)
-
-
-def finish_kernel(first, share, sizes, me, *refs):
+    )(sites, x, dpre, zl, zh, yl, yh, w)
+
+
+def merge_kernel(group, scale, count, *refs):
+    terms, outs = refs[:count], refs[count:]
+    rows = outs[0].shape[0]
+    me = place_in(group) if group else 0
+    for p, out in enumerate(outs):
+        at = pl.multiple_of((me ^ p) * rows, 16) if group else 0
+        value = terms[0][pl.ds(at, rows)]
+        for term in terms[1:]:
+            value = value + term[pl.ds(at, rows)].astype(F32)
+        out[...] = value if group and p == 0 else (value * scale).astype(BF16)
+
+
+def merge(keep, arrived, group=None, scale=1.0):
+    members = 1 << len(group) if group else 1
+    shape = (keep.shape[0] // members, C)
+    kinds = [F32] + [BF16] * (members - 1) if group else [BF16]
+    return pl.pallas_call(
+        functools.partial(merge_kernel, group, scale, 1 + len(arrived)),
+        out_shape=tuple(jax.ShapeDtypeStruct(shape, kind) for kind in kinds),
+        in_specs=[VMEM] * (1 + len(arrived)),
+        out_specs=(VMEM,) * members,
+        compiler_params=small(6),
+        name="merge",
+    )(keep, *arrived)
+
+
+def join_kernel(*refs):
+    out = refs[-1]
+    for k, ref in enumerate(refs[:-1]):
+        out[k * ref.shape[0] : (k + 1) * ref.shape[0]] = ref[...]
+
+
+def join(pieces):
+    rows = sum(p.shape[0] for p in pieces)
+    return pl.pallas_call(
+        join_kernel,
+        out_shape=jax.ShapeDtypeStruct((rows, C), BF16),
+        in_specs=[VMEM] * len(pieces),
+        out_specs=VMEM,
+        compiler_params=small(4),
+        name="join",
+    )(*pieces)
+
+
+def finish_kernel(first, share, plan, *refs):
     pieces, out = refs[:-1], refs[-1]
+    me = [place_in(group) for group in plan]
+    sizes = [1 << len(group) for group in plan]
     middle, inner_sizes = sizes[1], sizes[2:]
     inner = 1
     for n in inner_sizes:
@@ -487,16 +493,14 @@
 
 
 def finish(first, share, plan, pieces):
-    sizes = [1 << len(group) for group in plan]
-    me = jnp.stack([place_in(group) for group in plan])
-    return pl.pallas_call(
-        functools.partial(finish_kernel, first, share, sizes),
+    return pl.pallas_call(
+        functools.partial(finish_kernel, first, share, plan),
         out_shape=jax.ShapeDtypeStruct((TAPS * C, C), F32),
-        in_specs=[SMEM] + [VMEM] * len(pieces),
+        in_specs=[VMEM] * len(pieces),
         out_specs=VMEM,
         compiler_params=small(8),
         name="finish",
-    )(me, *pieces)
+    )(*pieces)
 
 
 def local(features, brick_sites, kernel, cotangent):
@@ -508,13 +512,7 @@
     zl, zh = neighbours(z_up, z_down, "gz")
     y_up, y_down = pack_y(own_up, own_down, z_up, zl, zh)
     yl, yh = neighbours(y_up, y_down, "gy")
-    codes = jnp.concatenate(
-        [sites[None]]
-        + [SITES - m[rows:, 0, :NB].astype(jnp.int32)
-           for m, rows in ((zl, Z_ROWS - 1), (zh, Z_ROWS - 1), (yl, Y_ROWS - 3), (yh, Y_ROWS - 3))]
-    )
-    core = (lax.axis_index("gy") & 1).reshape(1).astype(jnp.int32)
-    act, dpre, keep, send = forward(codes, core, x, g, zl, zh, yl, yh, kernel)
+    act, dpre, keep, send = forward(sites, x, g, zl, zh, yl, yh, kernel)
 
     plan = exchange_plan()
     first = HALF * C
@@ -522,26 +520,23 @@
     share = -(-first // (16 * sharers)) * 16
     half_rows = share * sharers
     arrived = swap_with(send, plan[0], 1)
-    total = (keep + arrived.astype(F32)).reshape(first, C)
-    total = jnp.pad(total, ((0, half_rows - first), (0, 0)))
-    done = []
-
-    def ahead(arrived):
-        grad = backward(codes, x, dpre, zl, zh, yl, yh, kernel)
-        tied = lax.optimization_barrier(tuple(arrived) + (grad,))
-        done.append(tied[-1])
-        return tied[:-1]
-
-    for level, group in enumerate(plan[1:]):
-        total = exchange_sum(total, group, ahead if level == 0 else None)
-    scale = 1.0 / (NB * VOX * devices) ** 0.5
-    piece = (total * scale).astype(BF16)
-    grad_in = done[0]
+    pad = ((0, half_rows - first), (0, 0))
+    keep = jnp.pad(keep.reshape(first, C), pad)
+    arrived = jnp.pad(arrived.reshape(first, C), pad)
+    grad_in = None
+    arrived = [arrived]
+    for group in plan[1:]:
+        keep, *sends = merge(keep, arrived, group)
+        arrived = [swap_with(send, group, 1 + k) for k, send in enumerate(sends)]
+        if grad_in is None:
+            grad_in = backward(sites, x, dpre, zl, zh, yl, yh, kernel)
+            *arrived, grad_in = lax.optimization_barrier((*arrived, grad_in))
+    (piece,) = merge(keep, arrived, scale=1.0 / (NB * VOX * devices) ** 0.5)
 
     pieces = [piece]
     for level, group in enumerate(reversed(plan[1:])):
         if level > 0:
-            pieces = [jnp.concatenate(pieces)]
+            pieces = [join(pieces)]
         pieces = [pieces[0]] + [swap_with(pieces[0], group, p) for p in range(1, 1 << len(group))]
     others = [swap_with(p, plan[0], 1) for p in pieces]
     grad_kernel = finish(first, share, plan, pieces + others)

time: 81.7 us -> 74.3 us (0.909)
  Pallas kernels: 19.9 us -> 15.3 us
  other arithmetic: 2.23 us -> 0 us
  local copies, waits for them, and re-layouts: 7.74 us -> 6.41 us
    pallas_call x1, Pallas kernels: 9.72 us -> 5.03 us  [forward(): pl.pallas_call(forward_kernel, out_shape=(rows, jax.ShapeDtypeStruct((64,...]
    add x2 -> x0, other arithmetic: 2.1 us -> none  [the longest x1 1.1 us: local(): total = (keep + arrived.astype(F32)).reshape(first, C)]
    pallas_call x1, Pallas kernels: 0.72 us -> 1.87 us  [pack_z(): pl.pallas_call(pack_z_kernel, out_shape=(shape, shape, beside, beside), i...]
    pallas_call x1 -> x5, Pallas kernels: 2.46 us -> 1.98 us  [the longest x1 1.79 us: finish(): pl.pallas_call(functools.partial(finish_kernel, first, share, plan), out_...]
  transfers between devices with their start and end apart: 21 -> 21, of which waited for: 15 -> 14; matrix products, arithmetic and copies ran while one was open for 0% -> 0% of each run, Pallas kernels for 9% -> 9%
where the time goes in v4:
time: 74.3 us; the launch traced here: 73.8 us
  starting transfers between devices  32 us (43%)
  waiting for transfers between devices  19.4 us (26%)
  Pallas kernels  15.3 us (21%)
  local copies, waits for them, and re-layouts  6.41 us (9%)
    ppermute x17, starting transfers between devices, swap_with(): return lax.ppermute(value, AXES, pairs)  21.9 us
    ppermute x17, waiting for transfers between devices, swap_with(): return lax.ppermute(value, AXES, pairs)  12.8 us
    ppermute x4, starting transfers between devices, neighbours(): return (lax.ppermute(up, axis, forward), lax.ppermute(down, axis, backward))  10 us
    ppermute x4, waiting for transfers between devices, neighbours(): return (lax.ppermute(up, axis, forward), lax.ppermute(down, axis, backward))  6.61 us
    unnamed x18, local copies, waits for them, and re-layouts  6.41 us
    pallas_call x1, Pallas kernels, backward(): pl.pallas_call(backward_kernel, out_shape=jax.ShapeDtypeStruct((NB, 64, 8...  6.37 us
    pallas_call x1, Pallas kernels, forward(): pl.pallas_call(forward_kernel, out_shape=(rows, jax.ShapeDtypeStruct((64,...  5.03 us
    pallas_call x1, Pallas kernels, pack_z(): pl.pallas_call(pack_z_kernel, out_shape=(shape, shape, beside, beside), i...  1.87 us
  transfers between devices with their start and end apart: 21, of which 14 were waited for; matrix products, arithmetic and copies ran while one was open for 0% of the time, Pallas kernels for 9%

profile of v4, /device:TPU:0, one launch (start us, length us, event | category | flops | bytes accessed | tf_op | source)
XLA Modules:
  0.0 73.8 jit_solution(4393291719999529318)
XLA Ops:
  0.6 1.9 %pack_z.1 = (bf16[49,8,128]{2,1,0:T(8,128)(2,1)}, bf16[49,8,128]{2,1,0:T(8,128)(2,1)}, bf16[48,8,128]{2,1,0:T(8,128)(2,1)}, bf16[48,8,128]{2,1,0:T(8,128)(2,1)}) custom-call(s32[2]{0:T(128)} %bitcast.15, bf16[2,8,8,8,128]{4,3,2,1,0:T(8,128)(2,1)} %bitcast.12, bf16[2,8,8,8,128]{4,3,2,1,0:T(8,128)(2,1)} %bitcast.10), custom_call_target="tpu_custom_call" | custom-call | tf_op jit(solution)/shard_map/pack_z/pallas_call | solution.py:114
  2.5 1.3 %collective-permute-start.1 = (bf16[49,8,128]{2,1,0:T(8,128)(2,1)}, bf16[49,8,128]{2,1,0:T(8,128)(2,1)S(1)}, u32[]{:S(2)}, u32[]{:S(2)}) collective-permute-start(bf16[49,8,128]{2,1,0:T(8,128)(2,1)} %get-tuple-element.26), channel_id=1, source_target_pairs={{4,0},{8,4},{12,8},{16,12},{20,16},{24,20},{28,24},{5,1},{9,5},{13... | collective-permute-start | bytes 301064 | tf_op jit(solution)/shard_map/ppermute | solution.py:68
  3.8 5.5 %collective-permute-start = (bf16[49,8,128]{2,1,0:T(8,128)(2,1)}, bf16[49,8,128]{2,1,0:T(8,128)(2,1)S(1)}, u32[]{:S(2)}, u32[]{:S(2)}) collective-permute-start(bf16[49,8,128]{2,1,0:T(8,128)(2,1)} %get-tuple-element.25.mine_ref), channel_id=1, source_target_pairs={{0,4},{4,8},{8,12},{12,16},{16,20},{20,24},{24,28},{1,5},{5,9},{9,... | collective-permute-start | bytes 301064 | tf_op jit(solution)/shard_map/ppermute | solution.py:68
  9.4 1.1 %collective-permute-done.1.high_ref.zh_ref = bf16[49,8,128]{2,1,0:T(8,128)(2,1)S(1)} collective-permute-done((bf16[49,8,128]{2,1,0:T(8,128)(2,1)}, bf16[49,8,128]{2,1,0:T(8,128)(2,1)S(1)}, u32[]{:S(2)}, u32[]{:S(2)}) %collective-permute-start.1) | collective-permute-done | bytes 100384 | tf_op jit(solution)/shard_map/ppermute | solution.py:68
  10.5 2.4 %collective-permute-done.low_ref.zl_ref = bf16[49,8,128]{2,1,0:T(8,128)(2,1)S(1)} collective-permute-done((bf16[49,8,128]{2,1,0:T(8,128)(2,1)}, bf16[49,8,128]{2,1,0:T(8,128)(2,1)S(1)}, u32[]{:S(2)}, u32[]{:S(2)}) %collective-permute-start) | collective-permute-done | bytes 100384 | tf_op jit(solution)/shard_map/ppermute | solution.py:68
  12.9 0.9 %copy-done.2 = bf16[49,8,128]{2,1,0:T(8,128)(2,1)S(1)} copy-done((bf16[49,8,128]{2,1,0:T(8,128)(2,1)S(1)}, bf16[49,8,128]{2,1,0:T(8,128)(2,1)}, u32[]{:S(2)}) %copy-start.2) | copy-done | bytes 100376
  13.8 0.9 %copy-done.3 = bf16[48,8,128]{2,1,0:T(8,128)(2,1)S(1)} copy-done((bf16[48,8,128]{2,1,0:T(8,128)(2,1)S(1)}, bf16[48,8,128]{2,1,0:T(8,128)(2,1)}, u32[]{:S(2)}) %copy-start.3) | copy-done | bytes 98328
  14.7 0.9 %copy-done.4 = bf16[48,8,128]{2,1,0:T(8,128)(2,1)S(1)} copy-done((bf16[48,8,128]{2,1,0:T(8,128)(2,1)S(1)}, bf16[48,8,128]{2,1,0:T(8,128)(2,1)}, u32[]{:S(2)}) %copy-start.4) | copy-done | bytes 98328
  15.6 1.9 %collective-permute-start.2 = (bf16[71,8,128]{2,1,0:T(8,128)(2,1)S(1)}, bf16[71,8,128]{2,1,0:T(8,128)(2,1)S(1)}, u32[]{:S(2)}, u32[]{:S(2)}) collective-permute-start(bf16[71,8,128]{2,1,0:T(8,128)(2,1)S(1)} %get-tuple-element.29), channel_id=1, source_target_pairs={{0,1},{1,2},{2,3},{4,5},{5,6},{6,7},{8,9},{9,10},{10,11},{12,13},{... | collective-permute-start | bytes 436232 | tf_op jit(solution)/shard_map/ppermute | solution.py:68
  17.5 0.0 copy-start.6
  17.5 1.3 %collective-permute-start.3 = (bf16[71,8,128]{2,1,0:T(8,128)(2,1)S(1)}, bf16[71,8,128]{2,1,0:T(8,128)(2,1)S(1)}, u32[]{:S(2)}, u32[]{:S(2)}) collective-permute-start(bf16[71,8,128]{2,1,0:T(8,128)(2,1)S(1)} %get-tuple-element.30), channel_id=1, source_target_pairs={{1,0},{2,1},{3,2},{5,4},{6,5},{7,6},{9,8},{10,9},{11,10},{13,12},{... | collective-permute-start | bytes 436232 | tf_op jit(solution)/shard_map/ppermute | solution.py:68
  18.8 3.1 %collective-permute-done.3.yh_ref = bf16[71,8,128]{2,1,0:T(8,128)(2,1)S(1)} collective-permute-done((bf16[71,8,128]{2,1,0:T(8,128)(2,1)S(1)}, bf16[71,8,128]{2,1,0:T(8,128)(2,1)S(1)}, u32[]{:S(2)}, u32[]{:S(2)}) %collective-permute-start.3) | collective-permute-done | bytes 145440 | tf_op jit(solution)/shard_map/ppermute | solution.py:68
  21.9 0.9 %copy-done = bf16[1,1,2,512,128]{4,3,2,1,0:T(8,128)(2,1)S(1)} copy-done((bf16[1,1,2,512,128]{4,3,2,1,0:T(8,128)(2,1)S(1)}, bf16[1,1,2,512,128]{4,3,2,1,0:T(8,128)(2,1)}, u32[]{:S(2)}) %copy-start) | copy-done | bytes 262168
  22.9 0.9 %copy-done.1 = bf16[1,1,2,512,128]{4,3,2,1,0:T(8,128)(2,1)S(1)} copy-done((bf16[1,1,2,512,128]{4,3,2,1,0:T(8,128)(2,1)S(1)}, bf16[1,1,2,512,128]{4,3,2,1,0:T(8,128)(2,1)}, u32[]{:S(2)}) %copy-start.1) | copy-done | bytes 262168
  23.8 0.7 copy-done.5
  24.5 1.2 %copy-done.7 = bf16[27,128,128]{2,1,0:T(8,128)(2,1)S(1)} copy-done((bf16[27,128,128]{2,1,0:T(8,128)(2,1)S(1)}, bf16[27,128,128]{2,1,0:T(8,128)(2,1)}, u32[]{:S(2)}) %copy-start.7) | copy-done | bytes 884760
  25.7 5.0 %forward.1 = (bf16[2,64,8,128]{3,2,1,0:T(8,128)(2,1)}, bf16[64,16,128]{2,1,0:T(8,128)(2,1)S(1)}, f32[14,128,128]{2,1,0:T(8,128)S(1)}, bf16[14,128,128]{2,1,0:T(8,128)(2,1)S(1)}) custom-call(s32[2]{0:T(128)S(1)} %bitcast.16, bf16[2,8,8,8,128]{4,3,2,1,0:T(8,128)(2,1)S(1)} %bitcast.13, bf16[2,8,8,8,128]{4,3,2,1,0:T(8,128)(2,1)S(1)} %bitcast.11, ...), custom_call_target="tpu_custom_call" | custom-call | flops 2000000000 | bytes 5242880 | tf_op jit(solution)/shard_map/forward/pallas_call | solution.py:294
  30.7 3.7 %collective-permute-start.4 = (bf16[14,128,128]{2,1,0:T(8,128)(2,1)S(1)}, bf16[14,128,128]{2,1,0:T(8,128)(2,1)S(1)}, u32[]{:S(2)}, u32[]{:S(2)}) collective-permute-start(bf16[14,128,128]{2,1,0:T(8,128)(2,1)S(1)} %get-tuple-element.33), channel_id=1, source_target_pairs={{0,1},{1,0},{2,3},{3,2},{4,5},{5,4},{6,7},{7,6},{8,9},{9,8},{10,11... | collective-permute-start | bytes 1376264 | tf_op jit(solution)/shard_map/ppermute | solution.py:54
  34.4 1.4 %collective-permute-done.4 = bf16[14,128,128]{2,1,0:T(8,128)(2,1)S(1)} collective-permute-done((bf16[14,128,128]{2,1,0:T(8,128)(2,1)S(1)}, bf16[14,128,128]{2,1,0:T(8,128)(2,1)S(1)}, u32[]{:S(2)}, u32[]{:S(2)}) %collective-permute-start.4) | collective-permute-done | bytes 458784 | tf_op jit(solution)/shard_map/ppermute | solution.py:54
  35.9 0.1 merge.3
  36.0 0.2 collective-permute-start.5
  36.2 2.4 %collective-permute-start.6 = (bf16[448,128]{1,0:T(8,128)(2,1)S(1)}, bf16[448,128]{1,0:T(8,128)(2,1)S(1)}, u32[]{:S(2)}, u32[]{:S(2)}) collective-permute-start(bf16[448,128]{1,0:T(8,128)(2,1)S(1)} %get-tuple-element.35), channel_id=1, source_target_pairs={{0,4},{1,5},{2,6},{3,7},{4,0},{5,1},{6,2},{7,3},{8,12},{9,13},{10,... | collective-permute-start | bytes 344072 | tf_op jit(solution)/shard_map/ppermute | solution.py:54
  38.5 1.4 %collective-permute-start.7 = (bf16[448,128]{1,0:T(8,128)(2,1)S(1)}, bf16[448,128]{1,0:T(8,128)(2,1)S(1)}, u32[]{:S(2)}, u32[]{:S(2)}) collective-permute-start(bf16[448,128]{1,0:T(8,128)(2,1)S(1)} %get-tuple-element.36), channel_id=1, source_target_pairs={{0,6},{1,7},{2,4},{3,5},{4,2},{5,3},{6,0},{7,1},{8,14},{9,15},{10,... | collective-permute-start | bytes 344072 | tf_op jit(solution)/shard_map/ppermute | solution.py:54
  39.9 6.4 %backward.1 = bf16[2,64,8,128]{3,2,1,0:T(8,128)(2,1)} custom-call(s32[2]{0:T(128)S(1)} %bitcast.17, bf16[2,8,8,8,128]{4,3,2,1,0:T(8,128)(2,1)S(1)} %bitcast.14, bf16[64,16,128]{2,1,0:T(8,128)(2,1)S(1)} %get-tuple-element.37.dpre_ref, bf16[49,8,128]{2,1,0:T(8,128)(2,1)S(1)} %collective-permute-done.low_ref.zl_ref, ...), custom_call_target="tpu_custom_call" | custom-call | flops 1000000000 | bytes 5242880 | tf_op jit(solution)/shard_map/backward/pallas_call | solution.py:403
  46.3 0.0 collective-permute-done.5.refs_1_
  46.3 0.0 collective-permute-done.6.refs_2_
  46.3 0.1 merge.4
  46.4 3.3 %collective-permute-start.8 = (bf16[112,128]{1,0:T(8,128)(2,1)S(1)}, bf16[112,128]{1,0:T(8,128)(2,1)S(1)}, u32[]{:S(2)}, u32[]{:S(2)}) collective-permute-start(bf16[112,128]{1,0:T(8,128)(2,1)S(1)} %get-tuple-element.44), channel_id=1, source_target_pairs={{0,8},{1,9},{2,10},{3,11},{4,12},{5,13},{6,14},{7,15},{8,0},{9,1},... | collective-permute-start | bytes 86024 | tf_op jit(solution)/shard_map/ppermute | solution.py:54
  49.6 2.6 %collective-permute-start.9 = (bf16[112,128]{1,0:T(8,128)(2,1)S(1)}, bf16[112,128]{1,0:T(8,128)(2,1)S(1)}, u32[]{:S(2)}, u32[]{:S(2)}) collective-permute-start(bf16[112,128]{1,0:T(8,128)(2,1)S(1)} %get-tuple-element.45), channel_id=1, source_target_pairs={{0,16},{1,17},{2,18},{3,19},{4,20},{5,21},{6,22},{7,23},{8,24},{9,... | collective-permute-start | bytes 86024 | tf_op jit(solution)/shard_map/ppermute | solution.py:54
  52.2 2.4 %collective-permute-done.9.refs_2_ = bf16[112,128]{1,0:T(8,128)(2,1)S(1)} collective-permute-done((bf16[112,128]{1,0:T(8,128)(2,1)S(1)}, bf16[112,128]{1,0:T(8,128)(2,1)S(1)}, u32[]{:S(2)}, u32[]{:S(2)}) %collective-permute-start.9) | collective-permute-done | bytes 28704 | tf_op jit(solution)/shard_map/ppermute | solution.py:54
  54.6 3.3 %collective-permute-done.10.refs_3_ = bf16[112,128]{1,0:T(8,128)(2,1)S(1)} collective-permute-done((bf16[112,128]{1,0:T(8,128)(2,1)S(1)}, bf16[112,128]{1,0:T(8,128)(2,1)S(1)}, u32[]{:S(2)}, u32[]{:S(2)}) %collective-permute-start.10) | collective-permute-done | bytes 28704 | tf_op jit(solution)/shard_map/ppermute | solution.py:54
  57.9 0.4 collective-permute-start.13
  58.3 0.0 collective-permute-start.12
  58.3 4.0 %collective-permute-start.11 = (bf16[112,128]{1,0:T(8,128)(2,1)S(1)}, bf16[112,128]{1,0:T(8,128)(2,1)S(1)}, u32[]{:S(2)}, u32[]{:S(2)}) collective-permute-start(bf16[112,128]{1,0:T(8,128)(2,1)S(1)} %merge.5.refs_0_), channel_id=1, source_target_pairs={{0,8},{1,9},{2,10},{3,11},{4,12},{5,13},{6,14},{7,15},{8,0},{9,1},... | collective-permute-start | bytes 86024 | tf_op jit(solution)/shard_map/ppermute | solution.py:54
  62.3 1.3 %collective-permute-done.13.refs_3_ = bf16[112,128]{1,0:T(8,128)(2,1)S(1)} collective-permute-done((bf16[112,128]{1,0:T(8,128)(2,1)S(1)}, bf16[112,128]{1,0:T(8,128)(2,1)S(1)}, u32[]{:S(2)}, u32[]{:S(2)}) %collective-permute-start.13) | collective-permute-done | bytes 28704 | tf_op jit(solution)/shard_map/ppermute | solution.py:54
  63.6 0.6 collective-permute-done.11.refs_1_
  64.2 0.1 collective-permute-start.16
  64.3 1.6 %collective-permute-start.15 = (bf16[448,128]{1,0:T(8,128)(2,1)S(1)}, bf16[448,128]{1,0:T(8,128)(2,1)S(1)}, u32[]{:S(2)}, u32[]{:S(2)}) collective-permute-start(bf16[448,128]{1,0:T(8,128)(2,1)S(1)} %join.1.refs_0_), channel_id=1, source_target_pairs={{0,4},{1,5},{2,6},{3,7},{4,0},{5,1},{6,2},{7,3},{8,12},{9,13},{10,... | collective-permute-start | bytes 344072 | tf_op jit(solution)/shard_map/ppermute | solution.py:54
  65.9 1.9 %collective-permute-start.14 = (bf16[448,128]{1,0:T(8,128)(2,1)S(1)}, bf16[448,128]{1,0:T(8,128)(2,1)S(1)}, u32[]{:S(2)}, u32[]{:S(2)}) collective-permute-start(bf16[448,128]{1,0:T(8,128)(2,1)S(1)} %join.1.refs_0_), channel_id=1, source_target_pairs={{0,2},{1,3},{2,0},{3,1},{4,6},{5,7},{6,4},{7,5},{8,10},{9,11},{10,... | collective-permute-start | bytes 344072 | tf_op jit(solution)/shard_map/ppermute | solution.py:54
  67.8 2.3 %collective-permute-done.16.refs_3_ = bf16[448,128]{1,0:T(8,128)(2,1)S(1)} collective-permute-done((bf16[448,128]{1,0:T(8,128)(2,1)S(1)}, bf16[448,128]{1,0:T(8,128)(2,1)S(1)}, u32[]{:S(2)}, u32[]{:S(2)}) %collective-permute-start.16) | collective-permute-done | bytes 114720 | tf_op jit(solution)/shard_map/ppermute | solution.py:54
  70.1 0.3 collective-permute-done.15.refs_2_
  70.4 0.2 collective-permute-start.19
  70.6 0.1 collective-permute-done.14.refs_1_
  70.7 0.2 collective-permute-start.18
  70.9 0.5 collective-permute-done.20.refs_7_
  71.4 0.3 collective-permute-done.19.refs_6_
  71.7 0.3 collective-permute-done.18.refs_5_
  72.0 1.8 %finish.1 = f32[3456,128]{1,0:T(8,128)} custom-call(bf16[448,128]{1,0:T(8,128)(2,1)S(1)} %join.1.refs_0_, bf16[448,128]{1,0:T(8,128)(2,1)S(1)} %collective-permute-done.14.refs_1_, bf16[448,128]{1,0:T(8,128)(2,1)S(1)} %collective-permute-done.15.refs_2_, bf16[448,128]{1,0:T(8,128)(2,1)S(1)} %collective-permute-done.16.refs_3_, ...), custom_call_target="tpu_custom_call" | custom-call | tf_op jit(solution)/shard_map/finish/pallas_call | solution.py:496
  (21 shorter events, 0.1 us)
Async XLA Ops:
  2.5 7.9 %collective-permute-start.1 = (bf16[49,8,128]{2,1,0:T(8,128)(2,1)}, bf16[49,8,128]{2,1,0:T(8,128)(2,1)S(1)}, u32[]{:S(2)}, u32[]{:S(2)}) collective-permute-start(bf16[49,8,128]{2,1,0:T(8,128)(2,1)} %get-tuple-element.26), channel_id=1, source_target_pairs={{4,0},{8,4},{12,8},{16,12},{20,16},{24,20},{28,24},{5,1},{9,5},{13... | collective-permute-start | bytes 301064 | tf_op jit(solution)/shard_map/ppermute | solution.py:68
  3.8 9.1 %collective-permute-start = (bf16[49,8,128]{2,1,0:T(8,128)(2,1)}, bf16[49,8,128]{2,1,0:T(8,128)(2,1)S(1)}, u32[]{:S(2)}, u32[]{:S(2)}) collective-permute-start(bf16[49,8,128]{2,1,0:T(8,128)(2,1)} %get-tuple-element.25.mine_ref), channel_id=1, source_target_pairs={{0,4},{4,8},{8,12},{12,16},{16,20},{20,24},{24,28},{1,5},{5,9},{9,... | collective-permute-start | bytes 301064 | tf_op jit(solution)/shard_map/ppermute | solution.py:68
  12.9 0.9 %copy-start.2 = (bf16[49,8,128]{2,1,0:T(8,128)(2,1)S(1)}, bf16[49,8,128]{2,1,0:T(8,128)(2,1)}, u32[]{:S(2)}) copy-start(bf16[49,8,128]{2,1,0:T(8,128)(2,1)} %get-tuple-element.25.mine_ref) | copy-start | bytes 301060
  13.8 0.9 %copy-start.3 = (bf16[48,8,128]{2,1,0:T(8,128)(2,1)S(1)}, bf16[48,8,128]{2,1,0:T(8,128)(2,1)}, u32[]{:S(2)}) copy-start(bf16[48,8,128]{2,1,0:T(8,128)(2,1)} %get-tuple-element.27.own_up) | copy-start | bytes 294916
  14.6 0.9 %copy-start.4 = (bf16[48,8,128]{2,1,0:T(8,128)(2,1)S(1)}, bf16[48,8,128]{2,1,0:T(8,128)(2,1)}, u32[]{:S(2)}) copy-start(bf16[48,8,128]{2,1,0:T(8,128)(2,1)} %get-tuple-element.28.own_down) | copy-start | bytes 294916
  15.6 3.3 %collective-permute-start.2 = (bf16[71,8,128]{2,1,0:T(8,128)(2,1)S(1)}, bf16[71,8,128]{2,1,0:T(8,128)(2,1)S(1)}, u32[]{:S(2)}, u32[]{:S(2)}) collective-permute-start(bf16[71,8,128]{2,1,0:T(8,128)(2,1)S(1)} %get-tuple-element.29), channel_id=1, source_target_pairs={{0,1},{1,2},{2,3},{4,5},{5,6},{6,7},{8,9},{9,10},{10,11},{12,13},{... | collective-permute-start | bytes 436232 | tf_op jit(solution)/shard_map/ppermute | solution.py:68
  17.5 22.4 %copy-start.6 = (s32[1,1,2]{2,1,0:T(1,128)S(1)}, s32[1,1,2]{2,1,0:T(1,128)}, u32[]{:S(2)}) copy-start(s32[1,1,2]{2,1,0:T(1,128)} %param.5) | copy-start | bytes 28
  17.5 4.4 %collective-permute-start.3 = (bf16[71,8,128]{2,1,0:T(8,128)(2,1)S(1)}, bf16[71,8,128]{2,1,0:T(8,128)(2,1)S(1)}, u32[]{:S(2)}, u32[]{:S(2)}) collective-permute-start(bf16[71,8,128]{2,1,0:T(8,128)(2,1)S(1)} %get-tuple-element.30), channel_id=1, source_target_pairs={{1,0},{2,1},{3,2},{5,4},{6,5},{7,6},{9,8},{10,9},{11,10},{13,12},{... | collective-permute-start | bytes 436232 | tf_op jit(solution)/shard_map/ppermute | solution.py:68
  21.9 1.0 %copy-start = (bf16[1,1,2,512,128]{4,3,2,1,0:T(8,128)(2,1)S(1)}, bf16[1,1,2,512,128]{4,3,2,1,0:T(8,128)(2,1)}, u32[]{:S(2)}) copy-start(bf16[1,1,2,512,128]{4,3,2,1,0:T(8,128)(2,1)} %param.7) | copy-start | bytes 786436
  22.9 0.9 %copy-start.1 = (bf16[1,1,2,512,128]{4,3,2,1,0:T(8,128)(2,1)S(1)}, bf16[1,1,2,512,128]{4,3,2,1,0:T(8,128)(2,1)}, u32[]{:S(2)}) copy-start(bf16[1,1,2,512,128]{4,3,2,1,0:T(8,128)(2,1)} %param.4) | copy-start | bytes 786436
  23.8 0.7 copy-start.5
  24.5 1.2 %copy-start.7 = (bf16[27,128,128]{2,1,0:T(8,128)(2,1)S(1)}, bf16[27,128,128]{2,1,0:T(8,128)(2,1)}, u32[]{:S(2)}) copy-start(bf16[27,128,128]{2,1,0:T(8,128)(2,1)} %w_ref.3) | copy-start | bytes 2654212
  25.7 14.2 %copy-start.8 = (bf16[27,128,128]{2,1,0:T(8,128)(2,1)S(1)}, bf16[27,128,128]{2,1,0:T(8,128)(2,1)}, u32[]{:S(2)}) copy-start(bf16[27,128,128]{2,1,0:T(8,128)(2,1)} %w_ref.3) | copy-start | bytes 2654212
  30.7 5.2 %collective-permute-start.4 = (bf16[14,128,128]{2,1,0:T(8,128)(2,1)S(1)}, bf16[14,128,128]{2,1,0:T(8,128)(2,1)S(1)}, u32[]{:S(2)}, u32[]{:S(2)}) collective-permute-start(bf16[14,128,128]{2,1,0:T(8,128)(2,1)S(1)} %get-tuple-element.33), channel_id=1, source_target_pairs={{0,1},{1,0},{2,3},{3,2},{4,5},{5,4},{6,7},{7,6},{8,9},{9,8},{10,11... | collective-permute-start | bytes 1376264 | tf_op jit(solution)/shard_map/ppermute | solution.py:54
  36.0 10.3 %collective-permute-start.5 = (bf16[448,128]{1,0:T(8,128)(2,1)S(1)}, bf16[448,128]{1,0:T(8,128)(2,1)S(1)}, u32[]{:S(2)}, u32[]{:S(2)}) collective-permute-start(bf16[448,128]{1,0:T(8,128)(2,1)S(1)} %get-tuple-element.34), channel_id=1, source_target_pairs={{0,2},{1,3},{2,0},{3,1},{4,6},{5,7},{6,4},{7,5},{8,10},{9,11},{10,... | collective-permute-start | bytes 344072 | tf_op jit(solution)/shard_map/ppermute | solution.py:54
  36.2 10.1 %collective-permute-start.6 = (bf16[448,128]{1,0:T(8,128)(2,1)S(1)}, bf16[448,128]{1,0:T(8,128)(2,1)S(1)}, u32[]{:S(2)}, u32[]{:S(2)}) collective-permute-start(bf16[448,128]{1,0:T(8,128)(2,1)S(1)} %get-tuple-element.35), channel_id=1, source_target_pairs={{0,4},{1,5},{2,6},{3,7},{4,0},{5,1},{6,2},{7,3},{8,12},{9,13},{10,... | collective-permute-start | bytes 344072 | tf_op jit(solution)/shard_map/ppermute | solution.py:54
  38.5 7.7 %collective-permute-start.7 = (bf16[448,128]{1,0:T(8,128)(2,1)S(1)}, bf16[448,128]{1,0:T(8,128)(2,1)S(1)}, u32[]{:S(2)}, u32[]{:S(2)}) collective-permute-start(bf16[448,128]{1,0:T(8,128)(2,1)S(1)} %get-tuple-element.36), channel_id=1, source_target_pairs={{0,6},{1,7},{2,4},{3,5},{4,2},{5,3},{6,0},{7,1},{8,14},{9,15},{10,... | collective-permute-start | bytes 344072 | tf_op jit(solution)/shard_map/ppermute | solution.py:54
  46.4 5.9 %collective-permute-start.8 = (bf16[112,128]{1,0:T(8,128)(2,1)S(1)}, bf16[112,128]{1,0:T(8,128)(2,1)S(1)}, u32[]{:S(2)}, u32[]{:S(2)}) collective-permute-start(bf16[112,128]{1,0:T(8,128)(2,1)S(1)} %get-tuple-element.44), channel_id=1, source_target_pairs={{0,8},{1,9},{2,10},{3,11},{4,12},{5,13},{6,14},{7,15},{8,0},{9,1},... | collective-permute-start | bytes 86024 | tf_op jit(solution)/shard_map/ppermute | solution.py:54
  49.6 5.0 %collective-permute-start.9 = (bf16[112,128]{1,0:T(8,128)(2,1)S(1)}, bf16[112,128]{1,0:T(8,128)(2,1)S(1)}, u32[]{:S(2)}, u32[]{:S(2)}) collective-permute-start(bf16[112,128]{1,0:T(8,128)(2,1)S(1)} %get-tuple-element.45), channel_id=1, source_target_pairs={{0,16},{1,17},{2,18},{3,19},{4,20},{5,21},{6,22},{7,23},{8,24},{9,... | collective-permute-start | bytes 86024 | tf_op jit(solution)/shard_map/ppermute | solution.py:54
  52.2 5.7 %collective-permute-start.10 = (bf16[112,128]{1,0:T(8,128)(2,1)S(1)}, bf16[112,128]{1,0:T(8,128)(2,1)S(1)}, u32[]{:S(2)}, u32[]{:S(2)}) collective-permute-start(bf16[112,128]{1,0:T(8,128)(2,1)S(1)} %get-tuple-element.46), channel_id=1, source_target_pairs={{0,24},{1,25},{2,26},{3,27},{4,28},{5,29},{6,30},{7,31},{8,16},{9,... | collective-permute-start | bytes 86024 | tf_op jit(solution)/shard_map/ppermute | solution.py:54
  57.9 5.7 %collective-permute-start.13 = (bf16[112,128]{1,0:T(8,128)(2,1)S(1)}, bf16[112,128]{1,0:T(8,128)(2,1)S(1)}, u32[]{:S(2)}, u32[]{:S(2)}) collective-permute-start(bf16[112,128]{1,0:T(8,128)(2,1)S(1)} %merge.5.refs_0_), channel_id=1, source_target_pairs={{0,24},{1,25},{2,26},{3,27},{4,28},{5,29},{6,30},{7,31},{8,16},{9,... | collective-permute-start | bytes 86024 | tf_op jit(solution)/shard_map/ppermute | solution.py:54
  58.3 5.4 %collective-permute-start.12 = (bf16[112,128]{1,0:T(8,128)(2,1)S(1)}, bf16[112,128]{1,0:T(8,128)(2,1)S(1)}, u32[]{:S(2)}, u32[]{:S(2)}) collective-permute-start(bf16[112,128]{1,0:T(8,128)(2,1)S(1)} %merge.5.refs_0_), channel_id=1, source_target_pairs={{0,16},{1,17},{2,18},{3,19},{4,20},{5,21},{6,22},{7,23},{8,24},{9,... | collective-permute-start | bytes 86024 | tf_op jit(solution)/shard_map/ppermute | solution.py:54
  58.3 5.9 %collective-permute-start.11 = (bf16[112,128]{1,0:T(8,128)(2,1)S(1)}, bf16[112,128]{1,0:T(8,128)(2,1)S(1)}, u32[]{:S(2)}, u32[]{:S(2)}) collective-permute-start(bf16[112,128]{1,0:T(8,128)(2,1)S(1)} %merge.5.refs_0_), channel_id=1, source_target_pairs={{0,8},{1,9},{2,10},{3,11},{4,12},{5,13},{6,14},{7,15},{8,0},{9,1},... | collective-permute-start | bytes 86024 | tf_op jit(solution)/shard_map/ppermute | solution.py:54
  64.2 5.9 %collective-permute-start.16 = (bf16[448,128]{1,0:T(8,128)(2,1)S(1)}, bf16[448,128]{1,0:T(8,128)(2,1)S(1)}, u32[]{:S(2)}, u32[]{:S(2)}) collective-permute-start(bf16[448,128]{1,0:T(8,128)(2,1)S(1)} %join.1.refs_0_), channel_id=1, source_target_pairs={{0,6},{1,7},{2,4},{3,5},{4,2},{5,3},{6,0},{7,1},{8,14},{9,15},{10,... | collective-permute-start | bytes 344072 | tf_op jit(solution)/shard_map/ppermute | solution.py:54
  64.3 6.1 %collective-permute-start.15 = (bf16[448,128]{1,0:T(8,128)(2,1)S(1)}, bf16[448,128]{1,0:T(8,128)(2,1)S(1)}, u32[]{:S(2)}, u32[]{:S(2)}) collective-permute-start(bf16[448,128]{1,0:T(8,128)(2,1)S(1)} %join.1.refs_0_), channel_id=1, source_target_pairs={{0,4},{1,5},{2,6},{3,7},{4,0},{5,1},{6,2},{7,3},{8,12},{9,13},{10,... | collective-permute-start | bytes 344072 | tf_op jit(solution)/shard_map/ppermute | solution.py:54
  65.9 4.8 %collective-permute-start.14 = (bf16[448,128]{1,0:T(8,128)(2,1)S(1)}, bf16[448,128]{1,0:T(8,128)(2,1)S(1)}, u32[]{:S(2)}, u32[]{:S(2)}) collective-permute-start(bf16[448,128]{1,0:T(8,128)(2,1)S(1)} %join.1.refs_0_), channel_id=1, source_target_pairs={{0,2},{1,3},{2,0},{3,1},{4,6},{5,7},{6,4},{7,5},{8,10},{9,11},{10,... | collective-permute-start | bytes 344072 | tf_op jit(solution)/shard_map/ppermute | solution.py:54
  67.8 3.1 %collective-permute-start.17 = (bf16[448,128]{1,0:T(8,128)(2,1)S(1)}, bf16[448,128]{1,0:T(8,128)(2,1)S(1)}, u32[]{:S(2)}, u32[]{:S(2)}) collective-permute-start(bf16[448,128]{1,0:T(8,128)(2,1)S(1)} %join.1.refs_0_), channel_id=1, source_target_pairs={{0,1},{1,0},{2,3},{3,2},{4,5},{5,4},{6,7},{7,6},{8,9},{9,8},{10,11... | collective-permute-start | bytes 344072 | tf_op jit(solution)/shard_map/ppermute | solution.py:54
  70.1 1.3 %collective-permute-start.20 = (bf16[448,128]{1,0:T(8,128)(2,1)S(1)}, bf16[448,128]{1,0:T(8,128)(2,1)S(1)}, u32[]{:S(2)}, u32[]{:S(2)}) collective-permute-start(bf16[448,128]{1,0:T(8,128)(2,1)S(1)} %collective-permute-done.16.refs_3_), channel_id=1, source_target_pairs={{0,1},{1,0},{2,3},{3,2},{4,5},{5,4},{6,7},{7,6},{8,9},{9,8},{10,11... | collective-permute-start | bytes 344072 | tf_op jit(solution)/shard_map/ppermute | solution.py:54
  70.4 1.3 %collective-permute-start.19 = (bf16[448,128]{1,0:T(8,128)(2,1)S(1)}, bf16[448,128]{1,0:T(8,128)(2,1)S(1)}, u32[]{:S(2)}, u32[]{:S(2)}) collective-permute-start(bf16[448,128]{1,0:T(8,128)(2,1)S(1)} %collective-permute-done.15.refs_2_), channel_id=1, source_target_pairs={{0,1},{1,0},{2,3},{3,2},{4,5},{5,4},{6,7},{7,6},{8,9},{9,8},{10,11... | collective-permute-start | bytes 344072 | tf_op jit(solution)/shard_map/ppermute | solution.py:54
  70.7 1.3 %collective-permute-start.18 = (bf16[448,128]{1,0:T(8,128)(2,1)S(1)}, bf16[448,128]{1,0:T(8,128)(2,1)S(1)}, u32[]{:S(2)}, u32[]{:S(2)}) collective-permute-start(bf16[448,128]{1,0:T(8,128)(2,1)S(1)} %collective-permute-done.14.refs_1_), channel_id=1, source_target_pairs={{0,1},{1,0},{2,3},{3,2},{4,5},{5,4},{6,7},{7,6},{8,9},{9,8},{10,11... | collective-permute-start | bytes 344072 | tf_op jit(solution)/shard_map/ppermute | solution.py:54

commit v5 on v4

--- a/solution.py
+++ b/solution.py
@@ -72,7 +72,15 @@
 Y_ROWS = NB * 24 + 2 * NB * 5 + 3
 
 
-def pack_z_kernel(sites_ref, x_ref, g_ref, up_ref, down_ref, beside_up, beside_down, sites, sems):
+def code_row(sites):
+    lane = lax.broadcasted_iota(jnp.int32, (8, C), 1)
+    code = jnp.zeros((8, C), jnp.int32)
+    for s in range(NB):
+        code = jnp.where(lane == s, SITES - sites[s], code)
+    return code.astype(F32).astype(BF16)
+
+
+def pack_z_kernel(sites_ref, x_ref, g_ref, up_ref, down_ref, sites, sems):
     moves = [(sites_ref, sites)]
     for s in range(NB):
         base = 24 * s
@@ -82,10 +90,6 @@
             (g_ref.at[s, 7], up_ref.at[last]),
             (x_ref.at[s, 0:2], down_ref.at[first].reshape(2, 8, 8, C)),
             (g_ref.at[s, 0], down_ref.at[last]),
-            (x_ref.at[s, :, 6:8], beside_up.at[first].reshape(8, 2, 8, C)),
-            (g_ref.at[s, :, 7], beside_up.at[last]),
-            (x_ref.at[s, :, 0:2], beside_down.at[first].reshape(8, 2, 8, C)),
-            (g_ref.at[s, :, 0], beside_down.at[last]),
         ]
     copies = [
         pltpu.make_async_copy(src, dst, sems.at[k]) for k, (src, dst) in enumerate(moves)
@@ -93,11 +97,7 @@
     for copy in copies:
         copy.start()
     copies[0].wait()
-    lane = lax.broadcasted_iota(jnp.int32, (8, C), 1)
-    code = jnp.zeros((8, C), jnp.int32)
-    for s in range(NB):
-        code = jnp.where(lane == s, SITES - sites[s], code)
-    code = code.astype(F32).astype(BF16)
+    code = code_row(sites)
     up_ref[Z_ROWS - 1] = code
     down_ref[Z_ROWS - 1] = code
     for copy in copies[1:]:
@@ -110,16 +110,42 @@
 
 def pack_z(sites, x, g):
     shape = jax.ShapeDtypeStruct((Z_ROWS, 8, C), BF16)
-    beside = jax.ShapeDtypeStruct((NB * 24, 8, C), BF16)
     return pl.pallas_call(
         pack_z_kernel,
-        out_shape=(shape, shape, beside, beside),
+        out_shape=(shape, shape),
         in_specs=[ANY, ANY, ANY],
-        out_specs=(VMEM,) * 4,
-        scratch_shapes=[pltpu.SMEM((NB,), jnp.int32), pltpu.SemaphoreType.DMA((1 + 8 * NB,))],
+        out_specs=(VMEM,) * 2,
+        scratch_shapes=[pltpu.SMEM((NB,), jnp.int32), pltpu.SemaphoreType.DMA((1 + 4 * NB,))],
         compiler_params=pltpu.CompilerParams(vmem_limit_bytes=67043328),
         name="pack_z",
     )(sites, x, g)
+
+
+def stage_kernel(sites, x_ref, g_ref, w_ref, x_out, g_out, w_out, code_out, up_ref, down_ref):
+    x_out[...] = x_ref[...]
+    g_out[...] = g_ref[...]
+    w_out[...] = w_ref[...]
+    code_out[0] = code_row(sites)
+    for s in range(NB):
+        first, last = slice(24 * s, 24 * s + 16), slice(24 * s + 16, 24 * s + 24)
+        up_ref[first] = x_ref[s, :, 6:8].reshape(16, 8, C)
+        up_ref[last] = g_ref[s, :, 7]
+        down_ref[first] = x_ref[s, :, 0:2].reshape(16, 8, C)
+        down_ref[last] = g_ref[s, :, 0]
+
+
+def stage(sites, x, g, w):
+    beside = jax.ShapeDtypeStruct((NB * 24, 8, C), BF16)
+    code = jax.ShapeDtypeStruct((1, 8, C), BF16)
+    kept = tuple(jax.ShapeDtypeStruct(a.shape, a.dtype) for a in (x, g, w))
+    return pl.pallas_call(
+        stage_kernel,
+        out_shape=kept + (code, beside, beside),
+        in_specs=[SMEM, VMEM, VMEM, VMEM],
+        out_specs=(VMEM,) * 6,
+        compiler_params=small(4),
+        name="stage",
+    )(sites, x, g, w)
 
 
 def pack_y_kernel(own_up, own_down, mine_ref, low_ref, high_ref, up_ref, down_ref):
@@ -134,9 +160,9 @@
                 down_ref[base + 2 * z : base + 2 * z + 2] = ref[src + 8 * z : src + 8 * z + 2]
             up_ref[base + 4] = ref[src + 16 + 7]
             down_ref[base + 4] = ref[src + 16]
-    for k, ref in enumerate((mine_ref, low_ref, high_ref)):
-        up_ref[Y_ROWS - 3 + k] = ref[Z_ROWS - 1]
-        down_ref[Y_ROWS - 3 + k] = ref[Z_ROWS - 1]
+    for k, row in enumerate((mine_ref[0], low_ref[Z_ROWS - 1], high_ref[Z_ROWS - 1])):
+        up_ref[Y_ROWS - 3 + k] = row
+        down_ref[Y_ROWS - 3 + k] = row
 
 
 def pack_y(own_up, own_down, mine, low, high):
@@ -163,14 +189,14 @@
     return inside // BX, pl.multiple_of(inside % BX * 8 + 8, 8)
 
 
-def read_codes(sites, zl_ref, zh_ref, yl_ref, yh_ref):
-    rows = [zl_ref[Z_ROWS - 1], zh_ref[Z_ROWS - 1]]
+def read_codes(mine_ref, zl_ref, zh_ref, yl_ref, yh_ref):
+    rows = [mine_ref[0], zl_ref[Z_ROWS - 1], zh_ref[Z_ROWS - 1]]
     rows += [ref[Y_ROWS - 3 + k] for ref in (yl_ref, yh_ref) for k in range(3)]
-    codes = {(0, s): sites[s] for s in range(NB)}
+    codes = {}
     for k, row in enumerate(rows):
         row = row.astype(F32)
         for s in range(NB):
-            codes[k + 1, s] = SITES - row[0, s].astype(jnp.int32)
+            codes[k, s] = SITES - row[0, s].astype(jnp.int32)
     return codes
 
 
@@ -242,9 +268,9 @@
     return total
 
 
-def forward_kernel(sites, x_ref, g_ref, zl_ref, zh_ref, yl_ref, yh_ref, w_ref,
+def forward_kernel(mine_ref, x_ref, g_ref, zl_ref, zh_ref, yl_ref, yh_ref, w_ref,
                    act_ref, dpre_ref, keep_ref, send_ref, vol, stack, turned, split):
-    codes = read_codes(sites, zl_ref, zh_ref, yl_ref, yh_ref)
+    codes = read_codes(mine_ref, zl_ref, zh_ref, yl_ref, yh_ref)
     core = lax.axis_index("gy") & 1
     clear(vol)
     fill(vol, codes, x_ref, zl_ref, zh_ref, yl_ref, yh_ref)
@@ -299,7 +325,7 @@
             jax.ShapeDtypeStruct((HALF, C, C), F32),
             jax.ShapeDtypeStruct((HALF, C, C), BF16),
         ),
-        in_specs=[SMEM] + [VMEM] * 7,
+        in_specs=[VMEM] * 8,
         out_specs=(VMEM,) * 4,
         scratch_shapes=[
             pltpu.VMEM((VZ, VY, VX, C), F32),
@@ -313,9 +339,9 @@
     )(sites, x, g, zl, zh, yl, yh, w)
 
 
-def backward_kernel(sites, x_ref, dpre_ref, zl_ref, zh_ref, yl_ref, yh_ref, w_ref,
+def backward_kernel(mine_ref, x_ref, dpre_ref, zl_ref, zh_ref, yl_ref, yh_ref, w_ref,
                     grad_ref, vol, stack):
-    codes = read_codes(sites, zl_ref, zh_ref, yl_ref, yh_ref)
+    codes = read_codes(mine_ref, zl_ref, zh_ref, yl_ref, yh_ref)
     clear(vol)
     fill(vol, codes, x_ref, zl_ref, zh_ref, yl_ref, yh_ref)
 
@@ -403,7 +429,7 @@
     return pl.pallas_call(
         backward_kernel,
         out_shape=jax.ShapeDtypeStruct((NB, 64, 8, C), BF16),
-        in_specs=[SMEM] + [VMEM] * 7,
+        in_specs=[VMEM] * 8,
         out_specs=VMEM,
         scratch_shapes=[
             pltpu.VMEM((VZ, VY, VX, C), F32),
@@ -508,11 +534,13 @@
     g = cotangent.reshape(NB, 8, 8, 8, C)
     sites = brick_sites.reshape(NB)
     devices = lax.axis_size("gz") * lax.axis_size("gy")
-    z_up, z_down, own_up, own_down = pack_z(sites, x, g)
+    z_up, z_down = pack_z(sites, x, g)
+    z_up, z_down, *later = lax.optimization_barrier((z_up, z_down, sites, x, g, kernel))
+    x, g, w, mine, own_up, own_down = stage(*later)
     zl, zh = neighbours(z_up, z_down, "gz")
-    y_up, y_down = pack_y(own_up, own_down, z_up, zl, zh)
+    y_up, y_down = pack_y(own_up, own_down, mine, zl, zh)
     yl, yh = neighbours(y_up, y_down, "gy")
-    act, dpre, keep, send = forward(sites, x, g, zl, zh, yl, yh, kernel)
+    act, dpre, keep, send = forward(mine, x, g, zl, zh, yl, yh, w)
 
     plan = exchange_plan()
     first = HALF * C
@@ -529,7 +557,7 @@
         keep, *sends = merge(keep, arrived, group)
         arrived = [swap_with(send, group, 1 + k) for k, send in enumerate(sends)]
         if grad_in is None:
-            grad_in = backward(sites, x, dpre, zl, zh, yl, yh, kernel)
+            grad_in = backward(mine, x, dpre, zl, zh, yl, yh, w)
             *arrived, grad_in = lax.optimization_barrier((*arrived, grad_in))
     (piece,) = merge(keep, arrived, scale=1.0 / (NB * VOX * devices) ** 0.5)
 

time: 74.3 us -> 67.1 us (0.903)
  local copies, waits for them, and re-layouts: 6.41 us -> 3.72 us
  starting transfers between devices: 32 us -> 29.9 us
  waiting for transfers between devices: 19.4 us -> 17.7 us
    unnamed x18 -> x8, local copies, waits for them, and re-layouts: 6.41 us -> 3.72 us
    ppermute x4, waiting for transfers between devices: 6.61 us -> 4.72 us  [neighbours(): return (lax.ppermute(up, axis, forward), lax.ppermute(down, axis, backward))]
    ppermute x4, starting transfers between devices: 10 us -> 8.79 us  [neighbours(): return (lax.ppermute(up, axis, forward), lax.ppermute(down, axis, backward))]
    ppermute x17, starting transfers between devices: 21.9 us -> 21.1 us  [swap_with(): return lax.ppermute(value, AXES, pairs)]
    pallas_call x1 -> x2, Pallas kernels: 1.87 us -> 2.27 us  [the longest x1 1.62 us: pack_z(): pl.pallas_call(pack_z_kernel, out_shape=(shape, shape), in_specs=[ANY, AN...]
  transfers between devices with their start and end apart: 21 -> 21, of which waited for: 14 -> 11; matrix products, arithmetic and copies ran while one was open for 0% -> 0% of each run, Pallas kernels for 9% -> 10%
where the time goes in v5:
time: 67.1 us; the launch traced here: 66.7 us
  starting transfers between devices  29.9 us (45%)
  waiting for transfers between devices  17.7 us (26%)
  Pallas kernels  14.6 us (22%)
  local copies, waits for them, and re-layouts  3.72 us (6%)
  between operations  0.75 us (1%)
    ppermute x17, starting transfers between devices, swap_with(): return lax.ppermute(value, AXES, pairs)  21.1 us
    ppermute x17, waiting for transfers between devices, swap_with(): return lax.ppermute(value, AXES, pairs)  13 us
    ppermute x4, starting transfers between devices, neighbours(): return (lax.ppermute(up, axis, forward), lax.ppermute(down, axis, backward))  8.79 us
    pallas_call x1, Pallas kernels, backward(): pl.pallas_call(backward_kernel, out_shape=jax.ShapeDtypeStruct((NB, 64, 8...  5.86 us
    ppermute x4, waiting for transfers between devices, neighbours(): return (lax.ppermute(up, axis, forward), lax.ppermute(down, axis, backward))  4.72 us
    pallas_call x1, Pallas kernels, forward(): pl.pallas_call(forward_kernel, out_shape=(rows, jax.ShapeDtypeStruct((64,...  4.5 us
    unnamed x8, local copies, waits for them, and re-layouts  3.72 us
    pallas_call x1, Pallas kernels, finish(): pl.pallas_call(functools.partial(finish_kernel, first, share, plan), out_...  1.79 us
  transfers between devices with their start and end apart: 21, of which 11 were waited for; matrix products, arithmetic and copies ran while one was open for 0% of the time, Pallas kernels for 10%

profile of v5, /device:TPU:0, one launch (start us, length us, event | category | flops | bytes accessed | tf_op | source)
XLA Modules:
  0.0 66.7 jit_solution(13627244693585767304)
XLA Ops:
  0.6 1.6 %pack_z.1 = (bf16[49,8,128]{2,1,0:T(8,128)(2,1)}, bf16[49,8,128]{2,1,0:T(8,128)(2,1)}) custom-call(s32[2]{0:T(128)} %bitcast.14, bf16[2,8,8,8,128]{4,3,2,1,0:T(8,128)(2,1)} %bitcast.8, bf16[2,8,8,8,128]{4,3,2,1,0:T(8,128)(2,1)} %bitcast.10), custom_call_target="tpu_custom_call" | custom-call | tf_op jit(solution)/shard_map/pack_z/pallas_call | solution.py:113
  2.3 4.9 %collective-permute-start = (bf16[49,8,128]{2,1,0:T(8,128)(2,1)}, bf16[49,8,128]{2,1,0:T(8,128)(2,1)S(1)}, u32[]{:S(2)}, u32[]{:S(2)}) collective-permute-start(bf16[49,8,128]{2,1,0:T(8,128)(2,1)} %get-tuple-element.44), channel_id=1, source_target_pairs={{0,4},{4,8},{8,12},{12,16},{16,20},{20,24},{24,28},{1,5},{5,9},{9,... | collective-permute-start | bytes 301064 | tf_op jit(solution)/shard_map/ppermute | solution.py:68
  7.2 1.3 %collective-permute-start.1 = (bf16[49,8,128]{2,1,0:T(8,128)(2,1)}, bf16[49,8,128]{2,1,0:T(8,128)(2,1)S(1)}, u32[]{:S(2)}, u32[]{:S(2)}) collective-permute-start(bf16[49,8,128]{2,1,0:T(8,128)(2,1)} %get-tuple-element.45), channel_id=1, source_target_pairs={{4,0},{8,4},{12,8},{16,12},{20,16},{24,20},{28,24},{5,1},{9,5},{13... | collective-permute-start | bytes 301064 | tf_op jit(solution)/shard_map/ppermute | solution.py:68
  8.5 0.0 copy-start
  8.5 0.9 %copy-done = bf16[1,1,2,512,128]{4,3,2,1,0:T(8,128)(2,1)S(1)} copy-done((bf16[1,1,2,512,128]{4,3,2,1,0:T(8,128)(2,1)S(1)}, bf16[1,1,2,512,128]{4,3,2,1,0:T(8,128)(2,1)}, u32[]{:S(2)}) %copy-start) | copy-done | bytes 262168
  9.4 0.9 %copy-done.1 = bf16[1,1,2,512,128]{4,3,2,1,0:T(8,128)(2,1)S(1)} copy-done((bf16[1,1,2,512,128]{4,3,2,1,0:T(8,128)(2,1)S(1)}, bf16[1,1,2,512,128]{4,3,2,1,0:T(8,128)(2,1)}, u32[]{:S(2)}) %copy-start.1) | copy-done | bytes 262168
  10.4 1.2 %copy-done.2 = bf16[27,128,128]{2,1,0:T(8,128)(2,1)S(1)} copy-done((bf16[27,128,128]{2,1,0:T(8,128)(2,1)S(1)}, bf16[27,128,128]{2,1,0:T(8,128)(2,1)}, u32[]{:S(2)}) %copy-start.2) | copy-done | bytes 884760
  11.5 0.7 copy-done.3
  12.2 0.7 stage.1
  12.9 0.0 collective-permute-done.low_ref.zl_ref
  12.9 1.0 %collective-permute-done.1.high_ref.zh_ref = bf16[49,8,128]{2,1,0:T(8,128)(2,1)S(1)} collective-permute-done((bf16[49,8,128]{2,1,0:T(8,128)(2,1)}, bf16[49,8,128]{2,1,0:T(8,128)(2,1)S(1)}, u32[]{:S(2)}, u32[]{:S(2)}) %collective-permute-start.1) | collective-permute-done | bytes 100384 | tf_op jit(solution)/shard_map/ppermute | solution.py:68
  13.9 1.3 %collective-permute-start.2 = (bf16[71,8,128]{2,1,0:T(8,128)(2,1)S(1)}, bf16[71,8,128]{2,1,0:T(8,128)(2,1)S(1)}, u32[]{:S(2)}, u32[]{:S(2)}) collective-permute-start(bf16[71,8,128]{2,1,0:T(8,128)(2,1)S(1)} %get-tuple-element.48), channel_id=1, source_target_pairs={{0,1},{1,2},{2,3},{4,5},{5,6},{6,7},{8,9},{9,10},{10,11},{12,13},{... | collective-permute-start | bytes 436232 | tf_op jit(solution)/shard_map/ppermute | solution.py:68
  15.2 1.3 %collective-permute-start.3 = (bf16[71,8,128]{2,1,0:T(8,128)(2,1)S(1)}, bf16[71,8,128]{2,1,0:T(8,128)(2,1)S(1)}, u32[]{:S(2)}, u32[]{:S(2)}) collective-permute-start(bf16[71,8,128]{2,1,0:T(8,128)(2,1)S(1)} %get-tuple-element.49), channel_id=1, source_target_pairs={{1,0},{2,1},{3,2},{5,4},{6,5},{7,6},{9,8},{10,9},{11,10},{13,12},{... | collective-permute-start | bytes 436232 | tf_op jit(solution)/shard_map/ppermute | solution.py:68
  16.5 0.0 collective-permute-done.2.yl_ref
  16.5 3.7 %collective-permute-done.3.yh_ref = bf16[71,8,128]{2,1,0:T(8,128)(2,1)S(1)} collective-permute-done((bf16[71,8,128]{2,1,0:T(8,128)(2,1)S(1)}, bf16[71,8,128]{2,1,0:T(8,128)(2,1)S(1)}, u32[]{:S(2)}, u32[]{:S(2)}) %collective-permute-start.3) | collective-permute-done | bytes 145440 | tf_op jit(solution)/shard_map/ppermute | solution.py:68
  20.2 4.5 %forward.1 = (bf16[2,64,8,128]{3,2,1,0:T(8,128)(2,1)}, bf16[64,16,128]{2,1,0:T(8,128)(2,1)S(1)}, f32[14,128,128]{2,1,0:T(8,128)S(1)}, bf16[14,128,128]{2,1,0:T(8,128)(2,1)S(1)}) custom-call(bf16[1,8,128]{2,1,0:T(8,128)(2,1)S(1)} %get-tuple-element.41.mine_ref, bf16[2,8,8,8,128]{4,3,2,1,0:T(8,128)(2,1)S(1)} %get-tuple-element.42.x_ref, ...), custom_call_target="tpu_custom_call" | custom-call | flops 2000000000 | bytes 5242880 | tf_op jit(solution)/shard_map/forward/pallas_call | solution.py:320
  24.7 3.8 %collective-permute-start.4 = (bf16[14,128,128]{2,1,0:T(8,128)(2,1)S(1)}, bf16[14,128,128]{2,1,0:T(8,128)(2,1)S(1)}, u32[]{:S(2)}, u32[]{:S(2)}) collective-permute-start(bf16[14,128,128]{2,1,0:T(8,128)(2,1)S(1)} %get-tuple-element.53), channel_id=1, source_target_pairs={{0,1},{1,0},{2,3},{3,2},{4,5},{5,4},{6,7},{7,6},{8,9},{9,8},{10,11... | collective-permute-start | bytes 1376264 | tf_op jit(solution)/shard_map/ppermute | solution.py:54
  28.5 1.4 %collective-permute-done.4 = bf16[14,128,128]{2,1,0:T(8,128)(2,1)S(1)} collective-permute-done((bf16[14,128,128]{2,1,0:T(8,128)(2,1)S(1)}, bf16[14,128,128]{2,1,0:T(8,128)(2,1)S(1)}, u32[]{:S(2)}, u32[]{:S(2)}) %collective-permute-start.4) | collective-permute-done | bytes 458784 | tf_op jit(solution)/shard_map/ppermute | solution.py:54
  29.9 0.1 merge.3
  30.0 0.2 collective-permute-start.5
  30.2 2.4 %collective-permute-start.6 = (bf16[448,128]{1,0:T(8,128)(2,1)S(1)}, bf16[448,128]{1,0:T(8,128)(2,1)S(1)}, u32[]{:S(2)}, u32[]{:S(2)}) collective-permute-start(bf16[448,128]{1,0:T(8,128)(2,1)S(1)} %get-tuple-element.55), channel_id=1, source_target_pairs={{0,4},{1,5},{2,6},{3,7},{4,0},{5,1},{6,2},{7,3},{8,12},{9,13},{10,... | collective-permute-start | bytes 344072 | tf_op jit(solution)/shard_map/ppermute | solution.py:54
  32.6 1.4 %collective-permute-start.7 = (bf16[448,128]{1,0:T(8,128)(2,1)S(1)}, bf16[448,128]{1,0:T(8,128)(2,1)S(1)}, u32[]{:S(2)}, u32[]{:S(2)}) collective-permute-start(bf16[448,128]{1,0:T(8,128)(2,1)S(1)} %get-tuple-element.56), channel_id=1, source_target_pairs={{0,6},{1,7},{2,4},{3,5},{4,2},{5,3},{6,0},{7,1},{8,14},{9,15},{10,... | collective-permute-start | bytes 344072 | tf_op jit(solution)/shard_map/ppermute | solution.py:54
  34.0 5.9 %backward.1 = bf16[2,64,8,128]{3,2,1,0:T(8,128)(2,1)} custom-call(bf16[1,8,128]{2,1,0:T(8,128)(2,1)S(1)} %get-tuple-element.41.mine_ref, bf16[2,8,8,8,128]{4,3,2,1,0:T(8,128)(2,1)S(1)} %get-tuple-element.42.x_ref, bf16[64,16,128]{2,1,0:T(8,128)(2,1)S(1)} %get-tuple-element.57.dpre_ref, bf16[49,8,128]{2,1,0:T(8,128)(2,1)S(1)} %collective-permute-done.low_ref.zl_ref, ...), custom_call_target="tpu_custom_call" | custom-call | flops 1000000000 | bytes 5242880 | tf_op jit(solution)/shard_map/backward/pallas_call | solution.py:429
  39.8 0.0 collective-permute-done.5.refs_1_
  39.8 0.0 collective-permute-done.6.refs_2_
  39.8 0.0 collective-permute-done.7.refs_3_
  39.8 0.1 merge.4
  39.9 2.2 %collective-permute-start.8 = (bf16[112,128]{1,0:T(8,128)(2,1)S(1)}, bf16[112,128]{1,0:T(8,128)(2,1)S(1)}, u32[]{:S(2)}, u32[]{:S(2)}) collective-permute-start(bf16[112,128]{1,0:T(8,128)(2,1)S(1)} %get-tuple-element.64), channel_id=1, source_target_pairs={{0,8},{1,9},{2,10},{3,11},{4,12},{5,13},{6,14},{7,15},{8,0},{9,1},... | collective-permute-start | bytes 86024 | tf_op jit(solution)/shard_map/ppermute | solution.py:54
  42.1 2.6 %collective-permute-start.9 = (bf16[112,128]{1,0:T(8,128)(2,1)S(1)}, bf16[112,128]{1,0:T(8,128)(2,1)S(1)}, u32[]{:S(2)}, u32[]{:S(2)}) collective-permute-start(bf16[112,128]{1,0:T(8,128)(2,1)S(1)} %get-tuple-element.65), channel_id=1, source_target_pairs={{0,16},{1,17},{2,18},{3,19},{4,20},{5,21},{6,22},{7,23},{8,24},{9,... | collective-permute-start | bytes 86024 | tf_op jit(solution)/shard_map/ppermute | solution.py:54
  44.8 0.0 collective-permute-start.10
  44.8 2.3 %collective-permute-done.9.refs_2_ = bf16[112,128]{1,0:T(8,128)(2,1)S(1)} collective-permute-done((bf16[112,128]{1,0:T(8,128)(2,1)S(1)}, bf16[112,128]{1,0:T(8,128)(2,1)S(1)}, u32[]{:S(2)}, u32[]{:S(2)}) %collective-permute-start.9) | collective-permute-done | bytes 28704 | tf_op jit(solution)/shard_map/ppermute | solution.py:54
  47.1 3.4 %collective-permute-done.10.refs_3_ = bf16[112,128]{1,0:T(8,128)(2,1)S(1)} collective-permute-done((bf16[112,128]{1,0:T(8,128)(2,1)S(1)}, bf16[112,128]{1,0:T(8,128)(2,1)S(1)}, u32[]{:S(2)}, u32[]{:S(2)}) %collective-permute-start.10) | collective-permute-done | bytes 28704 | tf_op jit(solution)/shard_map/ppermute | solution.py:54
  50.5 0.4 collective-permute-start.13
  50.9 0.0 collective-permute-start.12
  50.9 4.1 %collective-permute-start.11 = (bf16[112,128]{1,0:T(8,128)(2,1)S(1)}, bf16[112,128]{1,0:T(8,128)(2,1)S(1)}, u32[]{:S(2)}, u32[]{:S(2)}) collective-permute-start(bf16[112,128]{1,0:T(8,128)(2,1)S(1)} %merge.5.refs_0_), channel_id=1, source_target_pairs={{0,8},{1,9},{2,10},{3,11},{4,12},{5,13},{6,14},{7,15},{8,0},{9,1},... | collective-permute-start | bytes 86024 | tf_op jit(solution)/shard_map/ppermute | solution.py:54
  54.9 1.3 %collective-permute-done.13.refs_3_ = bf16[112,128]{1,0:T(8,128)(2,1)S(1)} collective-permute-done((bf16[112,128]{1,0:T(8,128)(2,1)S(1)}, bf16[112,128]{1,0:T(8,128)(2,1)S(1)}, u32[]{:S(2)}, u32[]{:S(2)}) %collective-permute-start.13) | collective-permute-done | bytes 28704 | tf_op jit(solution)/shard_map/ppermute | solution.py:54
  56.2 0.6 collective-permute-done.11.refs_1_
  56.8 0.6 collective-permute-start.16
  57.4 1.2 %collective-permute-start.15 = (bf16[448,128]{1,0:T(8,128)(2,1)S(1)}, bf16[448,128]{1,0:T(8,128)(2,1)S(1)}, u32[]{:S(2)}, u32[]{:S(2)}) collective-permute-start(bf16[448,128]{1,0:T(8,128)(2,1)S(1)} %join.1.refs_0_), channel_id=1, source_target_pairs={{0,4},{1,5},{2,6},{3,7},{4,0},{5,1},{6,2},{7,3},{8,12},{9,13},{10,... | collective-permute-start | bytes 344072 | tf_op jit(solution)/shard_map/ppermute | solution.py:54
  58.5 1.8 %collective-permute-start.14 = (bf16[448,128]{1,0:T(8,128)(2,1)S(1)}, bf16[448,128]{1,0:T(8,128)(2,1)S(1)}, u32[]{:S(2)}, u32[]{:S(2)}) collective-permute-start(bf16[448,128]{1,0:T(8,128)(2,1)S(1)} %join.1.refs_0_), channel_id=1, source_target_pairs={{0,2},{1,3},{2,0},{3,1},{4,6},{5,7},{6,4},{7,5},{8,10},{9,11},{10,... | collective-permute-start | bytes 344072 | tf_op jit(solution)/shard_map/ppermute | solution.py:54
  60.4 2.3 %collective-permute-done.16.refs_3_ = bf16[448,128]{1,0:T(8,128)(2,1)S(1)} collective-permute-done((bf16[448,128]{1,0:T(8,128)(2,1)S(1)}, bf16[448,128]{1,0:T(8,128)(2,1)S(1)}, u32[]{:S(2)}, u32[]{:S(2)}) %collective-permute-start.16) | collective-permute-done | bytes 114720 | tf_op jit(solution)/shard_map/ppermute | solution.py:54
  62.7 0.8 %collective-permute-done.15.refs_2_ = bf16[448,128]{1,0:T(8,128)(2,1)S(1)} collective-permute-done((bf16[448,128]{1,0:T(8,128)(2,1)S(1)}, bf16[448,128]{1,0:T(8,128)(2,1)S(1)}, u32[]{:S(2)}, u32[]{:S(2)}) %collective-permute-start.15) | collective-permute-done | bytes 114720 | tf_op jit(solution)/shard_map/ppermute | solution.py:54
  63.4 0.0 collective-permute-start.19
  63.4 0.5 collective-permute-start.18
  63.9 0.1 collective-permute-done.20.refs_7_
  64.0 0.8 %collective-permute-done.19.refs_6_ = bf16[448,128]{1,0:T(8,128)(2,1)S(1)} collective-permute-done((bf16[448,128]{1,0:T(8,128)(2,1)S(1)}, bf16[448,128]{1,0:T(8,128)(2,1)S(1)}, u32[]{:S(2)}, u32[]{:S(2)}) %collective-permute-start.19) | collective-permute-done | bytes 114720 | tf_op jit(solution)/shard_map/ppermute | solution.py:54
  64.7 0.2 collective-permute-done.18.refs_5_
  64.9 1.8 %finish.1 = f32[3456,128]{1,0:T(8,128)} custom-call(bf16[448,128]{1,0:T(8,128)(2,1)S(1)} %join.1.refs_0_, bf16[448,128]{1,0:T(8,128)(2,1)S(1)} %collective-permute-done.14.refs_1_, bf16[448,128]{1,0:T(8,128)(2,1)S(1)} %collective-permute-done.15.refs_2_, bf16[448,128]{1,0:T(8,128)(2,1)S(1)} %collective-permute-done.16.refs_3_, ...), custom_call_target="tpu_custom_call" | custom-call | tf_op jit(solution)/shard_map/finish/pallas_call | solution.py:522
  (12 shorter events, 0.1 us)
Async XLA Ops:
  2.3 10.6 %collective-permute-start = (bf16[49,8,128]{2,1,0:T(8,128)(2,1)}, bf16[49,8,128]{2,1,0:T(8,128)(2,1)S(1)}, u32[]{:S(2)}, u32[]{:S(2)}) collective-permute-start(bf16[49,8,128]{2,1,0:T(8,128)(2,1)} %get-tuple-element.44), channel_id=1, source_target_pairs={{0,4},{4,8},{8,12},{12,16},{16,20},{20,24},{24,28},{1,5},{5,9},{9,... | collective-permute-start | bytes 301064 | tf_op jit(solution)/shard_map/ppermute | solution.py:68
  7.2 6.7 %collective-permute-start.1 = (bf16[49,8,128]{2,1,0:T(8,128)(2,1)}, bf16[49,8,128]{2,1,0:T(8,128)(2,1)S(1)}, u32[]{:S(2)}, u32[]{:S(2)}) collective-permute-start(bf16[49,8,128]{2,1,0:T(8,128)(2,1)} %get-tuple-element.45), channel_id=1, source_target_pairs={{4,0},{8,4},{12,8},{16,12},{20,16},{24,20},{28,24},{5,1},{9,5},{13... | collective-permute-start | bytes 301064 | tf_op jit(solution)/shard_map/ppermute | solution.py:68
  8.5 1.0 %copy-start = (bf16[1,1,2,512,128]{4,3,2,1,0:T(8,128)(2,1)S(1)}, bf16[1,1,2,512,128]{4,3,2,1,0:T(8,128)(2,1)}, u32[]{:S(2)}) copy-start(bf16[1,1,2,512,128]{4,3,2,1,0:T(8,128)(2,1)} %param.4) | copy-start | bytes 786436
  9.4 0.9 %copy-start.1 = (bf16[1,1,2,512,128]{4,3,2,1,0:T(8,128)(2,1)S(1)}, bf16[1,1,2,512,128]{4,3,2,1,0:T(8,128)(2,1)}, u32[]{:S(2)}) copy-start(bf16[1,1,2,512,128]{4,3,2,1,0:T(8,128)(2,1)} %param.7) | copy-start | bytes 786436
  10.4 1.2 %copy-start.2 = (bf16[27,128,128]{2,1,0:T(8,128)(2,1)S(1)}, bf16[27,128,128]{2,1,0:T(8,128)(2,1)}, u32[]{:S(2)}) copy-start(bf16[27,128,128]{2,1,0:T(8,128)(2,1)} %w_ref) | copy-start | bytes 2654212
  11.5 0.7 copy-start.3
  13.9 2.6 %collective-permute-start.2 = (bf16[71,8,128]{2,1,0:T(8,128)(2,1)S(1)}, bf16[71,8,128]{2,1,0:T(8,128)(2,1)S(1)}, u32[]{:S(2)}, u32[]{:S(2)}) collective-permute-start(bf16[71,8,128]{2,1,0:T(8,128)(2,1)S(1)} %get-tuple-element.48), channel_id=1, source_target_pairs={{0,1},{1,2},{2,3},{4,5},{5,6},{6,7},{8,9},{9,10},{10,11},{12,13},{... | collective-permute-start | bytes 436232 | tf_op jit(solution)/shard_map/ppermute | solution.py:68
  15.2 5.0 %collective-permute-start.3 = (bf16[71,8,128]{2,1,0:T(8,128)(2,1)S(1)}, bf16[71,8,128]{2,1,0:T(8,128)(2,1)S(1)}, u32[]{:S(2)}, u32[]{:S(2)}) collective-permute-start(bf16[71,8,128]{2,1,0:T(8,128)(2,1)S(1)} %get-tuple-element.49), channel_id=1, source_target_pairs={{1,0},{2,1},{3,2},{5,4},{6,5},{7,6},{9,8},{10,9},{11,10},{13,12},{... | collective-permute-start | bytes 436232 | tf_op jit(solution)/shard_map/ppermute | solution.py:68
  24.7 5.2 %collective-permute-start.4 = (bf16[14,128,128]{2,1,0:T(8,128)(2,1)S(1)}, bf16[14,128,128]{2,1,0:T(8,128)(2,1)S(1)}, u32[]{:S(2)}, u32[]{:S(2)}) collective-permute-start(bf16[14,128,128]{2,1,0:T(8,128)(2,1)S(1)} %get-tuple-element.53), channel_id=1, source_target_pairs={{0,1},{1,0},{2,3},{3,2},{4,5},{5,4},{6,7},{7,6},{8,9},{9,8},{10,11... | collective-permute-start | bytes 1376264 | tf_op jit(solution)/shard_map/ppermute | solution.py:54
  30.0 9.8 %collective-permute-start.5 = (bf16[448,128]{1,0:T(8,128)(2,1)S(1)}, bf16[448,128]{1,0:T(8,128)(2,1)S(1)}, u32[]{:S(2)}, u32[]{:S(2)}) collective-permute-start(bf16[448,128]{1,0:T(8,128)(2,1)S(1)} %get-tuple-element.54), channel_id=1, source_target_pairs={{0,2},{1,3},{2,0},{3,1},{4,6},{5,7},{6,4},{7,5},{8,10},{9,11},{10,... | collective-permute-start | bytes 344072 | tf_op jit(solution)/shard_map/ppermute | solution.py:54
  30.2 9.6 %collective-permute-start.6 = (bf16[448,128]{1,0:T(8,128)(2,1)S(1)}, bf16[448,128]{1,0:T(8,128)(2,1)S(1)}, u32[]{:S(2)}, u32[]{:S(2)}) collective-permute-start(bf16[448,128]{1,0:T(8,128)(2,1)S(1)} %get-tuple-element.55), channel_id=1, source_target_pairs={{0,4},{1,5},{2,6},{3,7},{4,0},{5,1},{6,2},{7,3},{8,12},{9,13},{10,... | collective-permute-start | bytes 344072 | tf_op jit(solution)/shard_map/ppermute | solution.py:54
  32.6 7.2 %collective-permute-start.7 = (bf16[448,128]{1,0:T(8,128)(2,1)S(1)}, bf16[448,128]{1,0:T(8,128)(2,1)S(1)}, u32[]{:S(2)}, u32[]{:S(2)}) collective-permute-start(bf16[448,128]{1,0:T(8,128)(2,1)S(1)} %get-tuple-element.56), channel_id=1, source_target_pairs={{0,6},{1,7},{2,4},{3,5},{4,2},{5,3},{6,0},{7,1},{8,14},{9,15},{10,... | collective-permute-start | bytes 344072 | tf_op jit(solution)/shard_map/ppermute | solution.py:54
  39.9 4.9 %collective-permute-start.8 = (bf16[112,128]{1,0:T(8,128)(2,1)S(1)}, bf16[112,128]{1,0:T(8,128)(2,1)S(1)}, u32[]{:S(2)}, u32[]{:S(2)}) collective-permute-start(bf16[112,128]{1,0:T(8,128)(2,1)S(1)} %get-tuple-element.64), channel_id=1, source_target_pairs={{0,8},{1,9},{2,10},{3,11},{4,12},{5,13},{6,14},{7,15},{8,0},{9,1},... | collective-permute-start | bytes 86024 | tf_op jit(solution)/shard_map/ppermute | solution.py:54
  42.1 4.9 %collective-permute-start.9 = (bf16[112,128]{1,0:T(8,128)(2,1)S(1)}, bf16[112,128]{1,0:T(8,128)(2,1)S(1)}, u32[]{:S(2)}, u32[]{:S(2)}) collective-permute-start(bf16[112,128]{1,0:T(8,128)(2,1)S(1)} %get-tuple-element.65), channel_id=1, source_target_pairs={{0,16},{1,17},{2,18},{3,19},{4,20},{5,21},{6,22},{7,23},{8,24},{9,... | collective-permute-start | bytes 86024 | tf_op jit(solution)/shard_map/ppermute | solution.py:54
  44.8 5.7 %collective-permute-start.10 = (bf16[112,128]{1,0:T(8,128)(2,1)S(1)}, bf16[112,128]{1,0:T(8,128)(2,1)S(1)}, u32[]{:S(2)}, u32[]{:S(2)}) collective-permute-start(bf16[112,128]{1,0:T(8,128)(2,1)S(1)} %get-tuple-element.66), channel_id=1, source_target_pairs={{0,24},{1,25},{2,26},{3,27},{4,28},{5,29},{6,30},{7,31},{8,16},{9,... | collective-permute-start | bytes 86024 | tf_op jit(solution)/shard_map/ppermute | solution.py:54
  50.5 5.7 %collective-permute-start.13 = (bf16[112,128]{1,0:T(8,128)(2,1)S(1)}, bf16[112,128]{1,0:T(8,128)(2,1)S(1)}, u32[]{:S(2)}, u32[]{:S(2)}) collective-permute-start(bf16[112,128]{1,0:T(8,128)(2,1)S(1)} %merge.5.refs_0_), channel_id=1, source_target_pairs={{0,24},{1,25},{2,26},{3,27},{4,28},{5,29},{6,30},{7,31},{8,16},{9,... | collective-permute-start | bytes 86024 | tf_op jit(solution)/shard_map/ppermute | solution.py:54
  50.9 5.4 %collective-permute-start.12 = (bf16[112,128]{1,0:T(8,128)(2,1)S(1)}, bf16[112,128]{1,0:T(8,128)(2,1)S(1)}, u32[]{:S(2)}, u32[]{:S(2)}) collective-permute-start(bf16[112,128]{1,0:T(8,128)(2,1)S(1)} %merge.5.refs_0_), channel_id=1, source_target_pairs={{0,16},{1,17},{2,18},{3,19},{4,20},{5,21},{6,22},{7,23},{8,24},{9,... | collective-permute-start | bytes 86024 | tf_op jit(solution)/shard_map/ppermute | solution.py:54
  50.9 5.9 %collective-permute-start.11 = (bf16[112,128]{1,0:T(8,128)(2,1)S(1)}, bf16[112,128]{1,0:T(8,128)(2,1)S(1)}, u32[]{:S(2)}, u32[]{:S(2)}) collective-permute-start(bf16[112,128]{1,0:T(8,128)(2,1)S(1)} %merge.5.refs_0_), channel_id=1, source_target_pairs={{0,8},{1,9},{2,10},{3,11},{4,12},{5,13},{6,14},{7,15},{8,0},{9,1},... | collective-permute-start | bytes 86024 | tf_op jit(solution)/shard_map/ppermute | solution.py:54
  56.8 5.9 %collective-permute-start.16 = (bf16[448,128]{1,0:T(8,128)(2,1)S(1)}, bf16[448,128]{1,0:T(8,128)(2,1)S(1)}, u32[]{:S(2)}, u32[]{:S(2)}) collective-permute-start(bf16[448,128]{1,0:T(8,128)(2,1)S(1)} %join.1.refs_0_), channel_id=1, source_target_pairs={{0,6},{1,7},{2,4},{3,5},{4,2},{5,3},{6,0},{7,1},{8,14},{9,15},{10,... | collective-permute-start | bytes 344072 | tf_op jit(solution)/shard_map/ppermute | solution.py:54
  57.4 6.0 %collective-permute-start.15 = (bf16[448,128]{1,0:T(8,128)(2,1)S(1)}, bf16[448,128]{1,0:T(8,128)(2,1)S(1)}, u32[]{:S(2)}, u32[]{:S(2)}) collective-permute-start(bf16[448,128]{1,0:T(8,128)(2,1)S(1)} %join.1.refs_0_), channel_id=1, source_target_pairs={{0,4},{1,5},{2,6},{3,7},{4,0},{5,1},{6,2},{7,3},{8,12},{9,13},{10,... | collective-permute-start | bytes 344072 | tf_op jit(solution)/shard_map/ppermute | solution.py:54
  58.5 4.9 %collective-permute-start.14 = (bf16[448,128]{1,0:T(8,128)(2,1)S(1)}, bf16[448,128]{1,0:T(8,128)(2,1)S(1)}, u32[]{:S(2)}, u32[]{:S(2)}) collective-permute-start(bf16[448,128]{1,0:T(8,128)(2,1)S(1)} %join.1.refs_0_), channel_id=1, source_target_pairs={{0,2},{1,3},{2,0},{3,1},{4,6},{5,7},{6,4},{7,5},{8,10},{9,11},{10,... | collective-permute-start | bytes 344072 | tf_op jit(solution)/shard_map/ppermute | solution.py:54
  60.3 3.6 %collective-permute-start.17 = (bf16[448,128]{1,0:T(8,128)(2,1)S(1)}, bf16[448,128]{1,0:T(8,128)(2,1)S(1)}, u32[]{:S(2)}, u32[]{:S(2)}) collective-permute-start(bf16[448,128]{1,0:T(8,128)(2,1)S(1)} %join.1.refs_0_), channel_id=1, source_target_pairs={{0,1},{1,0},{2,3},{3,2},{4,5},{5,4},{6,7},{7,6},{8,9},{9,8},{10,11... | collective-permute-start | bytes 344072 | tf_op jit(solution)/shard_map/ppermute | solution.py:54
  62.6 1.3 %collective-permute-start.20 = (bf16[448,128]{1,0:T(8,128)(2,1)S(1)}, bf16[448,128]{1,0:T(8,128)(2,1)S(1)}, u32[]{:S(2)}, u32[]{:S(2)}) collective-permute-start(bf16[448,128]{1,0:T(8,128)(2,1)S(1)} %collective-permute-done.16.refs_3_), channel_id=1, source_target_pairs={{0,1},{1,0},{2,3},{3,2},{4,5},{5,4},{6,7},{7,6},{8,9},{9,8},{10,11... | collective-permute-start | bytes 344072 | tf_op jit(solution)/shard_map/ppermute | solution.py:54
  63.4 1.3 %collective-permute-start.19 = (bf16[448,128]{1,0:T(8,128)(2,1)S(1)}, bf16[448,128]{1,0:T(8,128)(2,1)S(1)}, u32[]{:S(2)}, u32[]{:S(2)}) collective-permute-start(bf16[448,128]{1,0:T(8,128)(2,1)S(1)} %collective-permute-done.15.refs_2_), channel_id=1, source_target_pairs={{0,1},{1,0},{2,3},{3,2},{4,5},{5,4},{6,7},{7,6},{8,9},{9,8},{10,11... | collective-permute-start | bytes 344072 | tf_op jit(solution)/shard_map/ppermute | solution.py:54
  63.4 1.5 %collective-permute-start.18 = (bf16[448,128]{1,0:T(8,128)(2,1)S(1)}, bf16[448,128]{1,0:T(8,128)(2,1)S(1)}, u32[]{:S(2)}, u32[]{:S(2)}) collective-permute-start(bf16[448,128]{1,0:T(8,128)(2,1)S(1)} %collective-permute-done.14.refs_1_), channel_id=1, source_target_pairs={{0,1},{1,0},{2,3},{3,2},{4,5},{5,4},{6,7},{7,6},{8,9},{9,8},{10,11... | collective-permute-start | bytes 344072 | tf_op jit(solution)/shard_map/ppermute | solution.py:54

commit v6 on v5

--- a/solution.py
+++ b/solution.py
@@ -35,8 +35,7 @@
         groups.append((gy_bits.pop(0), gz_bits.pop(0)))
     rest = gy_bits + gz_bits
     while rest:
-        groups.append(tuple(rest[:2]))
-        rest = rest[2:]
+        groups.append((rest.pop(0),))
     return groups
 
 

time: 67.1 us -> 69.1 us (1.030)
  waiting for transfers between devices: 17.7 us -> 19 us
  starting transfers between devices: 29.9 us -> 30.7 us
    ppermute x17 -> x15, waiting for transfers between devices: 13 us -> 14.3 us  [swap_with(): return lax.ppermute(value, AXES, pairs)]
    ppermute x17 -> x15, starting transfers between devices: 21.1 us -> 21.9 us  [swap_with(): return lax.ppermute(value, AXES, pairs)]
  transfers between devices with their start and end apart: 21 -> 19, of which waited for: 11 -> 12; matrix products, arithmetic and copies ran while one was open for 0% -> 0% of each run, Pallas kernels for 10% -> 9%
where the time goes in v6:
time: 69.1 us; the launch traced here: 68.8 us
  starting transfers between devices  30.7 us (44%)
  waiting for transfers between devices  19 us (27%)
  Pallas kernels  14.6 us (21%)
  local copies, waits for them, and re-layouts  3.72 us (5%)
  between operations  0.75 us (1%)
    ppermute x15, starting transfers between devices, swap_with(): return lax.ppermute(value, AXES, pairs)  21.9 us
    ppermute x15, waiting for transfers between devices, swap_with(): return lax.ppermute(value, AXES, pairs)  14.3 us
    ppermute x4, starting transfers between devices, neighbours(): return (lax.ppermute(up, axis, forward), lax.ppermute(down, axis, backward))  8.79 us
    pallas_call x1, Pallas kernels, backward(): pl.pallas_call(backward_kernel, out_shape=jax.ShapeDtypeStruct((NB, 64, 8...  5.87 us
    ppermute x4, waiting for transfers between devices, neighbours(): return (lax.ppermute(up, axis, forward), lax.ppermute(down, axis, backward))  4.72 us
    pallas_call x1, Pallas kernels, forward(): pl.pallas_call(forward_kernel, out_shape=(rows, jax.ShapeDtypeStruct((64,...  4.49 us
    unnamed x8, local copies, waits for them, and re-layouts  3.72 us
    pallas_call x1, Pallas kernels, finish(): pl.pallas_call(functools.partial(finish_kernel, first, share, plan), out_...  1.79 us
  transfers between devices with their start and end apart: 19, of which 12 were waited for; matrix products, arithmetic and copies ran while one was open for 0% of the time, Pallas kernels for 9%

profile of v6, /device:TPU:0, one launch (start us, length us, event | category | flops | bytes accessed | tf_op | source)
XLA Modules:
  0.0 68.8 jit_solution(10104976281791873247)
XLA Ops:
  0.6 1.6 %pack_z.1 = (bf16[49,8,128]{2,1,0:T(8,128)(2,1)}, bf16[49,8,128]{2,1,0:T(8,128)(2,1)}) custom-call(s32[2]{0:T(128)} %bitcast.14, bf16[2,8,8,8,128]{4,3,2,1,0:T(8,128)(2,1)} %bitcast.8, bf16[2,8,8,8,128]{4,3,2,1,0:T(8,128)(2,1)} %bitcast.10), custom_call_target="tpu_custom_call" | custom-call | tf_op jit(solution)/shard_map/pack_z/pallas_call | solution.py:112
  2.3 4.9 %collective-permute-start = (bf16[49,8,128]{2,1,0:T(8,128)(2,1)}, bf16[49,8,128]{2,1,0:T(8,128)(2,1)S(1)}, u32[]{:S(2)}, u32[]{:S(2)}) collective-permute-start(bf16[49,8,128]{2,1,0:T(8,128)(2,1)} %get-tuple-element.44), channel_id=1, source_target_pairs={{0,4},{4,8},{8,12},{12,16},{16,20},{20,24},{24,28},{1,5},{5,9},{9,... | collective-permute-start | bytes 301064 | tf_op jit(solution)/shard_map/ppermute | solution.py:67
  7.2 1.3 %collective-permute-start.1 = (bf16[49,8,128]{2,1,0:T(8,128)(2,1)}, bf16[49,8,128]{2,1,0:T(8,128)(2,1)S(1)}, u32[]{:S(2)}, u32[]{:S(2)}) collective-permute-start(bf16[49,8,128]{2,1,0:T(8,128)(2,1)} %get-tuple-element.45), channel_id=1, source_target_pairs={{4,0},{8,4},{12,8},{16,12},{20,16},{24,20},{28,24},{5,1},{9,5},{13... | collective-permute-start | bytes 301064 | tf_op jit(solution)/shard_map/ppermute | solution.py:67
  8.5 0.0 copy-start
  8.5 0.9 %copy-done = bf16[1,1,2,512,128]{4,3,2,1,0:T(8,128)(2,1)S(1)} copy-done((bf16[1,1,2,512,128]{4,3,2,1,0:T(8,128)(2,1)S(1)}, bf16[1,1,2,512,128]{4,3,2,1,0:T(8,128)(2,1)}, u32[]{:S(2)}) %copy-start) | copy-done | bytes 262168
  9.4 0.9 %copy-done.1 = bf16[1,1,2,512,128]{4,3,2,1,0:T(8,128)(2,1)S(1)} copy-done((bf16[1,1,2,512,128]{4,3,2,1,0:T(8,128)(2,1)S(1)}, bf16[1,1,2,512,128]{4,3,2,1,0:T(8,128)(2,1)}, u32[]{:S(2)}) %copy-start.1) | copy-done | bytes 262168
  10.4 1.2 %copy-done.2 = bf16[27,128,128]{2,1,0:T(8,128)(2,1)S(1)} copy-done((bf16[27,128,128]{2,1,0:T(8,128)(2,1)S(1)}, bf16[27,128,128]{2,1,0:T(8,128)(2,1)}, u32[]{:S(2)}) %copy-start.2) | copy-done | bytes 884760
  11.5 0.7 copy-done.3
  12.2 0.7 stage.1
  12.9 0.0 collective-permute-done.low_ref.zl_ref
  12.9 1.0 %collective-permute-done.1.high_ref.zh_ref = bf16[49,8,128]{2,1,0:T(8,128)(2,1)S(1)} collective-permute-done((bf16[49,8,128]{2,1,0:T(8,128)(2,1)}, bf16[49,8,128]{2,1,0:T(8,128)(2,1)S(1)}, u32[]{:S(2)}, u32[]{:S(2)}) %collective-permute-start.1) | collective-permute-done | bytes 100384 | tf_op jit(solution)/shard_map/ppermute | solution.py:67
  13.9 1.3 %collective-permute-start.2 = (bf16[71,8,128]{2,1,0:T(8,128)(2,1)S(1)}, bf16[71,8,128]{2,1,0:T(8,128)(2,1)S(1)}, u32[]{:S(2)}, u32[]{:S(2)}) collective-permute-start(bf16[71,8,128]{2,1,0:T(8,128)(2,1)S(1)} %get-tuple-element.48), channel_id=1, source_target_pairs={{0,1},{1,2},{2,3},{4,5},{5,6},{6,7},{8,9},{9,10},{10,11},{12,13},{... | collective-permute-start | bytes 436232 | tf_op jit(solution)/shard_map/ppermute | solution.py:67
  15.2 1.3 %collective-permute-start.3 = (bf16[71,8,128]{2,1,0:T(8,128)(2,1)S(1)}, bf16[71,8,128]{2,1,0:T(8,128)(2,1)S(1)}, u32[]{:S(2)}, u32[]{:S(2)}) collective-permute-start(bf16[71,8,128]{2,1,0:T(8,128)(2,1)S(1)} %get-tuple-element.49), channel_id=1, source_target_pairs={{1,0},{2,1},{3,2},{5,4},{6,5},{7,6},{9,8},{10,9},{11,10},{13,12},{... | collective-permute-start | bytes 436232 | tf_op jit(solution)/shard_map/ppermute | solution.py:67
  16.5 0.0 collective-permute-done.2.yl_ref
  16.5 3.7 %collective-permute-done.3.yh_ref = bf16[71,8,128]{2,1,0:T(8,128)(2,1)S(1)} collective-permute-done((bf16[71,8,128]{2,1,0:T(8,128)(2,1)S(1)}, bf16[71,8,128]{2,1,0:T(8,128)(2,1)S(1)}, u32[]{:S(2)}, u32[]{:S(2)}) %collective-permute-start.3) | collective-permute-done | bytes 145440 | tf_op jit(solution)/shard_map/ppermute | solution.py:67
  20.2 4.5 %forward.1 = (bf16[2,64,8,128]{3,2,1,0:T(8,128)(2,1)}, bf16[64,16,128]{2,1,0:T(8,128)(2,1)S(1)}, f32[14,128,128]{2,1,0:T(8,128)S(1)}, bf16[14,128,128]{2,1,0:T(8,128)(2,1)S(1)}) custom-call(bf16[1,8,128]{2,1,0:T(8,128)(2,1)S(1)} %get-tuple-element.41.mine_ref, bf16[2,8,8,8,128]{4,3,2,1,0:T(8,128)(2,1)S(1)} %get-tuple-element.42.x_ref, ...), custom_call_target="tpu_custom_call" | custom-call | flops 2000000000 | bytes 5242880 | tf_op jit(solution)/shard_map/forward/pallas_call | solution.py:319
  24.7 3.7 %collective-permute-start.4 = (bf16[14,128,128]{2,1,0:T(8,128)(2,1)S(1)}, bf16[14,128,128]{2,1,0:T(8,128)(2,1)S(1)}, u32[]{:S(2)}, u32[]{:S(2)}) collective-permute-start(bf16[14,128,128]{2,1,0:T(8,128)(2,1)S(1)} %get-tuple-element.53), channel_id=1, source_target_pairs={{0,1},{1,0},{2,3},{3,2},{4,5},{5,4},{6,7},{7,6},{8,9},{9,8},{10,11... | collective-permute-start | bytes 1376264 | tf_op jit(solution)/shard_map/ppermute | solution.py:53
  28.5 1.4 %collective-permute-done.4 = bf16[14,128,128]{2,1,0:T(8,128)(2,1)S(1)} collective-permute-done((bf16[14,128,128]{2,1,0:T(8,128)(2,1)S(1)}, bf16[14,128,128]{2,1,0:T(8,128)(2,1)S(1)}, u32[]{:S(2)}, u32[]{:S(2)}) %collective-permute-start.4) | collective-permute-done | bytes 458784 | tf_op jit(solution)/shard_map/ppermute | solution.py:53
  29.9 0.1 merge.4
  30.0 0.2 collective-permute-start.5
  30.2 2.4 %collective-permute-start.6 = (bf16[448,128]{1,0:T(8,128)(2,1)S(1)}, bf16[448,128]{1,0:T(8,128)(2,1)S(1)}, u32[]{:S(2)}, u32[]{:S(2)}) collective-permute-start(bf16[448,128]{1,0:T(8,128)(2,1)S(1)} %get-tuple-element.55), channel_id=1, source_target_pairs={{0,4},{1,5},{2,6},{3,7},{4,0},{5,1},{6,2},{7,3},{8,12},{9,13},{10,... | collective-permute-start | bytes 344072 | tf_op jit(solution)/shard_map/ppermute | solution.py:53
  32.6 1.4 %collective-permute-start.7 = (bf16[448,128]{1,0:T(8,128)(2,1)S(1)}, bf16[448,128]{1,0:T(8,128)(2,1)S(1)}, u32[]{:S(2)}, u32[]{:S(2)}) collective-permute-start(bf16[448,128]{1,0:T(8,128)(2,1)S(1)} %get-tuple-element.56), channel_id=1, source_target_pairs={{0,6},{1,7},{2,4},{3,5},{4,2},{5,3},{6,0},{7,1},{8,14},{9,15},{10,... | collective-permute-start | bytes 344072 | tf_op jit(solution)/shard_map/ppermute | solution.py:53
  33.9 5.9 %backward.1 = bf16[2,64,8,128]{3,2,1,0:T(8,128)(2,1)} custom-call(bf16[1,8,128]{2,1,0:T(8,128)(2,1)S(1)} %get-tuple-element.41.mine_ref, bf16[2,8,8,8,128]{4,3,2,1,0:T(8,128)(2,1)S(1)} %get-tuple-element.42.x_ref, bf16[64,16,128]{2,1,0:T(8,128)(2,1)S(1)} %get-tuple-element.57.dpre_ref, bf16[49,8,128]{2,1,0:T(8,128)(2,1)S(1)} %collective-permute-done.low_ref.zl_ref, ...), custom_call_target="tpu_custom_call" | custom-call | flops 1000000000 | bytes 5242880 | tf_op jit(solution)/shard_map/backward/pallas_call | solution.py:428
  39.8 0.0 collective-permute-done.5.refs_1_
  39.8 0.0 collective-permute-done.6.refs_2_
  39.8 0.1 merge.5
  39.9 2.2 %collective-permute-start.8 = (bf16[224,128]{1,0:T(8,128)(2,1)S(1)}, bf16[224,128]{1,0:T(8,128)(2,1)S(1)}, u32[]{:S(2)}, u32[]{:S(2)}) collective-permute-start(bf16[224,128]{1,0:T(8,128)(2,1)S(1)} %get-tuple-element.64), channel_id=1, source_target_pairs={{0,8},{1,9},{2,10},{3,11},{4,12},{5,13},{6,14},{7,15},{8,0},{9,1},... | collective-permute-start | bytes 172040 | tf_op jit(solution)/shard_map/ppermute | solution.py:53
  42.1 2.2 %collective-permute-done.8.refs_1_ = bf16[224,128]{1,0:T(8,128)(2,1)S(1)} collective-permute-done((bf16[224,128]{1,0:T(8,128)(2,1)S(1)}, bf16[224,128]{1,0:T(8,128)(2,1)S(1)}, u32[]{:S(2)}, u32[]{:S(2)}) %collective-permute-start.8) | collective-permute-done | bytes 57376 | tf_op jit(solution)/shard_map/ppermute | solution.py:53
  44.3 3.1 %collective-permute-start.9 = (bf16[112,128]{1,0:T(8,128)(2,1)S(1)}, bf16[112,128]{1,0:T(8,128)(2,1)S(1)}, u32[]{:S(2)}, u32[]{:S(2)}) collective-permute-start(bf16[112,128]{1,0:T(8,128)(2,1)S(1)} %get-tuple-element.66), channel_id=1, source_target_pairs={{0,16},{1,17},{2,18},{3,19},{4,20},{5,21},{6,22},{7,23},{8,24},{9,... | collective-permute-start | bytes 86024 | tf_op jit(solution)/shard_map/ppermute | solution.py:53
  47.4 1.9 %collective-permute-done.9.refs_1_ = bf16[112,128]{1,0:T(8,128)(2,1)S(1)} collective-permute-done((bf16[112,128]{1,0:T(8,128)(2,1)S(1)}, bf16[112,128]{1,0:T(8,128)(2,1)S(1)}, u32[]{:S(2)}, u32[]{:S(2)}) %collective-permute-start.9) | collective-permute-done | bytes 28704 | tf_op jit(solution)/shard_map/ppermute | solution.py:53
  49.2 3.0 %collective-permute-start.10 = (bf16[112,128]{1,0:T(8,128)(2,1)S(1)}, bf16[112,128]{1,0:T(8,128)(2,1)S(1)}, u32[]{:S(2)}, u32[]{:S(2)}) collective-permute-start(bf16[112,128]{1,0:T(8,128)(2,1)S(1)} %merge.7.refs_0_), channel_id=1, source_target_pairs={{0,16},{1,17},{2,18},{3,19},{4,20},{5,21},{6,22},{7,23},{8,24},{9,... | collective-permute-start | bytes 86024 | tf_op jit(solution)/shard_map/ppermute | solution.py:53
  52.2 2.0 %collective-permute-done.10.refs_1_ = bf16[112,128]{1,0:T(8,128)(2,1)S(1)} collective-permute-done((bf16[112,128]{1,0:T(8,128)(2,1)S(1)}, bf16[112,128]{1,0:T(8,128)(2,1)S(1)}, u32[]{:S(2)}, u32[]{:S(2)}) %collective-permute-start.10) | collective-permute-done | bytes 28704 | tf_op jit(solution)/shard_map/ppermute | solution.py:53
  54.2 2.1 %collective-permute-start.11 = (bf16[224,128]{1,0:T(8,128)(2,1)S(1)}, bf16[224,128]{1,0:T(8,128)(2,1)S(1)}, u32[]{:S(2)}, u32[]{:S(2)}) collective-permute-start(bf16[224,128]{1,0:T(8,128)(2,1)S(1)} %join.2.refs_0_), channel_id=1, source_target_pairs={{0,8},{1,9},{2,10},{3,11},{4,12},{5,13},{6,14},{7,15},{8,0},{9,1},... | collective-permute-start | bytes 172040 | tf_op jit(solution)/shard_map/ppermute | solution.py:53
  56.3 2.2 %collective-permute-done.11.refs_1_ = bf16[224,128]{1,0:T(8,128)(2,1)S(1)} collective-permute-done((bf16[224,128]{1,0:T(8,128)(2,1)S(1)}, bf16[224,128]{1,0:T(8,128)(2,1)S(1)}, u32[]{:S(2)}, u32[]{:S(2)}) %collective-permute-start.11) | collective-permute-done | bytes 57376 | tf_op jit(solution)/shard_map/ppermute | solution.py:53
  58.4 1.4 %collective-permute-start.14 = (bf16[448,128]{1,0:T(8,128)(2,1)S(1)}, bf16[448,128]{1,0:T(8,128)(2,1)S(1)}, u32[]{:S(2)}, u32[]{:S(2)}) collective-permute-start(bf16[448,128]{1,0:T(8,128)(2,1)S(1)} %join.3.refs_0_), channel_id=1, source_target_pairs={{0,6},{1,7},{2,4},{3,5},{4,2},{5,3},{6,0},{7,1},{8,14},{9,15},{10,... | collective-permute-start | bytes 344072 | tf_op jit(solution)/shard_map/ppermute | solution.py:53
  59.8 0.4 collective-permute-start.13
  60.2 1.8 %collective-permute-start.12 = (bf16[448,128]{1,0:T(8,128)(2,1)S(1)}, bf16[448,128]{1,0:T(8,128)(2,1)S(1)}, u32[]{:S(2)}, u32[]{:S(2)}) collective-permute-start(bf16[448,128]{1,0:T(8,128)(2,1)S(1)} %join.3.refs_0_), channel_id=1, source_target_pairs={{0,2},{1,3},{2,0},{3,1},{4,6},{5,7},{6,4},{7,5},{8,10},{9,11},{10,... | collective-permute-start | bytes 344072 | tf_op jit(solution)/shard_map/ppermute | solution.py:53
  62.0 0.0 collective-permute-start.15
  62.0 2.3 %collective-permute-done.14.refs_3_ = bf16[448,128]{1,0:T(8,128)(2,1)S(1)} collective-permute-done((bf16[448,128]{1,0:T(8,128)(2,1)S(1)}, bf16[448,128]{1,0:T(8,128)(2,1)S(1)}, u32[]{:S(2)}, u32[]{:S(2)}) %collective-permute-start.14) | collective-permute-done | bytes 114720 | tf_op jit(solution)/shard_map/ppermute | solution.py:53
  64.3 1.1 %collective-permute-done.13.refs_2_ = bf16[448,128]{1,0:T(8,128)(2,1)S(1)} collective-permute-done((bf16[448,128]{1,0:T(8,128)(2,1)S(1)}, bf16[448,128]{1,0:T(8,128)(2,1)S(1)}, u32[]{:S(2)}, u32[]{:S(2)}) %collective-permute-start.13) | collective-permute-done | bytes 114720 | tf_op jit(solution)/shard_map/ppermute | solution.py:53
  65.4 0.0 collective-permute-start.17
  65.4 0.2 collective-permute-done.12.refs_1_
  65.6 0.3 collective-permute-start.16
  65.9 0.0 collective-permute-done.15.refs_4_
  65.9 0.0 collective-permute-done.18.refs_7_
  65.9 0.8 %collective-permute-done.17.refs_6_ = bf16[448,128]{1,0:T(8,128)(2,1)S(1)} collective-permute-done((bf16[448,128]{1,0:T(8,128)(2,1)S(1)}, bf16[448,128]{1,0:T(8,128)(2,1)S(1)}, u32[]{:S(2)}, u32[]{:S(2)}) %collective-permute-start.17) | collective-permute-done | bytes 114720 | tf_op jit(solution)/shard_map/ppermute | solution.py:53
  66.7 0.2 collective-permute-done.16.refs_5_
  67.0 1.8 %finish.1 = f32[3456,128]{1,0:T(8,128)} custom-call(bf16[448,128]{1,0:T(8,128)(2,1)S(1)} %join.3.refs_0_, bf16[448,128]{1,0:T(8,128)(2,1)S(1)} %collective-permute-done.12.refs_1_, bf16[448,128]{1,0:T(8,128)(2,1)S(1)} %collective-permute-done.13.refs_2_, bf16[448,128]{1,0:T(8,128)(2,1)S(1)} %collective-permute-done.14.refs_3_, ...), custom_call_target="tpu_custom_call" | custom-call | tf_op jit(solution)/shard_map/finish/pallas_call | solution.py:521
  (10 shorter events, 0.1 us)
Async XLA Ops:
  2.3 10.6 %collective-permute-start = (bf16[49,8,128]{2,1,0:T(8,128)(2,1)}, bf16[49,8,128]{2,1,0:T(8,128)(2,1)S(1)}, u32[]{:S(2)}, u32[]{:S(2)}) collective-permute-start(bf16[49,8,128]{2,1,0:T(8,128)(2,1)} %get-tuple-element.44), channel_id=1, source_target_pairs={{0,4},{4,8},{8,12},{12,16},{16,20},{20,24},{24,28},{1,5},{5,9},{9,... | collective-permute-start | bytes 301064 | tf_op jit(solution)/shard_map/ppermute | solution.py:67
  7.2 6.7 %collective-permute-start.1 = (bf16[49,8,128]{2,1,0:T(8,128)(2,1)}, bf16[49,8,128]{2,1,0:T(8,128)(2,1)S(1)}, u32[]{:S(2)}, u32[]{:S(2)}) collective-permute-start(bf16[49,8,128]{2,1,0:T(8,128)(2,1)} %get-tuple-element.45), channel_id=1, source_target_pairs={{4,0},{8,4},{12,8},{16,12},{20,16},{24,20},{28,24},{5,1},{9,5},{13... | collective-permute-start | bytes 301064 | tf_op jit(solution)/shard_map/ppermute | solution.py:67
  8.5 1.0 %copy-start = (bf16[1,1,2,512,128]{4,3,2,1,0:T(8,128)(2,1)S(1)}, bf16[1,1,2,512,128]{4,3,2,1,0:T(8,128)(2,1)}, u32[]{:S(2)}) copy-start(bf16[1,1,2,512,128]{4,3,2,1,0:T(8,128)(2,1)} %param.4) | copy-start | bytes 786436
  9.4 0.9 %copy-start.1 = (bf16[1,1,2,512,128]{4,3,2,1,0:T(8,128)(2,1)S(1)}, bf16[1,1,2,512,128]{4,3,2,1,0:T(8,128)(2,1)}, u32[]{:S(2)}) copy-start(bf16[1,1,2,512,128]{4,3,2,1,0:T(8,128)(2,1)} %param.7) | copy-start | bytes 786436
  10.4 1.2 %copy-start.2 = (bf16[27,128,128]{2,1,0:T(8,128)(2,1)S(1)}, bf16[27,128,128]{2,1,0:T(8,128)(2,1)}, u32[]{:S(2)}) copy-start(bf16[27,128,128]{2,1,0:T(8,128)(2,1)} %w_ref) | copy-start | bytes 2654212
  11.5 0.7 copy-start.3
  13.9 2.6 %collective-permute-start.2 = (bf16[71,8,128]{2,1,0:T(8,128)(2,1)S(1)}, bf16[71,8,128]{2,1,0:T(8,128)(2,1)S(1)}, u32[]{:S(2)}, u32[]{:S(2)}) collective-permute-start(bf16[71,8,128]{2,1,0:T(8,128)(2,1)S(1)} %get-tuple-element.48), channel_id=1, source_target_pairs={{0,1},{1,2},{2,3},{4,5},{5,6},{6,7},{8,9},{9,10},{10,11},{12,13},{... | collective-permute-start | bytes 436232 | tf_op jit(solution)/shard_map/ppermute | solution.py:67
  15.2 5.0 %collective-permute-start.3 = (bf16[71,8,128]{2,1,0:T(8,128)(2,1)S(1)}, bf16[71,8,128]{2,1,0:T(8,128)(2,1)S(1)}, u32[]{:S(2)}, u32[]{:S(2)}) collective-permute-start(bf16[71,8,128]{2,1,0:T(8,128)(2,1)S(1)} %get-tuple-element.49), channel_id=1, source_target_pairs={{1,0},{2,1},{3,2},{5,4},{6,5},{7,6},{9,8},{10,9},{11,10},{13,12},{... | collective-permute-start | bytes 436232 | tf_op jit(solution)/shard_map/ppermute | solution.py:67
  24.7 5.2 %collective-permute-start.4 = (bf16[14,128,128]{2,1,0:T(8,128)(2,1)S(1)}, bf16[14,128,128]{2,1,0:T(8,128)(2,1)S(1)}, u32[]{:S(2)}, u32[]{:S(2)}) collective-permute-start(bf16[14,128,128]{2,1,0:T(8,128)(2,1)S(1)} %get-tuple-element.53), channel_id=1, source_target_pairs={{0,1},{1,0},{2,3},{3,2},{4,5},{5,4},{6,7},{7,6},{8,9},{9,8},{10,11... | collective-permute-start | bytes 1376264 | tf_op jit(solution)/shard_map/ppermute | solution.py:53
  30.0 9.8 %collective-permute-start.5 = (bf16[448,128]{1,0:T(8,128)(2,1)S(1)}, bf16[448,128]{1,0:T(8,128)(2,1)S(1)}, u32[]{:S(2)}, u32[]{:S(2)}) collective-permute-start(bf16[448,128]{1,0:T(8,128)(2,1)S(1)} %get-tuple-element.54), channel_id=1, source_target_pairs={{0,2},{1,3},{2,0},{3,1},{4,6},{5,7},{6,4},{7,5},{8,10},{9,11},{10,... | collective-permute-start | bytes 344072 | tf_op jit(solution)/shard_map/ppermute | solution.py:53
  30.2 9.6 %collective-permute-start.6 = (bf16[448,128]{1,0:T(8,128)(2,1)S(1)}, bf16[448,128]{1,0:T(8,128)(2,1)S(1)}, u32[]{:S(2)}, u32[]{:S(2)}) collective-permute-start(bf16[448,128]{1,0:T(8,128)(2,1)S(1)} %get-tuple-element.55), channel_id=1, source_target_pairs={{0,4},{1,5},{2,6},{3,7},{4,0},{5,1},{6,2},{7,3},{8,12},{9,13},{10,... | collective-permute-start | bytes 344072 | tf_op jit(solution)/shard_map/ppermute | solution.py:53
  32.6 7.2 %collective-permute-start.7 = (bf16[448,128]{1,0:T(8,128)(2,1)S(1)}, bf16[448,128]{1,0:T(8,128)(2,1)S(1)}, u32[]{:S(2)}, u32[]{:S(2)}) collective-permute-start(bf16[448,128]{1,0:T(8,128)(2,1)S(1)} %get-tuple-element.56), channel_id=1, source_target_pairs={{0,6},{1,7},{2,4},{3,5},{4,2},{5,3},{6,0},{7,1},{8,14},{9,15},{10,... | collective-permute-start | bytes 344072 | tf_op jit(solution)/shard_map/ppermute | solution.py:53
  39.9 4.4 %collective-permute-start.8 = (bf16[224,128]{1,0:T(8,128)(2,1)S(1)}, bf16[224,128]{1,0:T(8,128)(2,1)S(1)}, u32[]{:S(2)}, u32[]{:S(2)}) collective-permute-start(bf16[224,128]{1,0:T(8,128)(2,1)S(1)} %get-tuple-element.64), channel_id=1, source_target_pairs={{0,8},{1,9},{2,10},{3,11},{4,12},{5,13},{6,14},{7,15},{8,0},{9,1},... | collective-permute-start | bytes 172040 | tf_op jit(solution)/shard_map/ppermute | solution.py:53
  44.3 4.9 %collective-permute-start.9 = (bf16[112,128]{1,0:T(8,128)(2,1)S(1)}, bf16[112,128]{1,0:T(8,128)(2,1)S(1)}, u32[]{:S(2)}, u32[]{:S(2)}) collective-permute-start(bf16[112,128]{1,0:T(8,128)(2,1)S(1)} %get-tuple-element.66), channel_id=1, source_target_pairs={{0,16},{1,17},{2,18},{3,19},{4,20},{5,21},{6,22},{7,23},{8,24},{9,... | collective-permute-start | bytes 86024 | tf_op jit(solution)/shard_map/ppermute | solution.py:53
  49.2 4.9 %collective-permute-start.10 = (bf16[112,128]{1,0:T(8,128)(2,1)S(1)}, bf16[112,128]{1,0:T(8,128)(2,1)S(1)}, u32[]{:S(2)}, u32[]{:S(2)}) collective-permute-start(bf16[112,128]{1,0:T(8,128)(2,1)S(1)} %merge.7.refs_0_), channel_id=1, source_target_pairs={{0,16},{1,17},{2,18},{3,19},{4,20},{5,21},{6,22},{7,23},{8,24},{9,... | collective-permute-start | bytes 86024 | tf_op jit(solution)/shard_map/ppermute | solution.py:53
  54.2 4.2 %collective-permute-start.11 = (bf16[224,128]{1,0:T(8,128)(2,1)S(1)}, bf16[224,128]{1,0:T(8,128)(2,1)S(1)}, u32[]{:S(2)}, u32[]{:S(2)}) collective-permute-start(bf16[224,128]{1,0:T(8,128)(2,1)S(1)} %join.2.refs_0_), channel_id=1, source_target_pairs={{0,8},{1,9},{2,10},{3,11},{4,12},{5,13},{6,14},{7,15},{8,0},{9,1},... | collective-permute-start | bytes 172040 | tf_op jit(solution)/shard_map/ppermute | solution.py:53
  58.4 5.8 %collective-permute-start.14 = (bf16[448,128]{1,0:T(8,128)(2,1)S(1)}, bf16[448,128]{1,0:T(8,128)(2,1)S(1)}, u32[]{:S(2)}, u32[]{:S(2)}) collective-permute-start(bf16[448,128]{1,0:T(8,128)(2,1)S(1)} %join.3.refs_0_), channel_id=1, source_target_pairs={{0,6},{1,7},{2,4},{3,5},{4,2},{5,3},{6,0},{7,1},{8,14},{9,15},{10,... | collective-permute-start | bytes 344072 | tf_op jit(solution)/shard_map/ppermute | solution.py:53
  59.8 5.6 %collective-permute-start.13 = (bf16[448,128]{1,0:T(8,128)(2,1)S(1)}, bf16[448,128]{1,0:T(8,128)(2,1)S(1)}, u32[]{:S(2)}, u32[]{:S(2)}) collective-permute-start(bf16[448,128]{1,0:T(8,128)(2,1)S(1)} %join.3.refs_0_), channel_id=1, source_target_pairs={{0,4},{1,5},{2,6},{3,7},{4,0},{5,1},{6,2},{7,3},{8,12},{9,13},{10,... | collective-permute-start | bytes 344072 | tf_op jit(solution)/shard_map/ppermute | solution.py:53
  60.2 5.4 %collective-permute-start.12 = (bf16[448,128]{1,0:T(8,128)(2,1)S(1)}, bf16[448,128]{1,0:T(8,128)(2,1)S(1)}, u32[]{:S(2)}, u32[]{:S(2)}) collective-permute-start(bf16[448,128]{1,0:T(8,128)(2,1)S(1)} %join.3.refs_0_), channel_id=1, source_target_pairs={{0,2},{1,3},{2,0},{3,1},{4,6},{5,7},{6,4},{7,5},{8,10},{9,11},{10,... | collective-permute-start | bytes 344072 | tf_op jit(solution)/shard_map/ppermute | solution.py:53
  62.0 3.9 %collective-permute-start.15 = (bf16[448,128]{1,0:T(8,128)(2,1)S(1)}, bf16[448,128]{1,0:T(8,128)(2,1)S(1)}, u32[]{:S(2)}, u32[]{:S(2)}) collective-permute-start(bf16[448,128]{1,0:T(8,128)(2,1)S(1)} %join.3.refs_0_), channel_id=1, source_target_pairs={{0,1},{1,0},{2,3},{3,2},{4,5},{5,4},{6,7},{7,6},{8,9},{9,8},{10,11... | collective-permute-start | bytes 344072 | tf_op jit(solution)/shard_map/ppermute | solution.py:53
  64.3 1.7 %collective-permute-start.18 = (bf16[448,128]{1,0:T(8,128)(2,1)S(1)}, bf16[448,128]{1,0:T(8,128)(2,1)S(1)}, u32[]{:S(2)}, u32[]{:S(2)}) collective-permute-start(bf16[448,128]{1,0:T(8,128)(2,1)S(1)} %collective-permute-done.14.refs_3_), channel_id=1, source_target_pairs={{0,1},{1,0},{2,3},{3,2},{4,5},{5,4},{6,7},{7,6},{8,9},{9,8},{10,11... | collective-permute-start | bytes 344072 | tf_op jit(solution)/shard_map/ppermute | solution.py:53
  65.4 1.3 %collective-permute-start.17 = (bf16[448,128]{1,0:T(8,128)(2,1)S(1)}, bf16[448,128]{1,0:T(8,128)(2,1)S(1)}, u32[]{:S(2)}, u32[]{:S(2)}) collective-permute-start(bf16[448,128]{1,0:T(8,128)(2,1)S(1)} %collective-permute-done.13.refs_2_), channel_id=1, source_target_pairs={{0,1},{1,0},{2,3},{3,2},{4,5},{5,4},{6,7},{7,6},{8,9},{9,8},{10,11... | collective-permute-start | bytes 344072 | tf_op jit(solution)/shard_map/ppermute | solution.py:53
  65.6 1.3 %collective-permute-start.16 = (bf16[448,128]{1,0:T(8,128)(2,1)S(1)}, bf16[448,128]{1,0:T(8,128)(2,1)S(1)}, u32[]{:S(2)}, u32[]{:S(2)}) collective-permute-start(bf16[448,128]{1,0:T(8,128)(2,1)S(1)} %collective-permute-done.12.refs_1_), channel_id=1, source_target_pairs={{0,1},{1,0},{2,3},{3,2},{4,5},{5,4},{6,7},{7,6},{8,9},{9,8},{10,11... | collective-permute-start | bytes 344072 | tf_op jit(solution)/shard_map/ppermute | solution.py:53

commit v7 on v5

--- a/solution.py
+++ b/solution.py
@@ -121,10 +121,9 @@
     )(sites, x, g)
 
 
-def stage_kernel(sites, x_ref, g_ref, w_ref, x_out, g_out, w_out, code_out, up_ref, down_ref):
+def stage_kernel(sites, x_ref, g_ref, x_out, g_out, code_out, up_ref, down_ref):
     x_out[...] = x_ref[...]
     g_out[...] = g_ref[...]
-    w_out[...] = w_ref[...]
     code_out[0] = code_row(sites)
     for s in range(NB):
         first, last = slice(24 * s, 24 * s + 16), slice(24 * s + 16, 24 * s + 24)
@@ -134,18 +133,33 @@
         down_ref[last] = g_ref[s, :, 0]
 
 
-def stage(sites, x, g, w):
+def stage(sites, x, g):
     beside = jax.ShapeDtypeStruct((NB * 24, 8, C), BF16)
     code = jax.ShapeDtypeStruct((1, 8, C), BF16)
-    kept = tuple(jax.ShapeDtypeStruct(a.shape, a.dtype) for a in (x, g, w))
+    kept = tuple(jax.ShapeDtypeStruct(a.shape, a.dtype) for a in (x, g))
     return pl.pallas_call(
         stage_kernel,
         out_shape=kept + (code, beside, beside),
-        in_specs=[SMEM, VMEM, VMEM, VMEM],
-        out_specs=(VMEM,) * 6,
+        in_specs=[SMEM, VMEM, VMEM],
+        out_specs=(VMEM,) * 5,
         compiler_params=small(4),
         name="stage",
-    )(sites, x, g, w)
+    )(sites, x, g)
+
+
+def keep_kernel(w_ref, w_out):
+    w_out[...] = w_ref[...]
+
+
+def keep_near(w):
+    return pl.pallas_call(
+        keep_kernel,
+        out_shape=jax.ShapeDtypeStruct(w.shape, w.dtype),
+        in_specs=[VMEM],
+        out_specs=VMEM,
+        compiler_params=small(4),
+        name="keep_near",
+    )(w)
 
 
 def pack_y_kernel(own_up, own_down, mine_ref, low_ref, high_ref, up_ref, down_ref):
@@ -535,10 +549,12 @@
     sites = brick_sites.reshape(NB)
     devices = lax.axis_size("gz") * lax.axis_size("gy")
     z_up, z_down = pack_z(sites, x, g)
-    z_up, z_down, *later = lax.optimization_barrier((z_up, z_down, sites, x, g, kernel))
-    x, g, w, mine, own_up, own_down = stage(*later)
+    z_up, z_down, *later = lax.optimization_barrier((z_up, z_down, sites, x, g))
+    x, g, mine, own_up, own_down = stage(*later)
     zl, zh = neighbours(z_up, z_down, "gz")
     y_up, y_down = pack_y(own_up, own_down, mine, zl, zh)
+    y_up, y_down, w = lax.optimization_barrier((y_up, y_down, kernel))
+    w = keep_near(w)
     yl, yh = neighbours(y_up, y_down, "gy")
     act, dpre, keep, send = forward(mine, x, g, zl, zh, yl, yh, w)
 

time: 67.1 us -> 66.3 us (0.988)
  no operation moved by 1% of the time
where the time goes in v7:
time: 66.3 us; the launch traced here: 66 us
  starting transfers between devices  29.4 us (44%)
  waiting for transfers between devices  17.5 us (26%)
  Pallas kernels  14.6 us (22%)
  local copies, waits for them, and re-layouts  3.71 us (6%)
  between operations  0.76 us (1%)
    ppermute x17, starting transfers between devices, swap_with(): return lax.ppermute(value, AXES, pairs)  20.7 us
    ppermute x17, waiting for transfers between devices, swap_with(): return lax.ppermute(value, AXES, pairs)  12.8 us
    ppermute x4, starting transfers between devices, neighbours(): return (lax.ppermute(up, axis, forward), lax.ppermute(down, axis, backward))  8.79 us
    pallas_call x1, Pallas kernels, backward(): pl.pallas_call(backward_kernel, out_shape=jax.ShapeDtypeStruct((NB, 64, 8...  5.81 us
    ppermute x4, waiting for transfers between devices, neighbours(): return (lax.ppermute(up, axis, forward), lax.ppermute(down, axis, backward))  4.7 us
    pallas_call x1, Pallas kernels, forward(): pl.pallas_call(forward_kernel, out_shape=(rows, jax.ShapeDtypeStruct((64,...  4.48 us
    unnamed x8, local copies, waits for them, and re-layouts  3.71 us
    pallas_call x1, Pallas kernels, finish(): pl.pallas_call(functools.partial(finish_kernel, first, share, plan), out_...  1.79 us
  transfers between devices with their start and end apart: 21, of which 11 were waited for; matrix products, arithmetic and copies ran while one was open for 0% of the time, Pallas kernels for 10%

profile of v7, /device:TPU:0, one launch (start us, length us, event | category | flops | bytes accessed | tf_op | source)
XLA Modules:
  0.0 66.0 jit_solution(13624434006606298784)
XLA Ops:
  0.6 1.6 %pack_z.1 = (bf16[49,8,128]{2,1,0:T(8,128)(2,1)}, bf16[49,8,128]{2,1,0:T(8,128)(2,1)}) custom-call(s32[2]{0:T(128)} %bitcast.14, bf16[2,8,8,8,128]{4,3,2,1,0:T(8,128)(2,1)} %bitcast.8, bf16[2,8,8,8,128]{4,3,2,1,0:T(8,128)(2,1)} %bitcast.10), custom_call_target="tpu_custom_call" | custom-call | tf_op jit(solution)/shard_map/pack_z/pallas_call | solution.py:113
  2.3 4.9 %collective-permute-start = (bf16[49,8,128]{2,1,0:T(8,128)(2,1)}, bf16[49,8,128]{2,1,0:T(8,128)(2,1)S(1)}, u32[]{:S(2)}, u32[]{:S(2)}) collective-permute-start(bf16[49,8,128]{2,1,0:T(8,128)(2,1)} %get-tuple-element.44), channel_id=1, source_target_pairs={{0,4},{4,8},{8,12},{12,16},{16,20},{20,24},{24,28},{1,5},{5,9},{9,... | collective-permute-start | bytes 301064 | tf_op jit(solution)/shard_map/ppermute | solution.py:68
  7.2 1.3 %collective-permute-start.1 = (bf16[49,8,128]{2,1,0:T(8,128)(2,1)}, bf16[49,8,128]{2,1,0:T(8,128)(2,1)S(1)}, u32[]{:S(2)}, u32[]{:S(2)}) collective-permute-start(bf16[49,8,128]{2,1,0:T(8,128)(2,1)} %get-tuple-element.45), channel_id=1, source_target_pairs={{4,0},{8,4},{12,8},{16,12},{20,16},{24,20},{28,24},{5,1},{9,5},{13... | collective-permute-start | bytes 301064 | tf_op jit(solution)/shard_map/ppermute | solution.py:68
  8.5 0.0 copy-start
  8.5 0.9 %copy-done = bf16[1,1,2,512,128]{4,3,2,1,0:T(8,128)(2,1)S(1)} copy-done((bf16[1,1,2,512,128]{4,3,2,1,0:T(8,128)(2,1)S(1)}, bf16[1,1,2,512,128]{4,3,2,1,0:T(8,128)(2,1)}, u32[]{:S(2)}) %copy-start) | copy-done | bytes 262168
  9.4 0.9 %copy-done.1 = bf16[1,1,2,512,128]{4,3,2,1,0:T(8,128)(2,1)S(1)} copy-done((bf16[1,1,2,512,128]{4,3,2,1,0:T(8,128)(2,1)S(1)}, bf16[1,1,2,512,128]{4,3,2,1,0:T(8,128)(2,1)}, u32[]{:S(2)}) %copy-start.1) | copy-done | bytes 262168
  10.4 0.7 copy-done.3
  11.0 0.6 stage.1
  11.6 0.0 collective-permute-done.low_ref.zl_ref
  11.7 2.3 %collective-permute-done.1.high_ref.zh_ref = bf16[49,8,128]{2,1,0:T(8,128)(2,1)S(1)} collective-permute-done((bf16[49,8,128]{2,1,0:T(8,128)(2,1)}, bf16[49,8,128]{2,1,0:T(8,128)(2,1)S(1)}, u32[]{:S(2)}, u32[]{:S(2)}) %collective-permute-start.1) | collective-permute-done | bytes 100384 | tf_op jit(solution)/shard_map/ppermute | solution.py:68
  13.9 1.3 %collective-permute-start.2 = (bf16[71,8,128]{2,1,0:T(8,128)(2,1)S(1)}, bf16[71,8,128]{2,1,0:T(8,128)(2,1)S(1)}, u32[]{:S(2)}, u32[]{:S(2)}) collective-permute-start(bf16[71,8,128]{2,1,0:T(8,128)(2,1)S(1)} %get-tuple-element.50), channel_id=1, source_target_pairs={{0,1},{1,2},{2,3},{4,5},{5,6},{6,7},{8,9},{9,10},{10,11},{12,13},{... | collective-permute-start | bytes 436232 | tf_op jit(solution)/shard_map/ppermute | solution.py:68
  15.2 1.3 %collective-permute-start.3 = (bf16[71,8,128]{2,1,0:T(8,128)(2,1)S(1)}, bf16[71,8,128]{2,1,0:T(8,128)(2,1)S(1)}, u32[]{:S(2)}, u32[]{:S(2)}) collective-permute-start(bf16[71,8,128]{2,1,0:T(8,128)(2,1)S(1)} %get-tuple-element.51), channel_id=1, source_target_pairs={{1,0},{2,1},{3,2},{5,4},{6,5},{7,6},{9,8},{10,9},{11,10},{13,12},{... | collective-permute-start | bytes 436232 | tf_op jit(solution)/shard_map/ppermute | solution.py:68
  16.5 0.0 copy-start.2
  16.6 1.2 %copy-done.2 = bf16[27,128,128]{2,1,0:T(8,128)(2,1)S(1)} copy-done((bf16[27,128,128]{2,1,0:T(8,128)(2,1)S(1)}, bf16[27,128,128]{2,1,0:T(8,128)(2,1)}, u32[]{:S(2)}) %copy-start.2) | copy-done | bytes 884760
  17.7 0.1 keep_near.1.w_ref
  17.8 0.0 collective-permute-done.2.yl_ref
  17.8 2.4 %collective-permute-done.3.yh_ref = bf16[71,8,128]{2,1,0:T(8,128)(2,1)S(1)} collective-permute-done((bf16[71,8,128]{2,1,0:T(8,128)(2,1)S(1)}, bf16[71,8,128]{2,1,0:T(8,128)(2,1)S(1)}, u32[]{:S(2)}, u32[]{:S(2)}) %collective-permute-start.3) | collective-permute-done | bytes 145440 | tf_op jit(solution)/shard_map/ppermute | solution.py:68
  20.2 4.5 %forward.1 = (bf16[2,64,8,128]{3,2,1,0:T(8,128)(2,1)}, bf16[64,16,128]{2,1,0:T(8,128)(2,1)S(1)}, f32[14,128,128]{2,1,0:T(8,128)S(1)}, bf16[14,128,128]{2,1,0:T(8,128)(2,1)S(1)}) custom-call(bf16[1,8,128]{2,1,0:T(8,128)(2,1)S(1)} %get-tuple-element.41.mine_ref, bf16[2,8,8,8,128]{4,3,2,1,0:T(8,128)(2,1)S(1)} %get-tuple-element.42.x_ref, ...), custom_call_target="tpu_custom_call" | custom-call | flops 2000000000 | bytes 5242880 | tf_op jit(solution)/shard_map/forward/pallas_call | solution.py:334
  24.7 3.7 %collective-permute-start.4 = (bf16[14,128,128]{2,1,0:T(8,128)(2,1)S(1)}, bf16[14,128,128]{2,1,0:T(8,128)(2,1)S(1)}, u32[]{:S(2)}, u32[]{:S(2)}) collective-permute-start(bf16[14,128,128]{2,1,0:T(8,128)(2,1)S(1)} %get-tuple-element.55), channel_id=1, source_target_pairs={{0,1},{1,0},{2,3},{3,2},{4,5},{5,4},{6,7},{7,6},{8,9},{9,8},{10,11... | collective-permute-start | bytes 1376264 | tf_op jit(solution)/shard_map/ppermute | solution.py:54
  28.5 1.4 %collective-permute-done.4 = bf16[14,128,128]{2,1,0:T(8,128)(2,1)S(1)} collective-permute-done((bf16[14,128,128]{2,1,0:T(8,128)(2,1)S(1)}, bf16[14,128,128]{2,1,0:T(8,128)(2,1)S(1)}, u32[]{:S(2)}, u32[]{:S(2)}) %collective-permute-start.4) | collective-permute-done | bytes 458784 | tf_op jit(solution)/shard_map/ppermute | solution.py:54
  29.9 0.1 merge.3
  30.0 0.2 collective-permute-start.5
  30.2 2.4 %collective-permute-start.6 = (bf16[448,128]{1,0:T(8,128)(2,1)S(1)}, bf16[448,128]{1,0:T(8,128)(2,1)S(1)}, u32[]{:S(2)}, u32[]{:S(2)}) collective-permute-start(bf16[448,128]{1,0:T(8,128)(2,1)S(1)} %get-tuple-element.57), channel_id=1, source_target_pairs={{0,4},{1,5},{2,6},{3,7},{4,0},{5,1},{6,2},{7,3},{8,12},{9,13},{10,... | collective-permute-start | bytes 344072 | tf_op jit(solution)/shard_map/ppermute | solution.py:54
  32.6 1.4 %collective-permute-start.7 = (bf16[448,128]{1,0:T(8,128)(2,1)S(1)}, bf16[448,128]{1,0:T(8,128)(2,1)S(1)}, u32[]{:S(2)}, u32[]{:S(2)}) collective-permute-start(bf16[448,128]{1,0:T(8,128)(2,1)S(1)} %get-tuple-element.58), channel_id=1, source_target_pairs={{0,6},{1,7},{2,4},{3,5},{4,2},{5,3},{6,0},{7,1},{8,14},{9,15},{10,... | collective-permute-start | bytes 344072 | tf_op jit(solution)/shard_map/ppermute | solution.py:54
  33.9 5.8 %backward.1 = bf16[2,64,8,128]{3,2,1,0:T(8,128)(2,1)} custom-call(bf16[1,8,128]{2,1,0:T(8,128)(2,1)S(1)} %get-tuple-element.41.mine_ref, bf16[2,8,8,8,128]{4,3,2,1,0:T(8,128)(2,1)S(1)} %get-tuple-element.42.x_ref, bf16[64,16,128]{2,1,0:T(8,128)(2,1)S(1)} %get-tuple-element.59.dpre_ref, bf16[49,8,128]{2,1,0:T(8,128)(2,1)S(1)} %collective-permute-done.low_ref.zl_ref, ...), custom_call_target="tpu_custom_call" | custom-call | flops 1000000000 | bytes 5242880 | tf_op jit(solution)/shard_map/backward/pallas_call | solution.py:443
  39.8 0.0 collective-permute-done.7.refs_3_
  39.8 0.1 merge.4
  39.8 1.7 %collective-permute-start.8 = (bf16[112,128]{1,0:T(8,128)(2,1)S(1)}, bf16[112,128]{1,0:T(8,128)(2,1)S(1)}, u32[]{:S(2)}, u32[]{:S(2)}) collective-permute-start(bf16[112,128]{1,0:T(8,128)(2,1)S(1)} %get-tuple-element.66), channel_id=1, source_target_pairs={{0,8},{1,9},{2,10},{3,11},{4,12},{5,13},{6,14},{7,15},{8,0},{9,1},... | collective-permute-start | bytes 86024 | tf_op jit(solution)/shard_map/ppermute | solution.py:54
  41.5 2.2 %collective-permute-start.9 = (bf16[112,128]{1,0:T(8,128)(2,1)S(1)}, bf16[112,128]{1,0:T(8,128)(2,1)S(1)}, u32[]{:S(2)}, u32[]{:S(2)}) collective-permute-start(bf16[112,128]{1,0:T(8,128)(2,1)S(1)} %get-tuple-element.67), channel_id=1, source_target_pairs={{0,16},{1,17},{2,18},{3,19},{4,20},{5,21},{6,22},{7,23},{8,24},{9,... | collective-permute-start | bytes 86024 | tf_op jit(solution)/shard_map/ppermute | solution.py:54
  43.7 0.6 collective-permute-start.10
  44.3 2.5 %collective-permute-done.9.refs_2_ = bf16[112,128]{1,0:T(8,128)(2,1)S(1)} collective-permute-done((bf16[112,128]{1,0:T(8,128)(2,1)S(1)}, bf16[112,128]{1,0:T(8,128)(2,1)S(1)}, u32[]{:S(2)}, u32[]{:S(2)}) %collective-permute-start.9) | collective-permute-done | bytes 28704 | tf_op jit(solution)/shard_map/ppermute | solution.py:54
  46.8 2.6 %collective-permute-done.10.refs_3_ = bf16[112,128]{1,0:T(8,128)(2,1)S(1)} collective-permute-done((bf16[112,128]{1,0:T(8,128)(2,1)S(1)}, bf16[112,128]{1,0:T(8,128)(2,1)S(1)}, u32[]{:S(2)}, u32[]{:S(2)}) %collective-permute-start.10) | collective-permute-done | bytes 28704 | tf_op jit(solution)/shard_map/ppermute | solution.py:54
  49.4 0.7 %collective-permute-start.13 = (bf16[112,128]{1,0:T(8,128)(2,1)S(1)}, bf16[112,128]{1,0:T(8,128)(2,1)S(1)}, u32[]{:S(2)}, u32[]{:S(2)}) collective-permute-start(bf16[112,128]{1,0:T(8,128)(2,1)S(1)} %merge.5.refs_0_), channel_id=1, source_target_pairs={{0,24},{1,25},{2,26},{3,27},{4,28},{5,29},{6,30},{7,31},{8,16},{9,... | collective-permute-start | bytes 86024 | tf_op jit(solution)/shard_map/ppermute | solution.py:54
  50.1 0.0 collective-permute-start.12
  50.1 3.8 %collective-permute-start.11 = (bf16[112,128]{1,0:T(8,128)(2,1)S(1)}, bf16[112,128]{1,0:T(8,128)(2,1)S(1)}, u32[]{:S(2)}, u32[]{:S(2)}) collective-permute-start(bf16[112,128]{1,0:T(8,128)(2,1)S(1)} %merge.5.refs_0_), channel_id=1, source_target_pairs={{0,8},{1,9},{2,10},{3,11},{4,12},{5,13},{6,14},{7,15},{8,0},{9,1},... | collective-permute-start | bytes 86024 | tf_op jit(solution)/shard_map/ppermute | solution.py:54
  53.8 1.3 %collective-permute-done.13.refs_3_ = bf16[112,128]{1,0:T(8,128)(2,1)S(1)} collective-permute-done((bf16[112,128]{1,0:T(8,128)(2,1)S(1)}, bf16[112,128]{1,0:T(8,128)(2,1)S(1)}, u32[]{:S(2)}, u32[]{:S(2)}) %collective-permute-start.13) | collective-permute-done | bytes 28704 | tf_op jit(solution)/shard_map/ppermute | solution.py:54
  55.1 0.6 collective-permute-done.11.refs_1_
  55.7 1.0 %collective-permute-start.16 = (bf16[448,128]{1,0:T(8,128)(2,1)S(1)}, bf16[448,128]{1,0:T(8,128)(2,1)S(1)}, u32[]{:S(2)}, u32[]{:S(2)}) collective-permute-start(bf16[448,128]{1,0:T(8,128)(2,1)S(1)} %join.1.refs_0_), channel_id=1, source_target_pairs={{0,6},{1,7},{2,4},{3,5},{4,2},{5,3},{6,0},{7,1},{8,14},{9,15},{10,... | collective-permute-start | bytes 344072 | tf_op jit(solution)/shard_map/ppermute | solution.py:54
  56.8 1.0 %collective-permute-start.15 = (bf16[448,128]{1,0:T(8,128)(2,1)S(1)}, bf16[448,128]{1,0:T(8,128)(2,1)S(1)}, u32[]{:S(2)}, u32[]{:S(2)}) collective-permute-start(bf16[448,128]{1,0:T(8,128)(2,1)S(1)} %join.1.refs_0_), channel_id=1, source_target_pairs={{0,4},{1,5},{2,6},{3,7},{4,0},{5,1},{6,2},{7,3},{8,12},{9,13},{10,... | collective-permute-start | bytes 344072 | tf_op jit(solution)/shard_map/ppermute | solution.py:54
  57.8 1.5 %collective-permute-start.14 = (bf16[448,128]{1,0:T(8,128)(2,1)S(1)}, bf16[448,128]{1,0:T(8,128)(2,1)S(1)}, u32[]{:S(2)}, u32[]{:S(2)}) collective-permute-start(bf16[448,128]{1,0:T(8,128)(2,1)S(1)} %join.1.refs_0_), channel_id=1, source_target_pairs={{0,2},{1,3},{2,0},{3,1},{4,6},{5,7},{6,4},{7,5},{8,10},{9,11},{10,... | collective-permute-start | bytes 344072 | tf_op jit(solution)/shard_map/ppermute | solution.py:54
  59.3 0.0 collective-permute-start.17
  59.3 2.3 %collective-permute-done.16.refs_3_ = bf16[448,128]{1,0:T(8,128)(2,1)S(1)} collective-permute-done((bf16[448,128]{1,0:T(8,128)(2,1)S(1)}, bf16[448,128]{1,0:T(8,128)(2,1)S(1)}, u32[]{:S(2)}, u32[]{:S(2)}) %collective-permute-start.16) | collective-permute-done | bytes 114720 | tf_op jit(solution)/shard_map/ppermute | solution.py:54
  61.6 0.0 collective-permute-start.20
  61.6 1.1 %collective-permute-done.15.refs_2_ = bf16[448,128]{1,0:T(8,128)(2,1)S(1)} collective-permute-done((bf16[448,128]{1,0:T(8,128)(2,1)S(1)}, bf16[448,128]{1,0:T(8,128)(2,1)S(1)}, u32[]{:S(2)}, u32[]{:S(2)}) %collective-permute-start.15) | collective-permute-done | bytes 114720 | tf_op jit(solution)/shard_map/ppermute | solution.py:54
  62.7 0.5 collective-permute-start.18
  63.2 0.8 %collective-permute-done.19.refs_6_ = bf16[448,128]{1,0:T(8,128)(2,1)S(1)} collective-permute-done((bf16[448,128]{1,0:T(8,128)(2,1)S(1)}, bf16[448,128]{1,0:T(8,128)(2,1)S(1)}, u32[]{:S(2)}, u32[]{:S(2)}) %collective-permute-start.19) | collective-permute-done | bytes 114720 | tf_op jit(solution)/shard_map/ppermute | solution.py:54
  64.0 0.2 collective-permute-done.18.refs_5_
  64.2 1.8 %finish.1 = f32[3456,128]{1,0:T(8,128)} custom-call(bf16[448,128]{1,0:T(8,128)(2,1)S(1)} %join.1.refs_0_, bf16[448,128]{1,0:T(8,128)(2,1)S(1)} %collective-permute-done.14.refs_1_, bf16[448,128]{1,0:T(8,128)(2,1)S(1)} %collective-permute-done.15.refs_2_, bf16[448,128]{1,0:T(8,128)(2,1)S(1)} %collective-permute-done.16.refs_3_, ...), custom_call_target="tpu_custom_call" | custom-call | tf_op jit(solution)/shard_map/finish/pallas_call | solution.py:536
  (13 shorter events, 0.1 us)
Async XLA Ops:
  2.3 9.4 %collective-permute-start = (bf16[49,8,128]{2,1,0:T(8,128)(2,1)}, bf16[49,8,128]{2,1,0:T(8,128)(2,1)S(1)}, u32[]{:S(2)}, u32[]{:S(2)}) collective-permute-start(bf16[49,8,128]{2,1,0:T(8,128)(2,1)} %get-tuple-element.44), channel_id=1, source_target_pairs={{0,4},{4,8},{8,12},{12,16},{16,20},{20,24},{24,28},{1,5},{5,9},{9,... | collective-permute-start | bytes 301064 | tf_op jit(solution)/shard_map/ppermute | solution.py:68
  7.2 6.7 %collective-permute-start.1 = (bf16[49,8,128]{2,1,0:T(8,128)(2,1)}, bf16[49,8,128]{2,1,0:T(8,128)(2,1)S(1)}, u32[]{:S(2)}, u32[]{:S(2)}) collective-permute-start(bf16[49,8,128]{2,1,0:T(8,128)(2,1)} %get-tuple-element.45), channel_id=1, source_target_pairs={{4,0},{8,4},{12,8},{16,12},{20,16},{24,20},{28,24},{5,1},{9,5},{13... | collective-permute-start | bytes 301064 | tf_op jit(solution)/shard_map/ppermute | solution.py:68
  8.5 1.0 %copy-start = (bf16[1,1,2,512,128]{4,3,2,1,0:T(8,128)(2,1)S(1)}, bf16[1,1,2,512,128]{4,3,2,1,0:T(8,128)(2,1)}, u32[]{:S(2)}) copy-start(bf16[1,1,2,512,128]{4,3,2,1,0:T(8,128)(2,1)} %param.4) | copy-start | bytes 786436
  9.4 0.9 %copy-start.1 = (bf16[1,1,2,512,128]{4,3,2,1,0:T(8,128)(2,1)S(1)}, bf16[1,1,2,512,128]{4,3,2,1,0:T(8,128)(2,1)}, u32[]{:S(2)}) copy-start(bf16[1,1,2,512,128]{4,3,2,1,0:T(8,128)(2,1)} %param.7) | copy-start | bytes 786436
  10.4 0.7 copy-start.3
  13.9 3.8 %collective-permute-start.2 = (bf16[71,8,128]{2,1,0:T(8,128)(2,1)S(1)}, bf16[71,8,128]{2,1,0:T(8,128)(2,1)S(1)}, u32[]{:S(2)}, u32[]{:S(2)}) collective-permute-start(bf16[71,8,128]{2,1,0:T(8,128)(2,1)S(1)} %get-tuple-element.50), channel_id=1, source_target_pairs={{0,1},{1,2},{2,3},{4,5},{5,6},{6,7},{8,9},{9,10},{10,11},{12,13},{... | collective-permute-start | bytes 436232 | tf_op jit(solution)/shard_map/ppermute | solution.py:68
  15.2 5.0 %collective-permute-start.3 = (bf16[71,8,128]{2,1,0:T(8,128)(2,1)S(1)}, bf16[71,8,128]{2,1,0:T(8,128)(2,1)S(1)}, u32[]{:S(2)}, u32[]{:S(2)}) collective-permute-start(bf16[71,8,128]{2,1,0:T(8,128)(2,1)S(1)} %get-tuple-element.51), channel_id=1, source_target_pairs={{1,0},{2,1},{3,2},{5,4},{6,5},{7,6},{9,8},{10,9},{11,10},{13,12},{... | collective-permute-start | bytes 436232 | tf_op jit(solution)/shard_map/ppermute | solution.py:68
  16.5 1.2 %copy-start.2 = (bf16[27,128,128]{2,1,0:T(8,128)(2,1)S(1)}, bf16[27,128,128]{2,1,0:T(8,128)(2,1)}, u32[]{:S(2)}) copy-start(bf16[27,128,128]{2,1,0:T(8,128)(2,1)} %w_ref) | copy-start | bytes 2654212
  24.7 5.2 %collective-permute-start.4 = (bf16[14,128,128]{2,1,0:T(8,128)(2,1)S(1)}, bf16[14,128,128]{2,1,0:T(8,128)(2,1)S(1)}, u32[]{:S(2)}, u32[]{:S(2)}) collective-permute-start(bf16[14,128,128]{2,1,0:T(8,128)(2,1)S(1)} %get-tuple-element.55), channel_id=1, source_target_pairs={{0,1},{1,0},{2,3},{3,2},{4,5},{5,4},{6,7},{7,6},{8,9},{9,8},{10,11... | collective-permute-start | bytes 1376264 | tf_op jit(solution)/shard_map/ppermute | solution.py:54
  30.0 9.8 %collective-permute-start.5 = (bf16[448,128]{1,0:T(8,128)(2,1)S(1)}, bf16[448,128]{1,0:T(8,128)(2,1)S(1)}, u32[]{:S(2)}, u32[]{:S(2)}) collective-permute-start(bf16[448,128]{1,0:T(8,128)(2,1)S(1)} %get-tuple-element.56), channel_id=1, source_target_pairs={{0,2},{1,3},{2,0},{3,1},{4,6},{5,7},{6,4},{7,5},{8,10},{9,11},{10,... | collective-permute-start | bytes 344072 | tf_op jit(solution)/shard_map/ppermute | solution.py:54
  30.2 9.6 %collective-permute-start.6 = (bf16[448,128]{1,0:T(8,128)(2,1)S(1)}, bf16[448,128]{1,0:T(8,128)(2,1)S(1)}, u32[]{:S(2)}, u32[]{:S(2)}) collective-permute-start(bf16[448,128]{1,0:T(8,128)(2,1)S(1)} %get-tuple-element.57), channel_id=1, source_target_pairs={{0,4},{1,5},{2,6},{3,7},{4,0},{5,1},{6,2},{7,3},{8,12},{9,13},{10,... | collective-permute-start | bytes 344072 | tf_op jit(solution)/shard_map/ppermute | solution.py:54
  32.6 7.2 %collective-permute-start.7 = (bf16[448,128]{1,0:T(8,128)(2,1)S(1)}, bf16[448,128]{1,0:T(8,128)(2,1)S(1)}, u32[]{:S(2)}, u32[]{:S(2)}) collective-permute-start(bf16[448,128]{1,0:T(8,128)(2,1)S(1)} %get-tuple-element.58), channel_id=1, source_target_pairs={{0,6},{1,7},{2,4},{3,5},{4,2},{5,3},{6,0},{7,1},{8,14},{9,15},{10,... | collective-permute-start | bytes 344072 | tf_op jit(solution)/shard_map/ppermute | solution.py:54
  39.8 4.5 %collective-permute-start.8 = (bf16[112,128]{1,0:T(8,128)(2,1)S(1)}, bf16[112,128]{1,0:T(8,128)(2,1)S(1)}, u32[]{:S(2)}, u32[]{:S(2)}) collective-permute-start(bf16[112,128]{1,0:T(8,128)(2,1)S(1)} %get-tuple-element.66), channel_id=1, source_target_pairs={{0,8},{1,9},{2,10},{3,11},{4,12},{5,13},{6,14},{7,15},{8,0},{9,1},... | collective-permute-start | bytes 86024 | tf_op jit(solution)/shard_map/ppermute | solution.py:54
  41.5 5.2 %collective-permute-start.9 = (bf16[112,128]{1,0:T(8,128)(2,1)S(1)}, bf16[112,128]{1,0:T(8,128)(2,1)S(1)}, u32[]{:S(2)}, u32[]{:S(2)}) collective-permute-start(bf16[112,128]{1,0:T(8,128)(2,1)S(1)} %get-tuple-element.67), channel_id=1, source_target_pairs={{0,16},{1,17},{2,18},{3,19},{4,20},{5,21},{6,22},{7,23},{8,24},{9,... | collective-permute-start | bytes 86024 | tf_op jit(solution)/shard_map/ppermute | solution.py:54
  43.7 5.7 %collective-permute-start.10 = (bf16[112,128]{1,0:T(8,128)(2,1)S(1)}, bf16[112,128]{1,0:T(8,128)(2,1)S(1)}, u32[]{:S(2)}, u32[]{:S(2)}) collective-permute-start(bf16[112,128]{1,0:T(8,128)(2,1)S(1)} %get-tuple-element.68), channel_id=1, source_target_pairs={{0,24},{1,25},{2,26},{3,27},{4,28},{5,29},{6,30},{7,31},{8,16},{9,... | collective-permute-start | bytes 86024 | tf_op jit(solution)/shard_map/ppermute | solution.py:54
  49.4 5.7 %collective-permute-start.13 = (bf16[112,128]{1,0:T(8,128)(2,1)S(1)}, bf16[112,128]{1,0:T(8,128)(2,1)S(1)}, u32[]{:S(2)}, u32[]{:S(2)}) collective-permute-start(bf16[112,128]{1,0:T(8,128)(2,1)S(1)} %merge.5.refs_0_), channel_id=1, source_target_pairs={{0,24},{1,25},{2,26},{3,27},{4,28},{5,29},{6,30},{7,31},{8,16},{9,... | collective-permute-start | bytes 86024 | tf_op jit(solution)/shard_map/ppermute | solution.py:54
  50.1 5.1 %collective-permute-start.12 = (bf16[112,128]{1,0:T(8,128)(2,1)S(1)}, bf16[112,128]{1,0:T(8,128)(2,1)S(1)}, u32[]{:S(2)}, u32[]{:S(2)}) collective-permute-start(bf16[112,128]{1,0:T(8,128)(2,1)S(1)} %merge.5.refs_0_), channel_id=1, source_target_pairs={{0,16},{1,17},{2,18},{3,19},{4,20},{5,21},{6,22},{7,23},{8,24},{9,... | collective-permute-start | bytes 86024 | tf_op jit(solution)/shard_map/ppermute | solution.py:54
  50.1 5.6 %collective-permute-start.11 = (bf16[112,128]{1,0:T(8,128)(2,1)S(1)}, bf16[112,128]{1,0:T(8,128)(2,1)S(1)}, u32[]{:S(2)}, u32[]{:S(2)}) collective-permute-start(bf16[112,128]{1,0:T(8,128)(2,1)S(1)} %merge.5.refs_0_), channel_id=1, source_target_pairs={{0,8},{1,9},{2,10},{3,11},{4,12},{5,13},{6,14},{7,15},{8,0},{9,1},... | collective-permute-start | bytes 86024 | tf_op jit(solution)/shard_map/ppermute | solution.py:54
  55.7 5.9 %collective-permute-start.16 = (bf16[448,128]{1,0:T(8,128)(2,1)S(1)}, bf16[448,128]{1,0:T(8,128)(2,1)S(1)}, u32[]{:S(2)}, u32[]{:S(2)}) collective-permute-start(bf16[448,128]{1,0:T(8,128)(2,1)S(1)} %join.1.refs_0_), channel_id=1, source_target_pairs={{0,6},{1,7},{2,4},{3,5},{4,2},{5,3},{6,0},{7,1},{8,14},{9,15},{10,... | collective-permute-start | bytes 344072 | tf_op jit(solution)/shard_map/ppermute | solution.py:54
  56.8 5.9 %collective-permute-start.15 = (bf16[448,128]{1,0:T(8,128)(2,1)S(1)}, bf16[448,128]{1,0:T(8,128)(2,1)S(1)}, u32[]{:S(2)}, u32[]{:S(2)}) collective-permute-start(bf16[448,128]{1,0:T(8,128)(2,1)S(1)} %join.1.refs_0_), channel_id=1, source_target_pairs={{0,4},{1,5},{2,6},{3,7},{4,0},{5,1},{6,2},{7,3},{8,12},{9,13},{10,... | collective-permute-start | bytes 344072 | tf_op jit(solution)/shard_map/ppermute | solution.py:54
  57.8 4.9 %collective-permute-start.14 = (bf16[448,128]{1,0:T(8,128)(2,1)S(1)}, bf16[448,128]{1,0:T(8,128)(2,1)S(1)}, u32[]{:S(2)}, u32[]{:S(2)}) collective-permute-start(bf16[448,128]{1,0:T(8,128)(2,1)S(1)} %join.1.refs_0_), channel_id=1, source_target_pairs={{0,2},{1,3},{2,0},{3,1},{4,6},{5,7},{6,4},{7,5},{8,10},{9,11},{10,... | collective-permute-start | bytes 344072 | tf_op jit(solution)/shard_map/ppermute | solution.py:54
  59.3 3.9 %collective-permute-start.17 = (bf16[448,128]{1,0:T(8,128)(2,1)S(1)}, bf16[448,128]{1,0:T(8,128)(2,1)S(1)}, u32[]{:S(2)}, u32[]{:S(2)}) collective-permute-start(bf16[448,128]{1,0:T(8,128)(2,1)S(1)} %join.1.refs_0_), channel_id=1, source_target_pairs={{0,1},{1,0},{2,3},{3,2},{4,5},{5,4},{6,7},{7,6},{8,9},{9,8},{10,11... | collective-permute-start | bytes 344072 | tf_op jit(solution)/shard_map/ppermute | solution.py:54
  61.6 1.7 %collective-permute-start.20 = (bf16[448,128]{1,0:T(8,128)(2,1)S(1)}, bf16[448,128]{1,0:T(8,128)(2,1)S(1)}, u32[]{:S(2)}, u32[]{:S(2)}) collective-permute-start(bf16[448,128]{1,0:T(8,128)(2,1)S(1)} %collective-permute-done.16.refs_3_), channel_id=1, source_target_pairs={{0,1},{1,0},{2,3},{3,2},{4,5},{5,4},{6,7},{7,6},{8,9},{9,8},{10,11... | collective-permute-start | bytes 344072 | tf_op jit(solution)/shard_map/ppermute | solution.py:54
  62.7 1.3 %collective-permute-start.19 = (bf16[448,128]{1,0:T(8,128)(2,1)S(1)}, bf16[448,128]{1,0:T(8,128)(2,1)S(1)}, u32[]{:S(2)}, u32[]{:S(2)}) collective-permute-start(bf16[448,128]{1,0:T(8,128)(2,1)S(1)} %collective-permute-done.15.refs_2_), channel_id=1, source_target_pairs={{0,1},{1,0},{2,3},{3,2},{4,5},{5,4},{6,7},{7,6},{8,9},{9,8},{10,11... | collective-permute-start | bytes 344072 | tf_op jit(solution)/shard_map/ppermute | solution.py:54
  62.7 1.5 %collective-permute-start.18 = (bf16[448,128]{1,0:T(8,128)(2,1)S(1)}, bf16[448,128]{1,0:T(8,128)(2,1)S(1)}, u32[]{:S(2)}, u32[]{:S(2)}) collective-permute-start(bf16[448,128]{1,0:T(8,128)(2,1)S(1)} %collective-permute-done.14.refs_1_), channel_id=1, source_target_pairs={{0,1},{1,0},{2,3},{3,2},{4,5},{5,4},{6,7},{7,6},{8,9},{9,8},{10,11... | collective-permute-start | bytes 344072 | tf_op jit(solution)/shard_map/ppermute | solution.py:54
